TPU v7x, 32 devices: a whole 2x2x4 slice. The times are simulated.
32 devices in a mesh: batch: 4 (over x, core), seq: 8 (over z, y).
Axes of the slice: x: 2, y: 2, z: 4, core: 2. Of those that a mesh axis runs over, the one named last changes fastest.
Arguments:
- tokens: bfloat16 [4, 4096, 1024], P('batch', 'seq'), may hold values from -6 to 6
- lengths: int32 [4, 4], P('batch'), may hold values from 1 to 2048, 4096 in all within a row
- key_mask: int32 [4, 4096], P('batch'), may hold values 0 or 1
- cotangent: bfloat16 [4, 4096, 1024], P('batch', 'seq'), may hold values from -6 to 6
- w_qkv: bfloat16 [1024, 3072], P('seq'), may hold values from -0.1875 to 0.1875
- w_out: bfloat16 [1024, 1024], P('seq'), may hold values from -1 to 1
- w_up: bfloat16 [1024, 4096], P('seq'), may hold values from -0.1875 to 0.1875
- w_down: bfloat16 [4096, 1024], P('seq'), may hold values from -0.09375 to 0.09375
- ln1_gain: bfloat16 [1024], P('seq'), may hold values from 0.5 to 1.5
- ln1_bias: bfloat16 [1024], P('seq'), may hold values from -1 to 1
- ln2_gain: bfloat16 [1024], P('seq'), may hold values from 0.5 to 1.5
- ln2_bias: bfloat16 [1024], P('seq'), may hold values from -1 to 1
- out_bias: bfloat16 [1024], P('seq'), may hold values from -3 to 3
- up_bias: bfloat16 [4096], P('seq'), may hold values from -3 to 3
- down_bias: bfloat16 [1024], P('seq'), may hold values from -3 to 3
Outputs:
- output: bfloat16 [4, 4096, 1024], P('batch', 'seq')
- input_grad: bfloat16 [4, 4096, 1024], P('batch', 'seq')
- grad_qkv_w: float32 [1024, 3072], P('seq')
- grad_out_w: float32 [1024, 1024], P('seq')
- grad_up_w: float32 [1024, 4096], P('seq')
- grad_down_w: float32 [4096, 1024], P('seq')
- grad_ln1_gain: float32 [1024], P('seq')
- grad_ln1_bias: float32 [1024], P('seq')
- grad_ln2_gain: float32 [1024], P('seq')
- grad_ln2_bias: float32 [1024], P('seq')
- grad_out_bias: float32 [1024], P('seq')
- grad_up_bias: float32 [4096], P('seq')
- grad_down_bias: float32 [1024], P('seq')
Inputs may be any that keep to these rules, and one draw needn't show every extreme that they name: Each row of lengths sums to 4096, and its longest utterance has exactly 2048 frames.
All inputs are finite; a program needn't handle non-finite values. No bound on the sum of `key_mask` on one device may be relied on, other than what follows from the above.
Results may differ from a plain program's by a relative error of at most 0.019.
Values may be sent and summed in bfloat16 or wider, within the bound.
No kernel may reach another device: no remote copies, remote signals or barrier semaphores. Data moves between devices by JAX's collectives and lax.ppermute only.
A program may use at most 256 MiB of HBM per device.

v0:
```python
import jax
import jax.numpy as jnp
from jax import lax
from jax.sharding import PartitionSpec as P

HEAD_COUNT = 16
HEAD_DIM = 64
MAXCAP = 2048


NEGATIVE = -1e30
EPSILON = 1e-05


def shifted(block, axis, distance):
    devices = range(lax.axis_size(axis))
    route = [(i - distance, i) for i in devices if i - distance in devices]
    return lax.ppermute(block, axis, route)


def norm_rows(values, gain, shift):
    centre = jnp.mean(values, axis=-1, keepdims=True)
    centred = values - centre
    spread = jnp.mean(centred * centred, axis=-1, keepdims=True)
    return centred * lax.rsqrt(spread + EPSILON) * gain + shift


def gelu_exact(values):
    return jax.nn.gelu(values, approximate=False)


def segment_ids(lengths_row, total):
    ends = jnp.cumsum(lengths_row)
    places = jnp.arange(total, dtype=jnp.int32)
    return jnp.sum((places[:, None] >= ends[None, :]).astype(jnp.int32), axis=1)


def times_trans(left, right):
    return lax.dot_general(
        left, right, (((1,), (1,)), ((), ())), preferred_element_type=jnp.float32
    )


def trans_times(left, right):
    return lax.dot_general(
        left, right, (((0,), (0,)), ((), ())), preferred_element_type=jnp.float32
    )


def head_split(matrix):
    return matrix.reshape(matrix.shape[0], HEAD_COUNT, HEAD_DIM)


def keep_same(carry):
    return carry


def block_allowed(my_index, offset, frames, seg_all, key_on, query_seg, query_pos):
    source = my_index - offset
    start = jnp.maximum(source, 0) * frames
    key_pos = source * frames + jnp.arange(frames, dtype=jnp.int32)
    key_seg = lax.dynamic_slice_in_dim(seg_all, start, frames)
    key_live = lax.dynamic_slice_in_dim(key_on, start, frames)
    same = key_seg[None, :] == query_seg[:, None]
    causal = (key_pos[None, :] <= query_pos[:, None]) & (key_pos[None, :] >= 0)
    usable = (key_live[None, :] == 1) | (key_pos[None, :] == query_pos[:, None])
    return same & causal & usable


def block_scores(queries, keys, allowed, score_scale):
    scores = (
        jnp.einsum(
            "qhd,khd->hqk",
            head_split(queries),
            head_split(keys),
            preferred_element_type=jnp.float32,
        )
        * score_scale
    )
    return jnp.where(allowed[None], scores, NEGATIVE)


def block_probs(queries, block, allowed, row_max, row_sum, score_scale):
    scores = block_scores(queries, block[:, : queries.shape[1]], allowed, score_scale)
    return jnp.exp(scores - row_max[:, :, None]) / row_sum[:, :, None]


def forward_chain(kv_own, reach):
    blocks = [kv_own]
    moving = kv_own
    for offset in range(reach):
        moving = shifted(moving, "seq", 1)
        blocks.append(moving)
    return blocks


def again_chain(kv_own, reach):
    blocks = [kv_own]
    moving = kv_own
    for offset in range(reach):
        moving = shifted(moving, "seq", 1)
        blocks.append(moving)
    return blocks


def softmax_stats(queries, blocks, allowed_list, live_list, score_scale):
    frames, model_width = queries.shape
    row_max = jnp.full((HEAD_COUNT, frames), NEGATIVE, jnp.float32)
    row_sum = jnp.zeros((HEAD_COUNT, frames), jnp.float32)
    for offset in range(len(blocks)):

        def softmax_update(carry, block=blocks[offset], allowed=allowed_list[offset]):
            old_max, old_sum = carry
            scores = block_scores(queries, block[:, :model_width], allowed, score_scale)
            new_max = jnp.maximum(old_max, jnp.max(scores, axis=2))
            new_sum = old_sum * jnp.exp(old_max - new_max) + jnp.sum(
                jnp.exp(scores - new_max[:, :, None]), axis=2
            )
            return (new_max, new_sum)

        row_max, row_sum = lax.cond(
            live_list[offset], softmax_update, keep_same, (row_max, row_sum)
        )
    return (row_max, row_sum)


def attend_values(queries, blocks, allowed_list, live_list, row_max, row_sum, score_scale):
    frames, model_width = queries.shape
    total = jnp.zeros((frames, HEAD_COUNT, HEAD_DIM), jnp.float32)
    for offset in range(len(blocks)):

        def attend_update(carry, block=blocks[offset], allowed=allowed_list[offset]):
            probs = block_probs(queries, block, allowed, row_max, row_sum, score_scale).astype(
                jnp.bfloat16
            )
            return carry + jnp.einsum(
                "hqk,khd->qhd",
                probs,
                head_split(block[:, model_width:]),
                preferred_element_type=jnp.float32,
            )

        total = lax.cond(live_list[offset], attend_update, keep_same, total)
    return total.reshape(frames, model_width).astype(jnp.bfloat16)


def attention_grads(
    queries, grad_attended, blocks, allowed_list, live_list, row_max, row_sum, score_scale
):
    frames, model_width = queries.shape
    grad_heads = head_split(grad_attended)
    query_heads = head_split(queries)
    delta = jnp.zeros((HEAD_COUNT, frames), jnp.float32)
    for offset in range(len(blocks)):

        def attention_update(carry, block=blocks[offset], allowed=allowed_list[offset]):
            probs = block_probs(queries, block, allowed, row_max, row_sum, score_scale)
            dprobs = jnp.einsum(
                "qhd,khd->hqk",
                grad_heads,
                head_split(block[:, model_width:]),
                preferred_element_type=jnp.float32,
            )
            return carry + jnp.sum(probs * dprobs, axis=2)

        delta = lax.cond(live_list[offset], attention_update, keep_same, delta)
    grad_queries = jnp.zeros((frames, HEAD_COUNT, HEAD_DIM), jnp.float32)
    contributions = []
    for offset in range(len(blocks)):

        def block_grads(block=blocks[offset], allowed=allowed_list[offset]):
            probs = block_probs(queries, block, allowed, row_max, row_sum, score_scale)
            value_heads = head_split(block[:, model_width:])
            dprobs = jnp.einsum(
                "qhd,khd->hqk", grad_heads, value_heads, preferred_element_type=jnp.float32
            )
            dscores = (probs * (dprobs - delta[:, :, None]) * score_scale).astype(jnp.bfloat16)
            query_part = jnp.einsum(
                "hqk,khd->qhd",
                dscores,
                head_split(block[:, :model_width]),
                preferred_element_type=jnp.float32,
            )
            key_part = jnp.einsum(
                "hqk,qhd->khd", dscores, query_heads, preferred_element_type=jnp.float32
            )
            value_part = jnp.einsum(
                "hqk,qhd->khd",
                probs.astype(jnp.bfloat16),
                grad_heads,
                preferred_element_type=jnp.float32,
            )
            joined = jnp.concatenate(
                [key_part.reshape(frames, model_width), value_part.reshape(frames, model_width)],
                axis=1,
            )
            return (query_part, joined)

        def no_grads():
            return (
                jnp.zeros((frames, HEAD_COUNT, HEAD_DIM), jnp.float32),
                jnp.zeros((frames, 2 * model_width), jnp.float32),
            )

        query_part, joined = lax.cond(live_list[offset], block_grads, no_grads)
        grad_queries = grad_queries + query_part
        contributions.append(joined)
    return (grad_queries.reshape(frames, model_width), contributions)


def shards(
    tokens,
    lengths,
    key_mask,
    cotangent,
    w_qkv,
    w_out,
    w_up,
    w_down,
    ln1_gain,
    ln1_bias,
    ln2_gain,
    ln2_bias,
    out_bias,
    up_bias,
    down_bias,
):
    gathered = (
        lax.all_gather(w_qkv, "seq", axis=0, tiled=True),
        lax.all_gather(w_out, "seq", axis=0, tiled=True),
        lax.all_gather(w_up, "seq", axis=0, tiled=True),
        lax.all_gather(w_down, "seq", axis=0, tiled=True),
        lax.all_gather(ln1_gain, "seq", axis=0, tiled=True),
        lax.all_gather(ln1_bias, "seq", axis=0, tiled=True),
        lax.all_gather(ln2_gain, "seq", axis=0, tiled=True),
        lax.all_gather(ln2_bias, "seq", axis=0, tiled=True),
        lax.all_gather(out_bias, "seq", axis=0, tiled=True),
        lax.all_gather(up_bias, "seq", axis=0, tiled=True),
        lax.all_gather(down_bias, "seq", axis=0, tiled=True),
    )
    qkv_full, out_full, up_full, down_full = (gathered[0], gathered[1], gathered[2], gathered[3])
    gain_one, shift_one, gain_two, shift_two, out_shift, up_shift, down_shift = tuple(
        (member.astype(jnp.float32) for member in gathered[4:])
    )
    frames = tokens.shape[1]
    model_width = tokens.shape[2]
    cycle_size = lax.axis_size("seq")
    group_frames = frames * cycle_size
    longest = min(MAXCAP, group_frames // 2)
    reach = longest // frames
    my_index = lax.axis_index("seq")
    score_scale = HEAD_DIM ** (-0.5)
    seg_all = segment_ids(lengths[0], group_frames)
    key_on = key_mask[0]
    query_pos = my_index * frames + jnp.arange(frames, dtype=jnp.int32)
    query_seg = lax.dynamic_slice_in_dim(seg_all, my_index * frames, frames)
    allowed_list = [
        block_allowed(my_index, offset, frames, seg_all, key_on, query_seg, query_pos)
        for offset in range(reach + 1)
    ]
    live_list = [jnp.any(allowed) for allowed in allowed_list]
    inputs = tokens[0].astype(jnp.float32)
    normed_one = norm_rows(inputs, gain_one, shift_one).astype(jnp.bfloat16)
    qkv_low = jnp.dot(normed_one, qkv_full, preferred_element_type=jnp.float32).astype(jnp.bfloat16)
    queries = qkv_low[:, :model_width]
    kv_own = qkv_low[:, model_width:]
    blocks = forward_chain(kv_own, reach)
    row_max, row_sum = softmax_stats(queries, blocks, allowed_list, live_list, score_scale)
    attended = attend_values(
        queries, blocks, allowed_list, live_list, row_max, row_sum, score_scale
    )
    branch = jnp.dot(attended, out_full, preferred_element_type=jnp.float32) + out_shift
    middle = inputs + branch
    normed_two = norm_rows(middle, gain_two, shift_two).astype(jnp.bfloat16)
    up_value = jnp.dot(normed_two, up_full, preferred_element_type=jnp.float32) + up_shift
    activated = gelu_exact(up_value).astype(jnp.bfloat16)
    result = middle + jnp.dot(activated, down_full, preferred_element_type=jnp.float32) + down_shift
    grad_result = cotangent[0]
    grad_down_w = trans_times(activated, grad_result)
    grad_down_b = jnp.sum(grad_result.astype(jnp.float32), axis=0)
    grad_act = times_trans(grad_result, down_full)
    grad_up = jax.vjp(gelu_exact, up_value)[1](grad_act)[0].astype(jnp.bfloat16)
    grad_up_w = trans_times(normed_two, grad_up)
    grad_up_b = jnp.sum(grad_up.astype(jnp.float32), axis=0)
    grad_normed_two = times_trans(grad_up, up_full)
    pull_two = jax.vjp(norm_rows, middle, gain_two, shift_two)[1]
    grad_mid_norm, grad_gain_two, grad_shift_two = pull_two(grad_normed_two)
    grad_middle = grad_result.astype(jnp.float32) + grad_mid_norm
    grad_branch = grad_middle.astype(jnp.bfloat16)
    grad_out_w = trans_times(attended, grad_branch)
    grad_out_b = jnp.sum(grad_branch.astype(jnp.float32), axis=0)
    grad_attended = times_trans(grad_branch, out_full).astype(jnp.bfloat16)
    back_blocks = again_chain(kv_own, reach)
    grad_queries, contributions = attention_grads(
        queries, grad_attended, back_blocks, allowed_list, live_list, row_max, row_sum, score_scale
    )
    flowing = contributions[reach]
    for offset in range(reach - 1, -1, -1):
        flowing = (
            shifted(flowing.astype(jnp.bfloat16), "seq", -1).astype(flowing.dtype)
            + contributions[offset]
        )
    grad_qkv = jnp.concatenate([grad_queries, flowing], axis=1).astype(jnp.bfloat16)
    grad_qkv_w = trans_times(normed_one, grad_qkv)
    grad_normed_one = times_trans(grad_qkv, qkv_full)
    pull_one = jax.vjp(norm_rows, inputs, gain_one, shift_one)[1]
    grad_in_norm, grad_gain_one, grad_shift_one = pull_one(grad_normed_one)
    grad_inputs = (grad_middle + grad_in_norm).astype(jnp.bfloat16)
    shares = (
        lax.psum_scatter(
            grad_qkv_w.astype(jnp.bfloat16), "seq", scatter_dimension=0, tiled=True
        ).astype(jnp.float32),
        lax.psum_scatter(
            grad_out_w.astype(jnp.bfloat16), "seq", scatter_dimension=0, tiled=True
        ).astype(jnp.float32),
        lax.psum_scatter(
            grad_up_w.astype(jnp.bfloat16), "seq", scatter_dimension=0, tiled=True
        ).astype(jnp.float32),
        lax.psum_scatter(
            grad_down_w.astype(jnp.bfloat16), "seq", scatter_dimension=0, tiled=True
        ).astype(jnp.float32),
        lax.psum_scatter(
            grad_gain_one.astype(jnp.bfloat16), "seq", scatter_dimension=0, tiled=True
        ).astype(jnp.float32),
        lax.psum_scatter(
            grad_shift_one.astype(jnp.bfloat16), "seq", scatter_dimension=0, tiled=True
        ).astype(jnp.float32),
        lax.psum_scatter(
            grad_gain_two.astype(jnp.bfloat16), "seq", scatter_dimension=0, tiled=True
        ).astype(jnp.float32),
        lax.psum_scatter(
            grad_shift_two.astype(jnp.bfloat16), "seq", scatter_dimension=0, tiled=True
        ).astype(jnp.float32),
        lax.psum_scatter(
            grad_out_b.astype(jnp.bfloat16), "seq", scatter_dimension=0, tiled=True
        ).astype(jnp.float32),
        lax.psum_scatter(
            grad_up_b.astype(jnp.bfloat16), "seq", scatter_dimension=0, tiled=True
        ).astype(jnp.float32),
        lax.psum_scatter(
            grad_down_b.astype(jnp.bfloat16), "seq", scatter_dimension=0, tiled=True
        ).astype(jnp.float32),
    )
    reduced = (
        lax.psum(shares[0].astype(jnp.bfloat16), "batch").astype(jnp.float32),
        lax.psum(shares[1].astype(jnp.bfloat16), "batch").astype(jnp.float32),
        lax.psum(shares[2].astype(jnp.bfloat16), "batch").astype(jnp.float32),
        lax.psum(shares[3].astype(jnp.bfloat16), "batch").astype(jnp.float32),
        lax.psum(shares[4].astype(jnp.bfloat16), "batch").astype(jnp.float32),
        lax.psum(shares[5].astype(jnp.bfloat16), "batch").astype(jnp.float32),
        lax.psum(shares[6].astype(jnp.bfloat16), "batch").astype(jnp.float32),
        lax.psum(shares[7].astype(jnp.bfloat16), "batch").astype(jnp.float32),
        lax.psum(shares[8].astype(jnp.bfloat16), "batch").astype(jnp.float32),
        lax.psum(shares[9].astype(jnp.bfloat16), "batch").astype(jnp.float32),
        lax.psum(shares[10].astype(jnp.bfloat16), "batch").astype(jnp.float32),
    )
    return (
        result.astype(jnp.bfloat16)[None],
        grad_inputs[None],
        reduced[0],
        reduced[1],
        reduced[2],
        reduced[3],
        reduced[4],
        reduced[5],
        reduced[6],
        reduced[7],
        reduced[8],
        reduced[9],
        reduced[10],
    )


def solution(mesh):
    return jax.shard_map(
        shards,
        mesh=mesh,
        in_specs=(
            P("batch", "seq", None),
            P("batch", None),
            P("batch", None),
            P("batch", "seq", None),
            P("seq", None),
            P("seq", None),
            P("seq", None),
            P("seq", None),
            P("seq"),
            P("seq"),
            P("seq"),
            P("seq"),
            P("seq"),
            P("seq"),
            P("seq"),
        ),
        out_specs=(
            P("batch", "seq", None),
            P("batch", "seq", None),
            P("seq", None),
            P("seq", None),
            P("seq", None),
            P("seq", None),
            P("seq"),
            P("seq"),
            P("seq"),
            P("seq"),
            P("seq"),
            P("seq"),
            P("seq"),
        ),
        check_vma=False,
    )
```

profile of v0, /device:TPU:1, one launch (start us, length us, event | category | flops | bytes accessed | tf_op | source)
XLA Modules:
  0.0 1636.3 jit_solution(14742294446530442316)
XLA Ops:
  9.4 18.0 %all-gather = bf16[8,1,128]{2,1,0:T(2,128)(2,1)S(1)} all-gather(bf16[1,1,128]{2,1,0:T(2,128)(2,1)} %bitcast.389), channel_id=1, replica_groups=mesh['batch'=4,'seq'=8] {'seq'}, dimensions={0}, use_global_device_ids=true | all-gather | bytes 2304 | tf_op jit(solution)/shard_map/all_gather | solution.py:233
  27.4 13.2 all-gather.1
  43.7 67.1 %all-gather.12.cloned.1.call-done = bf16[1024,3072]{1,0:T(8,128)(2,1)} async-done(((bf16[128,3072]{1,0:T(8,128)(2,1)}), bf16[1024,3072]{1,0:T(8,128)(2,1)}) %all-gather.12.cloned.1.call-update) | async-done | bytes 6291472 | tf_op jit(solution)/shard_map/all_gather | solution.py:229
  110.9 6.7 convolution_convert_fusion.3
  117.9 3.5 collective-permute-start
  121.4 57.6 %collective-permute-done = bf16[512,2048]{1,0:T(8,128)(2,1)} collective-permute-done((bf16[512,2048]{1,0:T(8,128)(2,1)S(1)}, bf16[512,2048]{1,0:T(8,128)(2,1)}, u32[]{:S(2)}, u32[]{:S(2)}) %collective-permute-start) | collective-permute-done | bytes 2097184 | tf_op jit(solution)/shard_map/ppermute | solution.py:18
  179.0 14.1 collective-permute-start.1
  193.2 53.7 %collective-permute-done.1 = bf16[512,2048]{1,0:T(8,128)(2,1)} collective-permute-done((bf16[512,2048]{1,0:T(8,128)(2,1)}, bf16[512,2048]{1,0:T(8,128)(2,1)}, u32[]{:S(2)}, u32[]{:S(2)}) %collective-permute-start.1) | collective-permute-done | bytes 2097184 | tf_op jit(solution)/shard_map/ppermute | solution.py:18
  246.9 35.0 %collective-permute-start.2 = (bf16[512,2048]{1,0:T(8,128)(2,1)}, bf16[512,2048]{1,0:T(8,128)(2,1)}, u32[]{:S(2)}, u32[]{:S(2)}) collective-permute-start(bf16[512,2048]{1,0:T(8,128)(2,1)} %collective-permute-done.1), channel_id=1, source_target_pairs={{0,1},{1,2},{2,3},{3,4},{4,5},{5,6},{6,7},{8,9},{9,10},{10,11},{11... | collective-permute-start | bytes 6291464 | tf_op jit(solution)/shard_map/ppermute | solution.py:18
  281.8 69.7 %collective-permute-done.2 = bf16[512,2048]{1,0:T(8,128)(2,1)} collective-permute-done((bf16[512,2048]{1,0:T(8,128)(2,1)}, bf16[512,2048]{1,0:T(8,128)(2,1)}, u32[]{:S(2)}, u32[]{:S(2)}) %collective-permute-start.2) | collective-permute-done | bytes 2097184 | tf_op jit(solution)/shard_map/ppermute | solution.py:18
  351.5 25.0 %collective-permute-start.3 = (bf16[512,2048]{1,0:T(8,128)(2,1)}, bf16[512,2048]{1,0:T(8,128)(2,1)}, u32[]{:S(2)}, u32[]{:S(2)}) collective-permute-start(bf16[512,2048]{1,0:T(8,128)(2,1)} %collective-permute-done.2), channel_id=1, source_target_pairs={{0,1},{1,2},{2,3},{3,4},{4,5},{5,6},{6,7},{8,9},{9,10},{10,11},{11... | collective-permute-start | bytes 6291464 | tf_op jit(solution)/shard_map/ppermute | solution.py:18
  376.7 98.5 %all-gather.3 = bf16[8,1,128]{2,1,0:T(2,128)(2,1)S(1)} all-gather(bf16[1,1,128]{2,1,0:T(2,128)(2,1)S(1)} %bitcast.391), channel_id=1, replica_groups=mesh['batch'=4,'seq'=8] {'seq'}, dimensions={0}, use_global_device_ids=true | all-gather | bytes 2304 | tf_op jit(solution)/shard_map/all_gather | solution.py:235
  475.7 16.2 all-gather.4
  492.6 13.1 all-gather.2
  506.2 22.9 %all-gather.5 = bf16[8,1,512]{2,1,0:T(2,128)(2,1)S(1)} all-gather(bf16[1,1,512]{2,1,0:T(2,128)(2,1)S(1)} %reshape.483), channel_id=1, replica_groups=mesh['batch'=4,'seq'=8] {'seq'}, dimensions={0}, use_global_device_ids=true | all-gather | bytes 9216 | tf_op jit(solution)/shard_map/all_gather | solution.py:238
  532.6 3.5 fusion.72
  540.0 27.5 %conditional.20 = (f32[16,512]{1,0:T(8,128)}, f32[16,512]{1,0:T(8,128)S(1)}) conditional(s32[]{:T(128)} %convert_element_type.264, () %tuple.151, (pred[512,512]{1,0:T(8,128)(4,1)}, bf16[512,1024]{1,0:T(8,128)(2,1)S(1)}, bf16[512,2048]{1,0:T(8,128)(2,1)S(1)}) %tuple.152), branch_computations={%region_9.10_spmd, %region_10.13_spmd} | conditional | flops 566255616 | bytes 45350928 | solution.py:121
  547.8 9.9 fusion
  558.3 9.2 exponential_reduce_fusion
  567.9 5.1 conditional.22
  573.0 4.7 conditional.23
  577.8 4.9 conditional.24
  582.6 22.7 %conditional.25 = (f32[512,16,64]{0,2,1:T(8,128)S(1)}) conditional(s32[]{:T(128)} %convert_element_type.264, () %tuple.150, (pred[512,512]{1,0:T(8,128)(4,1)}, bf16[512,1024]{1,0:T(8,128)(2,1)S(1)}, bf16[512,2048]{1,0:T(8,128)(2,1)S(1)}, f32[16,512]{1,0:T(8,128)}, f32[16,512]{1,0:T(8,128)S(1)}) %tuple.157), branch_computations={%region_29.30_spmd, %region_30.31_spmd} | conditional | flops 1094713344 | bytes 17104932 | solution.py:143
  595.8 9.6 fusion.6
  606.3 5.8 conditional.27
  612.1 6.3 conditional.28
  619.7 3.6 conditional.29
  630.2 29.6 %multiply_convert_fusion.5 = (bf16[512,4096]{1,0:T(8,128)(2,1)}, f32[512,4096]{1,0:T(8,128)}, f32[512,4096]{1,0:T(8,128)}) fusion(f32[4096]{0:T(1024)S(1)} %bitcast.378, bf16[1024,4096]{1,0:T(8,128)(2,1)} %all-gather.16.cloned.1.call-done, f32[512,1024]{1,0:T(8,128)} %copy-done.11, f32[1024]{0:T(1024)S(1)} %bitcast.386, f32[1024]{0:T(1024)S(1)} %bitcast.380, ...), kind=kOutput, calls=%fused_computation.84 | convolution fusion | flops 4436000768 | bytes 31485952 | tf_op jit(solution)/shard_map/dot_general | solution.py:275
  659.8 15.7 fusion.94
  675.5 7.9 multiply_reduce_fusion.5
  690.1 9.2 convolution_convert_fusion.1
  700.5 9.1 convolution_convert_fusion
  716.6 16.4 %conditional.30 = (f32[16,512]{1,0:T(8,128)S(1)}) conditional(s32[]{:T(128)} %convert_element_type.264, () %tuple.163, (pred[512,512]{1,0:T(8,128)(4,1)S(1)}, bf16[512,1024]{1,0:T(8,128)(2,1)S(1)}, bf16[512,2048]{1,0:T(8,128)(2,1)}, f32[16,512]{1,0:T(8,128)}, f32[16,512]{1,0:T(8,128)S(1)}, /*index=5*/bf16[512,16,64]{0,2,1:T(8,128)(2,1)S(1)}) %tuple.402), branch_computations={%region_43.44_spmd, %region_44.46_spmd} | conditional | flops 1098899456 | bytes 50167844 | solution.py:166
  718.2 3.9 copy.220
  726.2 6.4 multiply_reduce_fusion
  733.9 7.8 conditional.33
  742.9 4.5 conditional.39
  748.8 5.3 conditional.38
  754.1 70.8 %collective-permute-done.4 = bf16[512,2048]{0,1:T(8,128)(2,1)} collective-permute-done((bf16[512,2048]{0,1:T(8,128)(2,1)}, bf16[512,2048]{0,1:T(8,128)(2,1)}, u32[]{:S(2)}, u32[]{:S(2)}) %collective-permute-start.4) | collective-permute-done | bytes 2097184 | tf_op jit(solution)/shard_map/ppermute | solution.py:18
  824.9 4.9 add_convert_fusion.4
  831.1 4.3 conditional.37
  835.4 106.9 %collective-permute-done.5 = bf16[512,2048]{0,1:T(8,128)(2,1)} collective-permute-done((bf16[512,2048]{0,1:T(8,128)(2,1)}, bf16[512,2048]{0,1:T(8,128)(2,1)}, u32[]{:S(2)}, u32[]{:S(2)}) %collective-permute-start.5) | collective-permute-done | bytes 2097184 | tf_op jit(solution)/shard_map/ppermute | solution.py:18
  942.3 5.0 add_convert_fusion.3
  948.6 4.3 conditional.36
  952.9 55.7 %collective-permute-done.6 = bf16[512,2048]{0,1:T(8,128)(2,1)} collective-permute-done((bf16[512,2048]{0,1:T(8,128)(2,1)}, bf16[512,2048]{0,1:T(8,128)(2,1)}, u32[]{:S(2)}, u32[]{:S(2)}) %collective-permute-start.6) | collective-permute-done | bytes 2097184 | tf_op jit(solution)/shard_map/ppermute | solution.py:18
  1008.6 4.9 add_convert_fusion.2
  1014.8 36.9 %conditional.35 = (f32[512,16,64]{0,2,1:T(8,128)}, f32[512,2048]{0,1:T(8,128)}) conditional(s32[]{:T(128)} %convert_element_type.264, () %tuple.162, (pred[512,512]{1,0:T(8,128)(4,1)S(1)}, bf16[512,1024]{1,0:T(8,128)(2,1)S(1)}, bf16[512,2048]{1,0:T(8,128)(2,1)}, f32[16,512]{1,0:T(8,128)}, f32[16,512]{1,0:T(8,128)S(1)}, ...), branch_computations={%region_58.59_spmd, %region_59.60_spmd} | conditional | flops 2723151872 | bytes 175472688 | solution.py:205
  1016.6 3.9 copy.235
  1022.2 6.9 exponential_divide_fusion
  1029.1 5.7 copy-done.5
  1036.4 7.3 multiply_convert_fusion
  1045.3 4.0 convolution_bitcast_fusion
  1051.8 5.2 add_convert_fusion.6
  1057.0 4.0 add_convert_fusion.1
  1062.4 7.0 convolution_convert_fusion.2
  1072.9 91.8 %all-gather.6 = bf16[8,1,128]{2,1,0:T(2,128)(2,1)S(1)} all-gather(bf16[1,1,128]{2,1,0:T(2,128)(2,1)S(1)} %bitcast.394), channel_id=1, replica_groups=mesh['batch'=4,'seq'=8] {'seq'}, dimensions={0}, use_global_device_ids=true | all-gather | bytes 2304 | tf_op jit(solution)/shard_map/all_gather | solution.py:239
  1164.8 10.3 fusion.51
  1175.0 101.4 %reduce-scatter.9.cloned.1.call-done = bf16[128,4096]{1,0:T(8,128)(2,1)} async-done(((bf16[1024,4096]{1,0:T(8,128)(2,1)}), bf16[128,4096]{1,0:T(8,128)(2,1)}) %reduce-scatter.9.cloned.1.call-update) | async-done | bytes 1048592 | tf_op jit(solution)/shard_map/reduce_scatter | solution.py:316
  1276.4 152.1 %reduce-scatter.11.cloned.1.call-done = bf16[512,1024]{1,0:T(8,128)(2,1)} async-done(((bf16[4096,1024]{1,0:T(8,128)(2,1)}), bf16[512,1024]{1,0:T(8,128)(2,1)}) %reduce-scatter.11.cloned.1.call-update) | async-done | bytes 1048592 | tf_op jit(solution)/shard_map/reduce_scatter | solution.py:319
  1428.5 119.7 %reduce-scatter.5.cloned.1.call-done = bf16[128,3072]{1,0:T(8,128)(2,1)} async-done(((bf16[1024,3072]{1,0:T(8,128)(2,1)}), bf16[128,3072]{1,0:T(8,128)(2,1)}) %reduce-scatter.5.cloned.1.call-update) | async-done | bytes 786448 | tf_op jit(solution)/shard_map/reduce_scatter | solution.py:310
  1548.3 7.4 fusion.67
  1558.1 29.1 %all-reduce.7 = (bf16[1024]{0:T(1024)(128)(2,1)S(1)}, bf16[1024]{0:T(1024)(128)(2,1)S(1)}, bf16[1024]{0:T(1024)(128)(2,1)S(1)}, bf16[1024]{0:T(1024)(128)(2,1)S(...) all-reduce(bf16[1024]{0:T(1024)(128)(2,1)S(1)} %get-tuple-element.9, ...), channel_id=6, replica_groups=mesh['batch'=4,'seq'=8] {'seq'}, use_global_device_ids=true, to_apply=%region_79.80.clone | all-reduce | flops 10240 | bytes 40960
  1587.7 12.8 all-reduce.8
  1607.4 12.5 all-reduce.12.cloned.1.call-done
  (240 shorter events, 112.1 us)
Async XLA Ops:
  7.2 103.7 %all-gather.12.cloned.1.call-start = ((), (), s32[]{:S(2)}) async-start(), calls=%async_computation.4 | async-start | bytes 7077888 | tf_op jit(solution)/shard_map/all_gather | solution.py:229
  7.9 617.2 %all-gather.14.cloned.1.call-start = ((), (), s32[]{:S(2)}) async-start(), calls=%async_computation.5 | async-start | bytes 2359296 | tf_op jit(solution)/shard_map/all_gather | solution.py:230
  8.7 621.5 %all-gather.16.cloned.1.call-start = ((), (), s32[]{:S(2)}) async-start(), calls=%async_computation.6 | async-start | bytes 9437184 | tf_op jit(solution)/shard_map/all_gather | solution.py:231
  9.4 650.4 %all-gather.18.cloned.1.call-start = ((), (), s32[]{:S(2)}) async-start(), calls=%async_computation.7 | async-start | bytes 9437184 | tf_op jit(solution)/shard_map/all_gather | solution.py:232
  27.4 90.2 %copy-start.42 = (f32[8,1,128]{2,1,0:T(1,128)}, f32[8,1,128]{2,1,0:T(1,128)S(1)}, u32[]{:S(2)}) copy-start(f32[8,1,128]{2,1,0:T(1,128)S(1)} %convert_element_type.311) | copy-start | bytes 12292
  40.6 77.0 %copy-start.57 = (f32[8,1,128]{2,1,0:T(1,128)}, f32[8,1,128]{2,1,0:T(1,128)S(1)}, u32[]{:S(2)}) copy-start(f32[8,1,128]{2,1,0:T(1,128)S(1)} %convert_element_type.312) | copy-start | bytes 12292
  42.0 75.6 %copy-start.44 = (f32[512]{0:T(512)}, f32[512]{0:T(512)S(1)}, u32[]{:S(2)}) copy-start(f32[512]{0:T(512)S(1)} %broadcast_multiply_fusion.1) | copy-start | bytes 6148
  43.7 73.9 %copy-start.48 = (f32[512]{0:T(512)}, f32[512]{0:T(512)S(1)}, u32[]{:S(2)}) copy-start(f32[512]{0:T(512)S(1)} %fusion.48) | copy-start | bytes 6148
  43.7 73.9 %copy-start.50 = (f32[512]{0:T(512)}, f32[512]{0:T(512)S(1)}, u32[]{:S(2)}) copy-start(f32[512]{0:T(512)S(1)} %fusion.59) | copy-start | bytes 6148
  110.9 265.6 %copy-start.68 = (s32[1,4]{1,0:T(1,128)S(1)}, s32[1,4]{1,0:T(1,128)}, u32[]{:S(2)}) copy-start(s32[1,4]{1,0:T(1,128)} %param.56) | copy-start | bytes 52
  110.9 265.8 %copy-start.62 = (bf16[512]{0:T(512)(128)(2,1)S(1)}, bf16[512]{0:T(512)(128)(2,1)}, u32[]{:S(2)}) copy-start(bf16[512]{0:T(512)(128)(2,1)} %param.68) | copy-start | bytes 3076
  110.9 265.8 %copy-start.63 = (bf16[128]{0:T(256)(128)(2,1)S(1)}, bf16[128]{0:T(256)(128)(2,1)}, u32[]{:S(2)}) copy-start(bf16[128]{0:T(256)(128)(2,1)} %param.65) | copy-start | bytes 772
  110.9 364.8 %copy-start.64 = (bf16[128]{0:T(256)(128)(2,1)S(1)}, bf16[128]{0:T(256)(128)(2,1)}, u32[]{:S(2)}) copy-start(bf16[128]{0:T(256)(128)(2,1)} %param.66) | copy-start | bytes 772
  110.9 381.7 %copy-start.65 = (bf16[128]{0:T(256)(128)(2,1)S(1)}, bf16[128]{0:T(256)(128)(2,1)}, u32[]{:S(2)}) copy-start(bf16[128]{0:T(256)(128)(2,1)} %param.67) | copy-start | bytes 772
  110.9 418.9 %copy-start.56 = (s32[1,4096]{1,0:T(1,128)S(1)}, s32[1,4096]{1,0:T(1,128)}, u32[]{:S(2)}) copy-start(s32[1,4096]{1,0:T(1,128)} %param.57) | copy-start | bytes 49156
  117.7 61.3 %copy-start.20 = (bf16[512,3072]{1,0:T(8,128)(2,1)}, bf16[512,3072]{1,0:T(8,128)(2,1)S(1)}, u32[]{:S(2)}) copy-start(bf16[512,3072]{1,0:T(8,128)(2,1)S(1)} %convolution_convert_fusion.3) | copy-start | bytes 9437188
  117.9 464.8 %copy-start.6 = (bf16[512,2048]{1,0:T(8,128)(2,1)}, bf16[512,2048]{1,0:T(8,128)(2,1)S(1)}, u32[]{:S(2)}) copy-start(bf16[512,2048]{1,0:T(8,128)(2,1)S(1)} %slice.154) | copy-start | bytes 6291460
  117.9 61.1 %collective-permute-start = (bf16[512,2048]{1,0:T(8,128)(2,1)S(1)}, bf16[512,2048]{1,0:T(8,128)(2,1)}, u32[]{:S(2)}, u32[]{:S(2)}) collective-permute-start(bf16[512,2048]{1,0:T(8,128)(2,1)S(1)} %slice.154), channel_id=1, source_target_pairs={{0,1},{1,2},{2,3},{3,4},{4,5},{5,6},{6,7},{8,9},{9,10},{10,11},{11... | collective-permute-start | bytes 6291464 | tf_op jit(solution)/shard_map/ppermute | solution.py:18
  179.0 67.9 %collective-permute-start.1 = (bf16[512,2048]{1,0:T(8,128)(2,1)}, bf16[512,2048]{1,0:T(8,128)(2,1)}, u32[]{:S(2)}, u32[]{:S(2)}) collective-permute-start(bf16[512,2048]{1,0:T(8,128)(2,1)} %collective-permute-done), channel_id=1, source_target_pairs={{0,1},{1,2},{2,3},{3,4},{4,5},{5,6},{6,7},{8,9},{9,10},{10,11},{11... | collective-permute-start | bytes 6291464 | tf_op jit(solution)/shard_map/ppermute | solution.py:18
  193.1 981.9 %reduce-scatter.7.cloned.1.call-start = ((), (), s32[]{:S(2)}) async-start(), calls=%async_computation.9 | async-start | bytes 2359296 | tf_op jit(solution)/shard_map/reduce_scatter | solution.py:313
  246.9 104.6 %collective-permute-start.2 = (bf16[512,2048]{1,0:T(8,128)(2,1)}, bf16[512,2048]{1,0:T(8,128)(2,1)}, u32[]{:S(2)}, u32[]{:S(2)}) collective-permute-start(bf16[512,2048]{1,0:T(8,128)(2,1)} %collective-permute-done.1), channel_id=1, source_target_pairs={{0,1},{1,2},{2,3},{3,4},{4,5},{5,6},{6,7},{8,9},{9,10},{10,11},{11... | collective-permute-start | bytes 6291464 | tf_op jit(solution)/shard_map/ppermute | solution.py:18
  351.5 226.3 %collective-permute-start.3 = (bf16[512,2048]{1,0:T(8,128)(2,1)}, bf16[512,2048]{1,0:T(8,128)(2,1)}, u32[]{:S(2)}, u32[]{:S(2)}) collective-permute-start(bf16[512,2048]{1,0:T(8,128)(2,1)} %collective-permute-done.2), channel_id=1, source_target_pairs={{0,1},{1,2},{2,3},{3,4},{4,5},{5,6},{6,7},{8,9},{9,10},{10,11},{11... | collective-permute-start | bytes 6291464 | tf_op jit(solution)/shard_map/ppermute | solution.py:18
  588.9 6.8 copy-start.26
  619.7 5.4 copy-start.7
  619.7 5.4 copy-start.41
  623.3 6.8 copy-start.52
  623.3 6.8 copy-start.53
  623.3 6.8 copy-start.59
  625.1 34.7 %copy-start.18 = (bf16[512,16,64]{0,2,1:T(8,128)(2,1)}, bf16[512,16,64]{0,2,1:T(8,128)(2,1)S(1)}, u32[]{:S(2)}) copy-start(bf16[512,16,64]{0,2,1:T(8,128)(2,1)S(1)} %convert_element_type.269) | copy-start | bytes 3145732
  659.8 15.7 copy-start.12
  659.8 15.7 copy-start.67
  675.5 9.9 copy-start.14
  684.1 15.2 copy-start.46
  690.0 586.4 %reduce-scatter.9.cloned.1.call-start = ((), (), s32[]{:S(2)}) async-start(), calls=%async_computation.10 | async-start | bytes 9437184 | tf_op jit(solution)/shard_map/reduce_scatter | solution.py:316
  699.3 729.2 %reduce-scatter.11.cloned.1.call-start = ((), (), s32[]{:S(2)}) async-start(), calls=%async_computation.11 | async-start | bytes 9437184 | tf_op jit(solution)/shard_map/reduce_scatter | solution.py:319
  709.6 6.9 copy-start.24
  709.7 838.6 %reduce-scatter.5.cloned.1.call-start = ((), (), s32[]{:S(2)}) async-start(), calls=%async_computation.8 | async-start | bytes 7077888 | tf_op jit(solution)/shard_map/reduce_scatter | solution.py:310
  733.9 7.8 copy-start.30
  742.9 5.8 copy-start.28
  747.5 77.4 %collective-permute-start.4 = (bf16[512,2048]{0,1:T(8,128)(2,1)}, bf16[512,2048]{0,1:T(8,128)(2,1)}, u32[]{:S(2)}, u32[]{:S(2)}) collective-permute-start(bf16[512,2048]{0,1:T(8,128)(2,1)} %get-tuple-element.486), channel_id=1, source_target_pairs={{1,0},{2,1},{3,2},{4,3},{5,4},{6,5},{7,6},{9,8},{10,9},{11,10},{12... | collective-permute-start | bytes 6291464 | tf_op jit(solution)/shard_map/ppermute | solution.py:18
  754.1 77.0 %copy-start.23 = (pred[512,512]{1,0:T(8,128)(4,1)S(1)}, pred[512,512]{1,0:T(8,128)(4,1)}, u32[]{:S(2)}) copy-start(pred[512,512]{1,0:T(8,128)(4,1)} %get-tuple-element.1036) | copy-start | bytes 786436
  829.8 112.5 %collective-permute-start.5 = (bf16[512,2048]{0,1:T(8,128)(2,1)}, bf16[512,2048]{0,1:T(8,128)(2,1)}, u32[]{:S(2)}, u32[]{:S(2)}) collective-permute-start(bf16[512,2048]{0,1:T(8,128)(2,1)} %add_convert_fusion.4), channel_id=1, source_target_pairs={{1,0},{2,1},{3,2},{4,3},{5,4},{6,5},{7,6},{9,8},{10,9},{11,10},{12... | collective-permute-start | bytes 6291464 | tf_op jit(solution)/shard_map/ppermute | solution.py:18
  835.4 113.2 %copy-start.27 = (pred[512,512]{1,0:T(8,128)(4,1)S(1)}, pred[512,512]{1,0:T(8,128)(4,1)}, u32[]{:S(2)}) copy-start(pred[512,512]{1,0:T(8,128)(4,1)} %get-tuple-element.1090) | copy-start | bytes 786436
  947.3 61.3 %collective-permute-start.6 = (bf16[512,2048]{0,1:T(8,128)(2,1)}, bf16[512,2048]{0,1:T(8,128)(2,1)}, u32[]{:S(2)}, u32[]{:S(2)}) collective-permute-start(bf16[512,2048]{0,1:T(8,128)(2,1)} %add_convert_fusion.3), channel_id=1, source_target_pairs={{1,0},{2,1},{3,2},{4,3},{5,4},{6,5},{7,6},{9,8},{10,9},{11,10},{12... | collective-permute-start | bytes 6291464 | tf_op jit(solution)/shard_map/ppermute | solution.py:18
  952.9 61.9 %copy-start.25 = (pred[512,512]{1,0:T(8,128)(4,1)S(1)}, pred[512,512]{1,0:T(8,128)(4,1)}, u32[]{:S(2)}) copy-start(pred[512,512]{1,0:T(8,128)(4,1)} %get-tuple-element.1032) | copy-start | bytes 786436
  1013.5 43.5 %collective-permute-start.7 = (bf16[512,2048]{0,1:T(8,128)(2,1)}, bf16[512,2048]{0,1:T(8,128)(2,1)}, u32[]{:S(2)}, u32[]{:S(2)}) collective-permute-start(bf16[512,2048]{0,1:T(8,128)(2,1)} %add_convert_fusion.2), channel_id=1, source_target_pairs={{1,0},{2,1},{3,2},{4,3},{5,4},{6,5},{7,6},{9,8},{10,9},{11,10},{12... | collective-permute-start | bytes 6291464 | tf_op jit(solution)/shard_map/ppermute | solution.py:18
  1029.1 5.8 copy-start.5
  1051.8 10.6 copy-start.8
  1051.8 10.6 copy-start.43
  1051.8 10.6 copy-start.45
  1051.8 10.6 copy-start.51
  1051.8 10.6 copy-start.58
  1057.0 4.0 copy-start.35
  1062.4 7.3 copy-start.69
  1062.4 10.6 copy-start.66
  1062.4 102.4 %copy-start.13 = (f32[512,1024]{1,0:T(8,128)S(1)}, f32[512,1024]{1,0:T(8,128)}, u32[]{:S(2)}) copy-start(f32[512,1024]{1,0:T(8,128)} %copy-done.11) | copy-start | bytes 6291460
  1069.4 550.4 %all-reduce.12.cloned.1.call-start = ((), (), s32[]{:S(2)}) async-start(), calls=%async_computation.12 | async-start | bytes 6291456 | tf_op jit(solution)/shard_map/psum | solution.py:345
  1548.3 7.5 copy-start.49
  1548.3 9.8 copy-start.54
  1548.3 9.8 copy-start.55
  1548.3 9.8 copy-start.60
  1548.3 9.8 copy-start.61
  1548.3 55.8 %copy-start.10 = (f32[512,1024]{1,0:T(8,128)S(1)}, f32[512,1024]{1,0:T(8,128)}, u32[]{:S(2)}) copy-start(f32[512,1024]{1,0:T(8,128)} %copy-done.9) | copy-start | bytes 6291460
  1548.3 55.8 %copy-start.47 = (f32[512]{0:T(512)S(1)}, f32[512]{0:T(512)}, u32[]{:S(2)}) copy-start(f32[512]{0:T(512)} %copy-done.46) | copy-start | bytes 6148
  (13 other events, 20.3 us)
Sparse Core Ops, SparseCore 0:
  10.2 100.6 all-gather.11
  113.0 63.7 all-gather.13
  178.9 189.4 all-gather.15
  370.4 170.5 all-gather.17
  690.2 388.2 reduce-scatter.6
  1081.9 194.4 reduce-scatter.8
  1280.5 147.9 reduce-scatter.10
  1432.1 116.0 reduce-scatter.4
  1550.8 68.9 all-reduce.11
where the time goes:
time: 1640 us
  waiting for transfers between devices  869 us (53%)
  blocking collectives  315 us (19%)
  matrix products  162 us (10%)
  starting transfers between devices  83.2 us (5%)
  other arithmetic  70.4 us (4%)
  local copies, waits for them, and re-layouts  68.3 us (4%)
  loops' own time  48.2 us (3%)
  between operations  19.5 us (1%)
    ppermute x8, waiting for transfers between devices, shifted(): return lax.ppermute(block, axis, route)  414 us
    reduce_scatter x1, waiting for transfers between devices, shards(): lax.psum_scatter(grad_down_w.astype(jnp.bfloat16), 'seq', scatter_dimensi...  152 us
    reduce_scatter x1, waiting for transfers between devices, shards(): lax.psum_scatter(grad_qkv_w.astype(jnp.bfloat16), 'seq', scatter_dimensio...  120 us
    reduce_scatter x1, waiting for transfers between devices, shards(): lax.psum_scatter(grad_up_w.astype(jnp.bfloat16), 'seq', scatter_dimension...  101 us
    all_gather x1, blocking collectives, shards(): lax.all_gather(ln2_gain, 'seq', axis=0, tiled=True)  98.5 us
    all_gather x1, blocking collectives, shards(): lax.all_gather(down_bias, 'seq', axis=0, tiled=True)  91.8 us
    ppermute x8, starting transfers between devices, shifted(): return lax.ppermute(block, axis, route)  82.7 us
    all_gather x1, waiting for transfers between devices, shards(): lax.all_gather(w_qkv, 'seq', axis=0, tiled=True)  67.1 us
  transfers between devices with their start and end apart: 17, of which 11 were waited for; matrix products, arithmetic and copies ran while one was open for 15% of the time, Pallas kernels for 0%

commit v1 on v0

--- a/solution.py
+++ b/solution.py
@@ -1,6 +1,8 @@
 import jax
 import jax.numpy as jnp
 from jax import lax
+from jax.experimental import pallas as pl
+from jax.experimental.pallas import tpu as pltpu
 from jax.sharding import PartitionSpec as P
 
 HEAD_COUNT = 16
@@ -371,9 +373,968 @@
     )
 
 
+LANES = 128
+TILE = 512
+UTTERANCES = 4
+SHRINK = 1
+PARAMS = pltpu.CompilerParams(dimension_semantics=("arbitrary",), vmem_limit_bytes=56 << 20)
+
+
+def dot_nt(left, right):
+    return lax.dot_general(
+        left, right, (((1,), (1,)), ((), ())), preferred_element_type=jnp.float32
+    )
+
+
+def dot_nn(left, right):
+    return lax.dot_general(
+        left, right, (((1,), (0,)), ((), ())), preferred_element_type=jnp.float32
+    )
+
+
+def dot_tn(left, right):
+    return lax.dot_general(
+        left, right, (((0,), (0,)), ((), ())), preferred_element_type=jnp.float32
+    )
+
+
+def norm_stats(values):
+    centre = jnp.mean(values, axis=-1, keepdims=True)
+    centred = values - centre
+    spread = jnp.mean(centred * centred, axis=-1, keepdims=True)
+    inverse = lax.rsqrt(spread + EPSILON)
+    return centred * inverse, inverse
+
+
+def norm_back(grad, normed, inverse, gain):
+    g = grad * gain
+    return inverse * (
+        g
+        - jnp.mean(g, axis=-1, keepdims=True)
+        - normed * jnp.mean(g * normed, axis=-1, keepdims=True)
+    )
+
+
+def whole(*shape):
+    return pl.BlockSpec(shape, lambda *_: (0,) * len(shape))
+
+
+def like(shape, kind):
+    return jax.ShapeDtypeStruct(shape, kind)
+
+
+def call(kernel, name, grid, in_specs, out_specs, out_shape, scratch=(), flops=0):
+    def run(ids, *args):
+        bytes_accessed = sum(a.size * a.dtype.itemsize for a in args)
+        return pl.pallas_call(
+            kernel,
+            out_shape=out_shape,
+            grid_spec=pltpu.PrefetchScalarGridSpec(
+                num_scalar_prefetch=1,
+                grid=(grid,),
+                in_specs=in_specs,
+                out_specs=out_specs,
+                scratch_shapes=list(scratch),
+            ),
+            compiler_params=PARAMS,
+            cost_estimate=pl.CostEstimate(
+                flops=flops // SHRINK,
+                bytes_accessed=2 * bytes_accessed // SHRINK,
+                transcendentals=0,
+            ),
+            name=name,
+        )(ids, *args)
+
+    return run
+
+
+CORE, CHIP_X, SQUARE, Y_BIT = 0, 1, 2, 3
+
+
+def norm_kernel(ids, tokens, vectors, out):
+    normed, _ = norm_stats(tokens[...].astype(jnp.float32))
+    out[...] = (normed * vectors[0:1, :] + vectors[1:2, :]).astype(jnp.bfloat16)
+
+
+def project_kernel(ids, own, y_one, z_one, top, bottom, w_own, w_other, out, leaving, natural):
+    square = ids[SQUARE]
+    width = own.shape[1]
+    part = width // 8
+    weights = [w[:, 0:part, :].reshape(width, 3 * LANES) for w in (w_own, w_other)]
+    corner = jnp.where(pl.program_id(0) < 2, top[...], bottom[...])
+    for j, rows in enumerate((own[...], y_one[...], z_one[...], corner)):
+        at = pl.ds(square ^ j, 1)
+        natural[at] = rows[None]
+        out[at] = dot_nn(rows, weights[0]).astype(jnp.bfloat16)[None]
+        leaving[at] = dot_nn(rows, weights[1]).astype(jnp.bfloat16)[None]
+
+
+def head_lanes(block, head):
+    lane = lax.broadcasted_iota(jnp.int32, block.shape, 1)
+    keep = (lane < HEAD_DIM) if head == 0 else (lane >= HEAD_DIM)
+    return jnp.where(keep, block, jnp.zeros_like(block))
+
+
+def join_heads(ids, own, came, qkv):
+    half = own.shape[0]
+    for rows, side in ((own, ids[CORE]), (came, 1 - ids[CORE])):
+        at = pl.ds(pl.multiple_of(side * half, half), half)
+        qkv[at, 0:LANES] = rows[:, 0:LANES] * jnp.bfloat16(HEAD_DIM ** (-0.5))
+        qkv[at, LANES : 3 * LANES] = rows[:, LANES : 3 * LANES]
+
+
+def first_frames(bounds, positions):
+    start = jnp.zeros_like(positions)
+    for u in range(1, UTTERANCES):
+        start = jnp.where(positions >= bounds[4, u], bounds[4, u], start)
+    return start
+
+
+def attend_kernel(ids, bounds, own, came, bias_row, out, lse, qkv, top, total, acc):
+    tile = pl.program_id(0)
+    base = pl.multiple_of(tile * TILE, TILE)
+
+    @pl.when(tile == 0)
+    def _():
+        join_heads(ids, own, came, qkv)
+
+    queries = [head_lanes(qkv[pl.ds(base, TILE), 0:LANES], head) for head in range(2)]
+    top[...] = jnp.full_like(top, NEGATIVE)
+    total[...] = jnp.zeros_like(total)
+    acc[...] = jnp.zeros_like(acc)
+
+    def step(j, masked):
+        at = pl.multiple_of(j * TILE, TILE)
+        keys = qkv[pl.ds(at, TILE), LANES : 2 * LANES]
+        values = qkv[pl.ds(at, TILE), 2 * LANES : 3 * LANES]
+        bias = bias_row[:, pl.ds(at, TILE)]
+        if masked:
+            key_pos = at + lax.broadcasted_iota(jnp.int32, (TILE, TILE), 1)
+            query_pos = base + lax.broadcasted_iota(jnp.int32, (TILE, TILE), 0)
+            column = base + lax.broadcasted_iota(jnp.int32, (TILE, 1), 0)
+            allowed = (
+                (key_pos >= first_frames(bounds, column))
+                & (key_pos <= query_pos)
+                & ((bias == 0.0) | (key_pos == query_pos))
+            )
+        for head in range(2):
+            scores = dot_nt(queries[head], keys)
+            if masked:
+                scores = jnp.where(allowed, scores, NEGATIVE)
+            else:
+                scores = scores + bias
+            old = top[head]
+            new = jnp.maximum(old, jnp.max(scores, axis=1, keepdims=True))
+            probs = jnp.exp(scores - new[:, 0:1])
+            shrink = jnp.exp(old - new)
+            total[head] = total[head] * shrink + jnp.sum(probs, axis=1, keepdims=True)
+            acc[head] = acc[head] * shrink + dot_nn(probs.astype(jnp.bfloat16), values)
+            top[head] = new
+
+    def masked_step(j, carry):
+        step(j, True)
+        return carry
+
+    def free_step(j, carry):
+        step(j, False)
+        return carry
+
+    lax.fori_loop(bounds[0, tile], bounds[1, tile], masked_step, 0)
+    lax.fori_loop(bounds[1, tile], tile, free_step, 0)
+    step(tile, True)
+    lane = lax.broadcasted_iota(jnp.int32, (TILE, LANES), 1)
+    out[0] = jnp.where(lane < HEAD_DIM, acc[0] / total[0], acc[1] / total[1]).astype(jnp.bfloat16)
+    for head in range(2):
+        column = top[head] + jnp.log(total[head])
+        lse[head : head + 1, pl.ds(base, TILE)] = jnp.transpose(column)[0:1, :]
+
+
+def block_order(i):
+    return 2 * (i % 4) + i // 4
+
+
+def attend(ids, bounds, own, came, bias_row):
+    rows = 2 * own.shape[0]
+    return pl.pallas_call(
+        attend_kernel,
+        out_shape=(like((8, TILE, LANES), jnp.bfloat16), like((2, rows), jnp.float32)),
+        grid_spec=pltpu.PrefetchScalarGridSpec(
+            num_scalar_prefetch=2,
+            grid=(rows // TILE,),
+            in_specs=[
+                whole(*own.shape),
+                whole(*came.shape),
+                whole(1, rows),
+            ],
+            out_specs=[
+                pl.BlockSpec((1, TILE, LANES), lambda i, *_: (block_order(i), 0, 0)),
+                whole(2, rows),
+            ],
+            scratch_shapes=[pltpu.VMEM((rows, 3 * LANES), jnp.bfloat16)]
+            + [pltpu.VMEM((2, TILE, LANES), jnp.float32)] * 3,
+        ),
+        compiler_params=PARAMS,
+        cost_estimate=pl.CostEstimate(
+            flops=rows * rows * 256 // SHRINK, bytes_accessed=rows * 2400, transcendentals=rows * rows
+        ),
+        name="attend",
+    )(ids, bounds, own, came, bias_row)
+
+
+def attend_back_kernel(
+    ids,
+    bounds,
+    own,
+    came,
+    grad_own,
+    grad_came,
+    attended,
+    bias_row,
+    lse,
+    out,
+    leaving,
+    qkv,
+    grad,
+    delta,
+    grad_queries,
+    grad_kv,
+):
+    tile = pl.program_id(0)
+    base = pl.multiple_of(tile * TILE, TILE)
+    core = ids[CORE]
+
+    @pl.when(tile == 0)
+    def _():
+        join_heads(ids, own, came, qkv)
+        grad_queries[...] = jnp.zeros_like(grad_queries)
+        for j in range(4):
+            for rows, side in ((grad_own, core), (grad_came, 1 - core)):
+                at = pl.multiple_of((4 * side + j) * TILE, TILE)
+                block = rows[pl.ds(2 * j + core, 1)].reshape(TILE, LANES)
+                grad[pl.ds(at, TILE), :] = block
+                product = block.astype(jnp.float32) * attended[
+                    pl.ds(2 * j + side, 1)
+                ].reshape(TILE, LANES).astype(jnp.float32)
+                turned = jnp.transpose(product)
+                delta[0:1, pl.ds(at, TILE)] = jnp.sum(turned[:HEAD_DIM], axis=0, keepdims=True)
+                delta[1:2, pl.ds(at, TILE)] = jnp.sum(turned[HEAD_DIM:], axis=0, keepdims=True)
+
+    keys = qkv[pl.ds(base, TILE), LANES : 2 * LANES]
+    values = qkv[pl.ds(base, TILE), 2 * LANES : 3 * LANES]
+    head_keys = [head_lanes(keys, head) for head in range(2)]
+    bias = jnp.broadcast_to(bias_row[:, pl.ds(base, TILE)], (LANES, TILE))
+    bias = jnp.transpose(bias)[:, 0:1]
+    grad_kv[...] = jnp.zeros_like(grad_kv)
+
+    def step(i, masked):
+        at = pl.multiple_of(i * TILE, TILE)
+        scaled = qkv[pl.ds(at, TILE), 0:LANES]
+        grads = grad[pl.ds(at, TILE), :]
+        if masked:
+            key_pos = base + lax.broadcasted_iota(jnp.int32, (TILE, TILE), 0)
+            query_pos = at + lax.broadcasted_iota(jnp.int32, (TILE, TILE), 1)
+            row = at + lax.broadcasted_iota(jnp.int32, (1, TILE), 1)
+            allowed = (
+                (key_pos >= first_frames(bounds, row))
+                & (key_pos <= query_pos)
+                & ((bias == 0.0) | (key_pos == query_pos))
+            )
+        query_part = jnp.zeros((TILE, LANES), jnp.float32)
+        key_part = grad_kv[0]
+        value_part = grad_kv[1]
+        for head in range(2):
+            queries = head_lanes(scaled, head)
+            head_grads = head_lanes(grads, head)
+            scores = dot_nt(keys, queries)
+            if masked:
+                scores = jnp.where(allowed, scores, NEGATIVE)
+            else:
+                scores = scores + bias
+            probs = jnp.exp(scores - lse[head : head + 1, pl.ds(at, TILE)])
+            dprobs = dot_nt(values, head_grads)
+            dscores = (probs * (dprobs - delta[head : head + 1, pl.ds(at, TILE)])).astype(
+                jnp.bfloat16
+            )
+            value_part = value_part + dot_nn(probs.astype(jnp.bfloat16), head_grads)
+            key_part = key_part + dot_nn(dscores, queries)
+            query_part = query_part + dot_tn(dscores, head_keys[head])
+        grad_kv[0] = key_part
+        grad_kv[1] = value_part
+        grad_queries[pl.ds(at, TILE), :] += query_part
+
+    def masked_step(i, carry):
+        step(i, True)
+        return carry
+
+    def free_step(i, carry):
+        step(i, False)
+        return carry
+
+    step(tile, True)
+    lax.fori_loop(tile + 1, bounds[2, tile], free_step, 0)
+    lax.fori_loop(bounds[2, tile], bounds[3, tile], masked_step, 0)
+
+    def store(target):
+        at = pl.ds(pl.multiple_of((tile % 4) * TILE, TILE), TILE)
+        target[at, 0:LANES] = (
+            grad_queries[pl.ds(base, TILE), :] * HEAD_DIM ** (-0.5)
+        ).astype(jnp.bfloat16)
+        target[at, LANES : 2 * LANES] = grad_kv[0].astype(jnp.bfloat16)
+        target[at, 2 * LANES : 3 * LANES] = grad_kv[1].astype(jnp.bfloat16)
+
+    @pl.when(tile // 4 == core)
+    def _():
+        store(out)
+
+    @pl.when(tile // 4 != core)
+    def _():
+        store(leaving)
+
+
+def attend_back(ids, bounds, own, came, grad_own, grad_came, attended, bias_row, lse):
+    half = own.shape[0]
+    rows = 2 * half
+    return pl.pallas_call(
+        attend_back_kernel,
+        out_shape=(like(own.shape, jnp.bfloat16), like(own.shape, jnp.bfloat16)),
+        grid_spec=pltpu.PrefetchScalarGridSpec(
+            num_scalar_prefetch=2,
+            grid=(rows // TILE,),
+            in_specs=[
+                whole(*own.shape),
+                whole(*came.shape),
+                whole(*grad_own.shape),
+                whole(*grad_came.shape),
+                whole(*attended.shape),
+                whole(1, rows),
+                whole(2, rows),
+            ],
+            out_specs=[whole(*own.shape), whole(*own.shape)],
+            scratch_shapes=[
+                pltpu.VMEM((rows, 3 * LANES), jnp.bfloat16),
+                pltpu.VMEM((rows, LANES), jnp.bfloat16),
+                pltpu.VMEM((2, rows), jnp.float32),
+                pltpu.VMEM((rows, LANES), jnp.float32),
+                pltpu.VMEM((2, TILE, LANES), jnp.float32),
+            ],
+        ),
+        compiler_params=PARAMS,
+        cost_estimate=pl.CostEstimate(
+            flops=rows * rows * 640 // SHRINK, bytes_accessed=rows * 2400, transcendentals=rows * rows
+        ),
+        name="attend_back",
+    )(ids, bounds, own, came, grad_own, grad_came, attended, bias_row, lse)
+
+
+def attend_bounds(start, starts, rows):
+    tiles = rows // TILE
+    index = jnp.arange(tiles, dtype=jnp.int32)
+    first = start[:: TILE]
+    last = start[TILE - 1 :: TILE]
+    low = first // TILE
+    middle = jnp.clip((last + TILE - 1) // TILE, low, index)
+    key_first = index * TILE
+    free_end = jnp.sum((last[None, :] <= key_first[:, None]).astype(jnp.int32), axis=1)
+    free_end = jnp.maximum(free_end, index + 1)
+    far_end = jnp.sum(
+        (first[None, :] <= key_first[:, None] + TILE - 1).astype(jnp.int32), axis=1
+    )
+    starts = jnp.pad(starts, (0, tiles - starts.shape[0]))
+    return jnp.stack([low, middle, free_end, far_end, starts]).astype(jnp.int32)
+
+
+def out_kernel(ids, own, came, tokens, w_out, vectors, attended, middle, normed):
+    core = ids[CORE]
+    rows, width = tokens.shape
+    mine, other = [], []
+    for j in range(4):
+        mine.append(own[pl.ds(2 * j + core, 1)].reshape(rows, LANES))
+        other.append(came[pl.ds(2 * j + core, 1)].reshape(rows, LANES))
+    mine, other = jnp.concatenate(mine, axis=1), jnp.concatenate(other, axis=1)
+    first = jnp.where(core == 0, mine, other)
+    second = jnp.where(core == 0, other, mine)
+    joined = jnp.concatenate([first, second], axis=1)
+    attended[...] = joined
+    branch = dot_nn(joined, w_out[...].reshape(width, width)) + vectors[4:5, :]
+    value = tokens[...].astype(jnp.float32) + branch
+    middle[...] = value
+    xhat, _ = norm_stats(value)
+    normed[...] = (xhat * vectors[2:3, :] + vectors[3:4, :]).astype(jnp.bfloat16)
+
+
+def forward_kernel(
+    ids,
+    normed_own,
+    normed_came,
+    grad_own,
+    grad_came,
+    up_a,
+    up_b,
+    down_a,
+    down_b,
+    vectors,
+    act,
+    grad_up,
+    up_bias,
+    result_own,
+    result_came,
+    back_own,
+    back_came,
+    result,
+    back,
+):
+    step = pl.program_id(0)
+    core = ids[CORE]
+    frames, width = normed_own.shape
+
+    @pl.when(step == 0)
+    def _():
+        result[...] = jnp.zeros_like(result)
+        back[...] = jnp.zeros_like(back)
+
+    w_up = jnp.concatenate(
+        [up_a[...].reshape(width, LANES), up_b[...].reshape(width, LANES)], axis=1
+    )
+    w_down = jnp.concatenate(
+        [down_a[...].reshape(LANES, width), down_b[...].reshape(LANES, width)], axis=0
+    )
+    shift = jnp.where(
+        core == 0,
+        jnp.concatenate([vectors[6:7, :], vectors[7:8, :]], axis=1),
+        jnp.concatenate([vectors[8:9, :], vectors[9:10, :]], axis=1),
+    )
+    bias = jnp.zeros((1, 2 * LANES), jnp.float32)
+    for side, (normed, grad) in enumerate(((normed_own, grad_own), (normed_came, grad_came))):
+        value = dot_nn(normed[...], w_up) + shift
+        half = 0.5 + 0.5 * lax.erf(value * 0.7071067811865476)
+        bell = jnp.exp(-0.5 * value * value) * 0.3989422804014327
+        activated = (value * half).astype(jnp.bfloat16)
+        act[side] = activated
+        change = dot_nt(grad[...], w_down) * (half + value * bell)
+        bias = bias + jnp.sum(change.astype(jnp.bfloat16).astype(jnp.float32), axis=0, keepdims=True)
+        change = change.astype(jnp.bfloat16)
+        grad_up[side] = change
+        result[side] += dot_nn(activated, w_down)
+        back[side] += dot_nt(change, w_up)
+    up_bias[0:1, :] = bias[:, 0:LANES]
+    up_bias[1:2, :] = bias[:, LANES:]
+
+    @pl.when(step == 7)
+    def _():
+        result_own[...] = result[0]
+        result_came[...] = result[1].astype(jnp.bfloat16)
+        back_own[...] = back[0]
+        back_came[...] = back[1].astype(jnp.bfloat16)
+
+
+def middle_kernel(
+    ids, back_own, back_came, middle, cotangent, w_out, vectors, grad_middle, grad_branch, out, sums
+):
+    step = pl.program_id(0)
+    xhat, inverse = norm_stats(middle[...])
+    grad = back_own[...] + back_came[...].astype(jnp.float32)
+    value = cotangent[...].astype(jnp.float32) + norm_back(grad, xhat, inverse, vectors[2:3, :])
+    grad_middle[...] = value
+    low = value.astype(jnp.bfloat16)
+    grad_branch[...] = low
+
+    @pl.when(step == 0)
+    def _():
+        sums[...] = jnp.zeros_like(sums)
+
+    sums[0:1, :] += jnp.sum(grad * xhat, axis=0, keepdims=True)
+    sums[1:2, :] += jnp.sum(grad, axis=0, keepdims=True)
+    sums[2:3, :] += jnp.sum(low.astype(jnp.float32), axis=0, keepdims=True)
+    sums[3:4, :] += jnp.sum(cotangent[...].astype(jnp.float32), axis=0, keepdims=True)
+    width = w_out.shape[-1]
+    spread = dot_nt(low, w_out[...].reshape(width, width)).astype(jnp.bfloat16)
+    for group in range(8):
+        out[block_order(group)] = spread[:, group * LANES : (group + 1) * LANES]
+
+
+def grad_out_kernel(ids, attended, grad_branch, kept, leaving):
+    core = ids[CORE]
+    grad = dot_tn(attended[...], grad_branch[...]).astype(jnp.bfloat16)
+    half = grad.shape[1] // 2
+    shape = kept.shape
+    kept[...] = jnp.where(core == 0, grad[:, :half], grad[:, half:]).reshape(shape)
+    leaving[...] = jnp.where(core == 0, grad[:, half:], grad[:, :half]).reshape(shape)
+
+
+def grad_down_kernel(ids, act, grad_own, grad_came, out):
+    grad = dot_tn(act[0], grad_own[...]) + dot_tn(act[1], grad_came[...])
+    out[...] = grad.astype(jnp.bfloat16)
+
+
+def grad_up_kernel(ids, normed_own, normed_came, grad_up, out_own, out_came, kept, leaving):
+    chip_x = ids[CHIP_X]
+    grad = (dot_tn(normed_own[...], grad_up[0]) + dot_tn(normed_came[...], grad_up[1])).astype(
+        jnp.bfloat16
+    )
+    half = grad.shape[1] // 2
+    shape = kept.shape[:2] + (half,)
+    kept[:, :, :half] = jnp.where(chip_x == 0, grad[:, :half], grad[:, half:]).reshape(shape)
+    leaving[:, :, :half] = jnp.where(chip_x == 0, grad[:, half:], grad[:, :half]).reshape(shape)
+    more = (out_own[...].astype(jnp.float32) + out_came[...].astype(jnp.float32)).astype(
+        jnp.bfloat16
+    )
+    cut = more.shape[2] // 2
+    kept[:, :, half:] = jnp.where(chip_x == 0, more[:, :, :cut], more[:, :, cut:])
+    leaving[:, :, half:] = jnp.where(chip_x == 0, more[:, :, cut:], more[:, :, :cut])
+
+
+def back_project_kernel(ids, own, came, w_own, w_other, first, y_out, z_out, keep_left, keep_right):
+    square = ids[SQUARE]
+    width = first.shape[1]
+    part = width // 8
+    half = width // 2
+    weights = [w[:, 0:part, :].reshape(width, 3 * LANES) for w in (w_own, w_other)]
+    for j in range(4):
+        at = square ^ j
+        value = dot_nt(own[at], weights[0]) + dot_nt(came[at], weights[1])
+        if j == 0:
+            first[...] = value
+        if j == 1:
+            y_out[0] = value[:, :half].astype(jnp.bfloat16)
+            keep_right[...] = value[:, half:]
+        if j == 2:
+            z_out[0] = value[:, half:].astype(jnp.bfloat16)
+            keep_left[...] = value[:, :half]
+        if j == 3:
+            y_out[1] = value[:, :half].astype(jnp.bfloat16)
+            z_out[1] = value[:, half:].astype(jnp.bfloat16)
+
+
+def second_kernel(ids, keep_left, keep_right, y_came, z_came, z_out, y_out):
+    z_out[...] = (keep_left[...] + y_came[1].astype(jnp.float32)).astype(jnp.bfloat16)
+    y_out[...] = (keep_right[...] + z_came[1].astype(jnp.float32)).astype(jnp.bfloat16)
+
+
+def last_kernel(
+    ids, first, y_came, z_came, z_second, y_second, tokens, grad_middle, vectors, out, sums
+):
+    step = pl.program_id(0)
+    wide = jnp.float32
+    left = y_came[0].astype(wide) + z_second[...].astype(wide)
+    right = z_came[0].astype(wide) + y_second[...].astype(wide)
+    grad = first[...] + jnp.concatenate([left, right], axis=1)
+    xhat, inverse = norm_stats(tokens[...].astype(wide))
+    out[...] = (grad_middle[...] + norm_back(grad, xhat, inverse, vectors[0:1, :])).astype(
+        jnp.bfloat16
+    )
+
+    @pl.when(step == 0)
+    def _():
+        sums[...] = jnp.zeros_like(sums)
+
+    sums[0:1, :] += jnp.sum(grad * xhat, axis=0, keepdims=True)
+    sums[1:2, :] += jnp.sum(grad, axis=0, keepdims=True)
+
+
+def grad_heads_kernel(ids, normed, own, came, out, leaving):
+    out[...] = dot_tn(normed[...], own[...]).astype(jnp.bfloat16)
+    leaving[...] = dot_tn(normed[...], came[...]).astype(jnp.bfloat16)
+
+
+def hop_batch(block, bit):
+    size = lax.axis_size("batch")
+    return lax.ppermute(block, "batch", [(i, i ^ bit) for i in range(size)])
+
+
+def hop_seq(block, bits):
+    size = lax.axis_size("seq")
+    return lax.ppermute(block, "seq", [(i, i ^ bits) for i in range(size)])
+
+
+def swap_halves(block):
+    batches, seqs = lax.axis_size("batch"), lax.axis_size("seq")
+    route = []
+    for b in range(batches):
+        for s in range(seqs):
+            target = ((b & ~1) | (s >> 2)) * seqs + ((s & 3) | ((b & 1) << 2))
+            route.append((b * seqs + s, target))
+    return lax.ppermute(block, ("batch", "seq"), route)
+
+
+def after(value, *anchors):
+    return lax.optimization_barrier((value,) + anchors)[0]
+
+
+def trade(block, groups):
+    return lax.all_to_all(block, "seq", 0, 0, tiled=True, axis_index_groups=groups)
+
+
+IN_SQUARE = [[0, 1, 2, 3], [4, 5, 6, 7]]
+ALONG_Z = [[0, 2, 4, 6], [1, 3, 5, 7]]
+
+
+def by_side(side, own, other, axis):
+    return jnp.where(
+        side == 0,
+        jnp.concatenate([own, other], axis=axis),
+        jnp.concatenate([other, own], axis=axis),
+    )
+
+
+def square_shards(
+    tokens,
+    lengths,
+    key_mask,
+    cotangent,
+    w_qkv,
+    w_out,
+    w_up,
+    w_down,
+    ln1_gain,
+    ln1_bias,
+    ln2_gain,
+    ln2_bias,
+    out_bias,
+    up_bias,
+    down_bias,
+):
+    low, wide = jnp.bfloat16, jnp.float32
+    batch_index = lax.axis_index("batch")
+    seq_index = lax.axis_index("seq")
+    core = batch_index & 1
+    chip_x = batch_index >> 1
+    square = seq_index & 3
+    y_bit = seq_index & 1
+    ids = jnp.stack([core, chip_x, square, y_bit]).astype(jnp.int32)
+    frames, width = tokens.shape[1], tokens.shape[2]
+    rows = 8 * frames
+    part = width // 8
+    quarter = 2 * core + chip_x
+
+    up_piece = lax.dynamic_index_in_dim(w_up.reshape(part, 8, 4, LANES), quarter, 2, False)
+    down_piece = lax.dynamic_slice_in_dim(w_down, quarter * part, part, 0)
+    out_piece = lax.dynamic_slice_in_dim(w_out, batch_index * (part // 4), part // 4, 0)
+    bundle = jnp.concatenate([down_piece, up_piece.reshape(part, width), out_piece], axis=0)
+    deep = bundle.shape[0]
+
+    tokens_here = swap_halves(tokens[0])
+    heads = lax.dynamic_slice_in_dim(w_qkv.reshape(part, 3, 8, LANES), 4 * core, 4, 2)
+    heads = heads.transpose(2, 0, 1, 3).reshape(4, part, 3 * LANES)
+    small = jnp.concatenate(
+        [
+            jnp.stack([ln1_gain, ln1_bias, ln2_gain, ln2_bias, out_bias, down_bias]),
+            up_bias.reshape(4, part),
+            jnp.zeros((6, part), low),
+        ],
+        axis=0,
+    )
+    small = jnp.broadcast_to(jnp.pad(small, ((0, 0), (0, 2 * part)))[None], (4, 16, 3 * part))
+    heads = jnp.concatenate([heads, small], axis=1)
+    w_heads = lax.all_to_all(
+        jnp.concatenate([heads, heads], axis=0), "seq", 0, 0, tiled=True
+    )
+    tokens_here, w_heads, bundle = lax.optimization_barrier((tokens_here, w_heads, bundle))
+    bundle = lax.all_gather(bundle, ("seq", "batch"), axis=0, tiled=True)
+    bundle = bundle.reshape(8, 4, deep, width)
+    vectors = w_heads[:, part:, :part].astype(wide).transpose(1, 0, 2).reshape(16, width)
+    w_other = hop_batch(w_heads, 1)
+
+    meta = jnp.concatenate([key_mask[0], jnp.pad(lengths[0], (0, LANES - lengths.shape[1]))])
+    meta = meta.reshape(-1, LANES)
+    meta = jnp.where(core == (seq_index >> 2), meta, hop_batch(meta, 1)).reshape(-1)
+    ends = jnp.cumsum(meta[rows : rows + lengths.shape[1]])
+    starts = ends - meta[rows : rows + lengths.shape[1]]
+    positions = jnp.arange(rows, dtype=jnp.int32)
+    start = jnp.max(
+        jnp.where(starts[None, :] <= positions[:, None], starts[None, :], 0), axis=1
+    ).astype(jnp.int32)
+    bounds = attend_bounds(start, starts, rows)
+    bias = jnp.where(meta[:rows] == 1, 0.0, NEGATIVE).astype(wide)[None, :]
+
+    fourth = frames // 4
+    slab = pl.BlockSpec((fourth, width), lambda i, *_: (i, 0))
+    normed_one = call(
+        norm_kernel, "norm", 4, [slab, whole(16, width)], slab, like((frames, width), low)
+    )(ids, tokens_here, vectors)
+    y_one = hop_seq(normed_one, 1)
+    z_one = hop_seq(normed_one, 2)
+    half = frames // 2
+    top, bottom = hop_seq(y_one[:half], 2), hop_seq(z_one[half:], 1)
+    heads_shape = (4, frames, 3 * LANES)
+    top_slab = pl.BlockSpec((fourth, width), lambda i, *_: (jnp.minimum(i, 1), 0))
+    bottom_slab = pl.BlockSpec((fourth, width), lambda i, *_: (jnp.maximum(i, 2) - 2, 0))
+    heads_slab = pl.BlockSpec((4, fourth, 3 * LANES), lambda i, *_: (0, i, 0))
+    natural_slab = pl.BlockSpec((4, fourth, width), lambda i, *_: (0, i, 0))
+    heads_like = like(heads_shape, low)
+    qkv_own, leaving, natural = call(
+        project_kernel,
+        "project",
+        4,
+        [slab] * 3 + [top_slab, bottom_slab] + [whole(*w_heads.shape)] * 2,
+        [heads_slab, heads_slab, natural_slab],
+        (heads_like, heads_like, like((4, frames, width), low)),
+        flops=2 * 4 * frames * width * 6 * LANES,
+    )(ids, normed_one, y_one, z_one, top, bottom, w_heads, w_other)
+    qkv_came = hop_batch(leaving, 1).reshape(4 * frames, 3 * LANES)
+    qkv_own = qkv_own.reshape(4 * frames, 3 * LANES)
+    natural = natural.reshape(4 * frames, width)
+    cotangent_own = swap_halves(after(cotangent[0], leaving))
+
+    attended_heads, lse = attend(ids, bounds, qkv_own, qkv_came, bias)
+    cotangent_came = hop_batch(cotangent_own, 1)
+
+    mine = trade(attended_heads, IN_SQUARE)
+    mine_came = hop_batch(mine, 1)
+    blocks = pl.BlockSpec((8, fourth, LANES), lambda i, *_: (0, i, 0))
+    w_out_spec = pl.BlockSpec(
+        (8, 4, part // 4, width), lambda *_: (0, 0, (deep * 4) // part - 1, 0)
+    )
+    attended, middle, normed_two = call(
+        out_kernel,
+        "out_project",
+        4,
+        [blocks, blocks, slab, w_out_spec, whole(16, width)],
+        [slab] * 3,
+        (like((frames, width), low), like((frames, width), wide), like((frames, width), low)),
+        flops=2 * frames * width * width,
+    )(ids, mine, mine_came, tokens_here, bundle, vectors)
+    normed_two_came = hop_batch(normed_two, 1)
+
+    up_specs = [
+        pl.BlockSpec((8, 1, part, LANES), lambda s, ids, k=k: (0, 2 * k + ids[CORE], 1, s))
+        for k in range(2)
+    ]
+    down_specs = [
+        pl.BlockSpec((1, 1, part, width), lambda s, ids, k=k: (s, 2 * k + ids[CORE], 0, 0))
+        for k in range(2)
+    ]
+    hidden = pl.BlockSpec((2, frames, 2 * LANES), lambda s, *_: (0, 0, s))
+    act, grad_up, up_sums, result_own, result_leaving, back_own, back_leaving = call(
+        forward_kernel,
+        "feed_forward",
+        8,
+        [whole(frames, width)] * 4
+        + up_specs
+        + down_specs
+        + [pl.BlockSpec((16, LANES), lambda s, *_: (0, s))],
+        [hidden, hidden, pl.BlockSpec((8, LANES), lambda s, *_: (0, s))]
+        + [whole(frames, width)] * 4,
+        (
+            like((2, frames, 2 * width), low),
+            like((2, frames, 2 * width), low),
+            like((8, width), wide),
+            like((frames, width), wide),
+            like((frames, width), low),
+            like((frames, width), wide),
+            like((frames, width), low),
+        ),
+        scratch=[pltpu.VMEM((2, frames, width), wide)] * 2,
+        flops=2 * 4 * 2 * frames * width * 2 * width,
+    )(
+        ids,
+        normed_two,
+        normed_two_came,
+        cotangent_own,
+        cotangent_came,
+        bundle,
+        bundle,
+        bundle,
+        bundle,
+        vectors,
+    )
+    back_came = hop_batch(back_leaving, 1)
+
+    hidden_pair = pl.BlockSpec((2, frames, 4 * LANES), lambda s, *_: (0, 0, s))
+    down = call(
+        grad_down_kernel,
+        "grad_down",
+        4,
+        [hidden_pair, whole(frames, width), whole(frames, width)],
+        pl.BlockSpec((4 * LANES, width), lambda s, *_: (s, 0)),
+        like((2 * width, width), low),
+        flops=2 * 2 * frames * width * 2 * width,
+    )(ids, act, cotangent_own, cotangent_came)
+    back_own = after(back_own, down)
+    down = lax.psum_scatter(down, "seq", scatter_dimension=0, tiled=True)
+    grad_middle, grad_branch, spread, middle_sums = call(
+        middle_kernel,
+        "middle_back",
+        4,
+        [slab] * 4 + [w_out_spec, whole(16, width)],
+        [slab, slab, blocks, whole(8, width)],
+        (
+            like((frames, width), wide),
+            like((frames, width), low),
+            like((8, frames, LANES), low),
+            like((8, width), wide),
+        ),
+        flops=2 * frames * width * width,
+    )(ids, back_own, back_came, middle, cotangent_own, bundle, vectors)
+    grad_mine = trade(spread, IN_SQUARE)
+    grad_mine_came = hop_batch(grad_mine, 1)
+
+    split = like((8, part, width // 2), low)
+    split_spec = pl.BlockSpec((4,) + split.shape[1:], lambda s, *_: (s, 0, 0))
+    column = pl.BlockSpec((frames, 4 * part), lambda s, *_: (0, s))
+    out_kept, out_leaving = call(
+        grad_out_kernel,
+        "grad_out",
+        2,
+        [column, whole(frames, width)],
+        [split_spec, split_spec],
+        (split, split),
+        flops=2 * frames * width * width,
+    )(ids, attended, grad_branch)
+    out_came = hop_batch(out_leaving, 1)
+    broad = like((8, part, width + width // 4), low)
+    broad_spec = pl.BlockSpec((4,) + broad.shape[1:], lambda s, *_: (s, 0, 0))
+    up_kept, up_leaving = call(
+        grad_up_kernel,
+        "grad_up",
+        2,
+        [column, column, whole(2, frames, 2 * width), split_spec, split_spec],
+        [broad_spec, broad_spec],
+        (broad, broad),
+        flops=2 * 2 * frames * width * 2 * width,
+    )(ids, normed_two, normed_two_came, grad_up, out_kept, out_came)
+    up_came = hop_batch(up_leaving, 2)
+
+    result = (
+        middle
+        + result_own
+        + hop_batch(result_leaving, 1).astype(wide)
+        + vectors[5:6]
+    ).astype(low)
+    result_home = swap_halves(result)
+
+    ups = jnp.zeros((4, width), wide)
+    ups = lax.dynamic_update_slice(ups, up_sums[:2], (2 * core, 0))
+    sums = jnp.concatenate([middle_sums[:4], ups])
+    sums = sums.reshape(8, 8, 1, part).transpose(1, 2, 0, 3)
+    early = jnp.broadcast_to(sums, (8, 4, 8, part)).reshape(32, 8, part)
+
+    early = lax.all_to_all(early, ("seq", "batch"), 0, 0, tiled=True)
+
+    grad_mine = after(grad_mine, result, up_leaving)
+    grad_qkv, grad_leaving = attend_back(
+        ids,
+        bounds,
+        qkv_own,
+        qkv_came,
+        grad_mine,
+        grad_mine_came,
+        attended_heads,
+        bias,
+        lse,
+    )
+    grad_leaving = after(grad_leaving, up_came, result_home, early)
+    sums = jnp.sum(early, axis=0)
+    mixed = (up_kept.astype(wide) + after(up_came, grad_leaving).astype(wide)).astype(low)
+    mixed = lax.psum_scatter(
+        mixed.reshape(width, width + width // 4), "seq", scatter_dimension=0, tiled=True
+    )
+    grad_qkv_came = hop_batch(grad_leaving, 1)
+
+    pair = (2, frames, width // 2)
+    half_spec = pl.BlockSpec((fourth, width // 2), lambda i, *_: (i, 0))
+    pair_spec = pl.BlockSpec((2, fourth, width // 2), lambda i, *_: (0, i, 0))
+    first, y_out, z_out, keep_left, keep_right = call(
+        back_project_kernel,
+        "back_project",
+        4,
+        [heads_slab] * 2 + [whole(*w_heads.shape)] * 2,
+        [slab, pair_spec, pair_spec, half_spec, half_spec],
+        (
+            like((frames, width), wide),
+            like(pair, low),
+            like(pair, low),
+            like(pair[1:], wide),
+            like(pair[1:], wide),
+        ),
+        flops=2 * 4 * frames * width * 6 * LANES,
+    )(
+        ids,
+        grad_qkv.reshape(heads_shape),
+        grad_qkv_came.reshape(heads_shape),
+        w_heads,
+        w_other,
+    )
+    y_came, z_came = hop_seq(y_out, 1), hop_seq(z_out, 2)
+
+    z_second, y_second = call(
+        second_kernel,
+        "second",
+        4,
+        [half_spec, half_spec, pair_spec, pair_spec],
+        [half_spec, half_spec],
+        (like(pair[1:], low), like(pair[1:], low)),
+    )(ids, keep_left, keep_right, y_came, z_came)
+    z_second, y_second = hop_seq(z_second, 2), hop_seq(y_second, 1)
+    heads_out = like((width, 3 * LANES), low)
+    heads_kept, heads_leaving = call(
+        grad_heads_kernel,
+        "grad_heads",
+        2,
+        [pl.BlockSpec((4 * frames, 4 * part), lambda i, *_: (0, i))]
+        + [whole(4 * frames, 3 * LANES)] * 2,
+        [pl.BlockSpec((4 * part, 3 * LANES), lambda i, *_: (i, 0))] * 2,
+        (heads_out, heads_out),
+        flops=2 * 4 * frames * width * 6 * LANES,
+    )(ids, after(natural, z_out), grad_qkv, grad_qkv_came)
+    heads_came = hop_batch(heads_leaving, 1)
+
+    grad_inputs, last_sums = call(
+        last_kernel,
+        "last",
+        4,
+        [slab, pair_spec, pair_spec, half_spec, half_spec, slab, slab, whole(16, width)],
+        [slab, whole(8, width)],
+        (like((frames, width), low), like((8, width), wide)),
+    )(ids, first, y_came, z_came, z_second, y_second, tokens_here, grad_middle, vectors)
+    grad_inputs = swap_halves(grad_inputs)
+
+    heads_sum = (heads_kept.astype(wide) + heads_came.astype(wide)).astype(low)
+    heads_sum = lax.all_to_all(
+        heads_sum.reshape(8, part, 3 * LANES), "seq", 0, 0, tiled=True
+    ).astype(wide)
+    heads_sum = (heads_sum[:4] + heads_sum[4:]).astype(low)
+    heads_sum = (heads_sum.astype(wide) + hop_batch(heads_sum, 2).astype(wide)).astype(low)
+    grad_qkv_w = by_side(core, heads_sum, hop_batch(heads_sum, 1), 0).astype(wide)
+    grad_qkv_w = (
+        grad_qkv_w.reshape(8, part, 3, LANES).transpose(1, 2, 0, 3).reshape(part, 3 * width)
+    )
+
+    down = (down.astype(wide) + hop_batch(down, 2).astype(wide)).astype(low)
+    grad_down_w = by_side(core, down, hop_batch(down, 1), 0).astype(wide)
+    mixed = jnp.stack([mixed, hop_batch(mixed, 2)])
+    mixed = by_side(chip_x, mixed[:1], mixed[1:], 0)
+    mixed = by_side(core, mixed[None], hop_batch(mixed, 1)[None], 0).astype(wide)
+    grad_up_w = mixed[..., :width].reshape(2, 2, part, 4, 2 * LANES)
+    grad_up_w = grad_up_w.transpose(2, 1, 3, 0, 4).reshape(part, 4 * width)
+    grad_out_w = mixed[..., width:].transpose(2, 0, 1, 3).reshape(part, width)
+
+    late = last_sums[:2]
+    late = late + hop_batch(late, 2)
+    late = late + hop_batch(late, 1)
+    for bits in (1, 2, 4):
+        late = late + hop_seq(late, bits)
+    late = lax.dynamic_slice_in_dim(late, seq_index * part, part, 1)
+    return (
+        result_home[None],
+        grad_inputs[None],
+        grad_qkv_w,
+        grad_out_w,
+        grad_up_w,
+        grad_down_w,
+        late[0],
+        late[1],
+        sums[0],
+        sums[1],
+        sums[2],
+        sums[4:8].reshape(4 * LANES),
+        sums[3],
+    )
+
+
 def solution(mesh):
+    square = mesh.shape["seq"] == 8 and mesh.shape["batch"] == 4
     return jax.shard_map(
-        shards,
+        square_shards if square else shards,
         mesh=mesh,
         in_specs=(
             P("batch", "seq", None),

time: 1640 us -> 592 us (0.36)
  waiting for transfers between devices: 869 us -> 218 us
  blocking collectives: 315 us -> 0 us
  Pallas kernels: 0 us -> 223 us
  matrix products: 162 us -> 0 us
  other arithmetic: 70.4 us -> 21.9 us
  loops' own time: 48.2 us -> 0 us
  local copies, waits for them, and re-layouts: 68.3 us -> 37.4 us
    reduce_scatter x4 -> x2, waiting for transfers between devices: 373 us -> 0.04 us  [the longest x1 0.02 us: square_shards(): lax.psum_scatter(mixed.reshape(width, width + width // 4), 'seq', scatter...]
    all_gather x7 -> x0, blocking collectives: 274 us -> none  [the longest x1 98.5 us: shards(): lax.all_gather(ln2_gain, 'seq', axis=0, tiled=True)]
    ppermute x8 -> x36, waiting for transfers between devices: 414 us -> 189 us  [the longest x11 124 us: hop_seq(): return lax.ppermute(block, 'seq', [(i, i ^ bits) for i in range(size)])]
    pallas_call x0 -> x14, Pallas kernels: none -> 223 us  [the longest x12 117 us: run(): pl.pallas_call(kernel, out_shape=out_shape, grid_spec=pltpu.PrefetchScala...]
    dot_general x21 -> x0, matrix products: 162 us -> none  [the longest x4 34.4 us: times_trans(): lax.dot_general(left, right, (((1,), (1,)), ((), ())), preferred_element_...]
    all_gather x4 -> x1, waiting for transfers between devices: 67.2 us -> 0.02 us  [square_shards(): bundle = lax.all_gather(bundle, ('seq', 'batch'), axis=0, tiled=True)]
    another operation x20 -> x0, loops' own time: 48.2 us -> none  [the longest x5 22.4 us: attend_values(): total = lax.cond(live_list[offset], attend_update, keep_same, total)]
    ppermute x8 -> x36, starting transfers between devices: 82.7 us -> 45.1 us  [the longest x21 22.4 us: hop_batch(): return lax.ppermute(block, 'batch', [(i, i ^ bit) for i in range(size)])]
  transfers between devices with their start and end apart: 17 -> 44, of which waited for: 11 -> 20; matrix products, arithmetic and copies ran while one was open for 15% -> 5% of each run, Pallas kernels for 0% -> 32%
where the time goes in v1:
time: 592 us; the launch traced here: 583 us
  Pallas kernels  223 us (38%)
  waiting for transfers between devices  218 us (37%)
  starting transfers between devices  68.2 us (12%)
  local copies, waits for them, and re-layouts  37.4 us (6%)
  other arithmetic  21.9 us (4%)
  between operations  14.9 us (3%)
    ppermute x11, waiting for transfers between devices, hop_seq(): return lax.ppermute(block, 'seq', [(i, i ^ bits) for i in range(size)])  124 us
    pallas_call x12, Pallas kernels, run(): pl.pallas_call(kernel, out_shape=out_shape, grid_spec=pltpu.PrefetchScala...  117 us
    pallas_call x1, Pallas kernels, attend_back(): pl.pallas_call(attend_back_kernel, out_shape=(like(own.shape, jnp.bfloat1...  54.3 us
    pallas_call x1, Pallas kernels, attend(): pl.pallas_call(attend_kernel, out_shape=(like((8, TILE, LANES), jnp.bfloa...  52.1 us
    ppermute x4, waiting for transfers between devices, swap_halves(): return lax.ppermute(block, ('batch', 'seq'), route)  49.9 us
    all_to_all x2, waiting for transfers between devices, trade(): lax.all_to_all(block, 'seq', 0, 0, tiled=True, axis_index_groups=groups)  28.7 us
    ppermute x21, starting transfers between devices, hop_batch(): return lax.ppermute(block, 'batch', [(i, i ^ bit) for i in range(size)])  22.4 us
    ppermute x4, starting transfers between devices, swap_halves(): return lax.ppermute(block, ('batch', 'seq'), route)  16.5 us
  transfers between devices with their start and end apart: 44, of which 20 were waited for; matrix products, arithmetic and copies ran while one was open for 5% of the time, Pallas kernels for 32%

profile of v1, /device:TPU:1, one launch (start us, length us, event | category | flops | bytes accessed | tf_op | source)
XLA Modules:
  0.0 583.3 jit_solution(11915321631760310469)
XLA Ops:
  7.2 1.7 concatenate.71
  8.9 1.5 copy.53
  11.7 6.4 %all-to-all-start = ((bf16[8,144,384]{2,1,0:T(8,128)(2,1)}), bf16[8,144,384]{2,1,0:T(8,128)(2,1)}, u32[]{:S(2)}, u32[]{:S(2)}) async-start(bf16[8,144,384]{2,1,0:T(8,128)(2,1)} %maximum_maximum_fusion), calls=%async_computation | async-start | bytes 1769472 | tf_op jit(solution)/shard_map/all_to_all | solution.py:1028
  18.1 5.3 collective-permute-start.1
  23.5 1.8 reshape.244
  25.3 1.5 dynamic-slice_reduce_fusion
  28.6 34.6 %collective-permute-done.1.tokens = bf16[512,1024]{1,0:T(8,128)(2,1)S(1)} collective-permute-done((bf16[512,1024]{1,0:T(8,128)(2,1)}, bf16[512,1024]{1,0:T(8,128)(2,1)S(1)}, u32[]{:S(2)}, u32[]{:S(2)}) %collective-permute-start.1) | collective-permute-done | bytes 1048608 | tf_op jit(solution)/shard_map/ppermute | solution.py:956
  65.4 4.5 norm.1.own
  71.5 32.3 %collective-permute-done.3.z_one = bf16[512,1024]{1,0:T(8,128)(2,1)S(1)} collective-permute-done((bf16[512,1024]{1,0:T(8,128)(2,1)}, bf16[512,1024]{1,0:T(8,128)(2,1)S(1)}, u32[]{:S(2)}, u32[]{:S(2)}) %collective-permute-start.3) | collective-permute-done | bytes 1048608 | tf_op jit(solution)/shard_map/ppermute | solution.py:946
  105.4 15.5 %collective-permute-done.5.bottom = bf16[256,1024]{1,0:T(8,128)(2,1)} collective-permute-done((bf16[256,1024]{1,0:T(8,128)(2,1)S(1)}, bf16[256,1024]{1,0:T(8,128)(2,1)}, u32[]{:S(2)}, u32[]{:S(2)}) %collective-permute-start.5) | collective-permute-done | bytes 524320 | tf_op jit(solution)/shard_map/ppermute | solution.py:946
  120.9 16.2 %collective-permute-done.4.top = bf16[256,1024]{1,0:T(8,128)(2,1)} collective-permute-done((bf16[256,1024]{1,0:T(8,128)(2,1)S(1)}, bf16[256,1024]{1,0:T(8,128)(2,1)}, u32[]{:S(2)}, u32[]{:S(2)}) %collective-permute-start.4) | collective-permute-done | bytes 524320 | tf_op jit(solution)/shard_map/ppermute | solution.py:946
  137.1 9.7 %project.1 = (bf16[4,512,384]{2,1,0:T(8,128)(2,1)}, bf16[4,512,384]{2,1,0:T(8,128)(2,1)}, bf16[4,512,1024]{2,1,0:T(8,128)(2,1)}) custom-call(s32[4]{0:T(128)} %pad_add_fusion.1.ids, bf16[512,1024]{1,0:T(8,128)(2,1)} %norm.1.own, bf16[512,1024]{1,0:T(8,128)(2,1)} %copy-done.18, bf16[512,1024]{1,0:T(8,128)(2,1)} %copy-done.17, ...), custom_call_target="tpu_custom_call" | custom-call | flops 3221225472 | bytes 11927552 | tf_op jit(solution)/shard_map/project/pallas_call | solution.py:429
  148.8 3.5 collective-permute-done.7
  153.4 52.1 %attend.1 = (bf16[8,512,128]{2,1,0:T(8,128)(2,1)}, f32[2,4096]{1,0:T(2,128)}) custom-call(s32[4]{0:T(128)} %pad_add_fusion.1.ids, s32[5,8]{1,0:T(8,128)} %stack.64.bounds, bf16[2048,384]{1,0:T(8,128)(2,1)} %bitcast.149, bf16[2048,384]{1,0:T(8,128)(2,1)} %bitcast.144, f32[1,4096]{1,0:T(1,128)} %bitcast.129), custom_call_target="tpu_custom_call" | custom-call | flops 4294967296 | bytes 9830400 | tf_op jit(solution)/shard_map/attend/pallas_call | solution.py:558
  205.5 3.6 all-to-all-start.1
  209.2 2.1 collective-permute-start.10
  211.3 12.5 %all-to-all-done.1.own = bf16[8,512,128]{2,1,0:T(8,128)(2,1)S(1)} async-done(((bf16[8,512,128]{2,1,0:T(8,128)(2,1)}), bf16[8,512,128]{2,1,0:T(8,128)(2,1)S(1)}, u32[]{:S(2)}, u32[]{:S(2)}) %all-to-all-start.1) | async-done | bytes 1048608 | tf_op jit(solution)/shard_map/all_to_all | solution.py:964
  224.9 12.6 %collective-permute-done.10.grad_own.cotangent = bf16[512,1024]{1,0:T(8,128)(2,1)S(1)} collective-permute-done((bf16[512,1024]{1,0:T(8,128)(2,1)S(1)}, bf16[512,1024]{1,0:T(8,128)(2,1)S(1)}, u32[]{:S(2)}, u32[]{:S(2)}) %collective-permute-start.10) | collective-permute-done | bytes 1048608 | tf_op jit(solution)/shard_map/ppermute | solution.py:956
  237.6 6.7 %out_project.1 = (bf16[512,1024]{1,0:T(8,128)(2,1)}, f32[512,1024]{1,0:T(8,128)}, bf16[512,1024]{1,0:T(8,128)(2,1)}) custom-call(s32[4]{0:T(128)} %pad_add_fusion.1.ids, bf16[8,512,128]{2,1,0:T(8,128)(2,1)} %copy-done.7, bf16[8,512,128]{2,1,0:T(8,128)(2,1)} %collective-permute-done.8.came, bf16[512,1024]{1,0:T(8,128)(2,1)} %copy-done.2, ...), custom_call_target="tpu_custom_call" | custom-call | flops 1073741824 | bytes 44171264 | tf_op jit(solution)/shard_map/out_project/pallas_call | solution.py:429
  244.7 2.5 collective-permute-done.9.normed_came
  248.2 30.1 %feed_forward.1 = (bf16[2,512,2048]{2,1,0:T(8,128)(2,1)}, bf16[2,512,2048]{2,1,0:T(8,128)(2,1)}, f32[8,1024]{1,0:T(8,128)}, f32[512,1024]{1,0:T(8,128)}, bf16[51...) custom-call(s32[4]{0:T(128)} %pad_add_fusion.1.ids, ...), custom_call_target="tpu_custom_call" | custom-call | flops 17179869184 | bytes 159514624 | tf_op jit(solution)/shard_map/feed_forward/pallas_call | solution.py:429
  278.3 9.1 %grad_down.1 = bf16[2048,1024]{1,0:T(8,128)(2,1)} custom-call(s32[4]{0:T(128)} %pad_add_fusion.1.ids, bf16[2,512,2048]{2,1,0:T(8,128)(2,1)} %get-tuple-element.70.act, bf16[512,1024]{1,0:T(8,128)(2,1)} %copy-done.4, bf16[512,1024]{1,0:T(8,128)(2,1)} %copy-done.10), custom_call_target="tpu_custom_call" | custom-call | flops 4294967296 | bytes 12582912 | tf_op jit(solution)/shard_map/grad_down/pallas_call | solution.py:429
  287.4 1.2 copy-done.25
  289.0 2.3 collective-permute-done.14.back_came
  292.3 9.6 %middle_back.1 = (f32[512,1024]{1,0:T(8,128)}, bf16[512,1024]{1,0:T(8,128)(2,1)}, bf16[8,512,128]{2,1,0:T(8,128)(2,1)}, f32[8,1024]{1,0:T(8,128)}) custom-call(s32[4]{0:T(128)} %pad_add_fusion.1.ids, f32[512,1024]{1,0:T(8,128)} %get-tuple-element.71.back_own, bf16[512,1024]{1,0:T(8,128)(2,1)} %copy-done.11, f32[512,1024]{1,0:T(8,128)} %get-tuple-element.64.middle, ...), custom_call_target="tpu_custom_call" | custom-call | flops 1073741824 | bytes 50462720 | tf_op jit(solution)/shard_map/middle_back/pallas_call | solution.py:429
  301.9 4.6 grad_out.1
  306.8 4.3 all-to-all-start.2
  312.0 10.9 %grad_up.1 = (bf16[8,128,1280]{2,1,0:T(8,128)(2,1)}, bf16[8,128,1280]{2,1,0:T(8,128)(2,1)}) custom-call(s32[4]{0:T(128)} %pad_add_fusion.1.ids, bf16[512,1024]{1,0:T(8,128)(2,1)} %get-tuple-element.65.normed_own, bf16[512,1024]{1,0:T(8,128)(2,1)} %copy-done.9, bf16[2,512,2048]{2,1,0:T(8,128)(2,1)} %get-tuple-element.74.grad_up, ...), custom_call_target="tpu_custom_call" | custom-call | flops 4294967296 | bytes 16777216 | tf_op jit(solution)/shard_map/grad_up/pallas_call | solution.py:429
  323.3 16.2 %all-to-all-done.2.grad_own = bf16[8,512,128]{2,1,0:T(8,128)(2,1)} async-done(((bf16[8,512,128]{2,1,0:T(8,128)(2,1)}), bf16[8,512,128]{2,1,0:T(8,128)(2,1)}, u32[]{:S(2)}, u32[]{:S(2)}) %all-to-all-start.2) | async-done | bytes 1048608 | tf_op jit(solution)/shard_map/all_to_all | solution.py:964
  340.8 3.2 add_convert_fusion.1
  344.0 2.1 collective-permute-start.13
  346.8 4.7 all-to-all-start.3
  351.8 54.3 %attend_back.1 = (bf16[2048,384]{1,0:T(8,128)(2,1)}, bf16[2048,384]{1,0:T(8,128)(2,1)}) custom-call(s32[4]{0:T(128)} %pad_add_fusion.1.ids, s32[5,8]{1,0:T(8,128)} %stack.64.bounds, bf16[2048,384]{1,0:T(8,128)(2,1)} %bitcast.150, bf16[2048,384]{1,0:T(8,128)(2,1)} %bitcast.145, bf16[8,512,128]{2,1,0:T(8,128)(2,1)} %all-to-all-done.2.grad_own, ...), custom_call_target="tpu_custom_call" | custom-call | flops 10737418240 | bytes 9830400 | tf_op jit(solution)/shard_map/attend_back/pallas_call | solution.py:697
  406.5 4.6 add_convert_fusion
  412.3 11.8 %back_project.1 = (f32[512,1024]{1,0:T(8,128)}, bf16[2,512,512]{2,1,0:T(8,128)(2,1)}, bf16[2,512,512]{2,1,0:T(8,128)(2,1)}, f32[512,512]{1,0:T(8,128)}, f32[512,512]{1,0:T(8,128)}) custom-call(s32[4]{0:T(128)} %pad_add_fusion.1.ids, bf16[4,512,384]{2,1,0:T(8,128)(2,1)} %bitcast.151, bf16[4,512,384]{2,1,0:T(8,128)(2,1)} %bitcast.146, ...), custom_call_target="tpu_custom_call" | custom-call | flops 3221225472 | bytes 9830400 | tf_op jit(solution)/shard_map/back_project/pallas_call | solution.py:429
  424.1 8.7 %grad_heads.1 = (bf16[1024,384]{1,0:T(8,128)(2,1)}, bf16[1024,384]{1,0:T(8,128)(2,1)}) custom-call(s32[4]{0:T(128)} %pad_add_fusion.1.ids, bf16[2048,1024]{1,0:T(8,128)(2,1)} %bitcast.148, bf16[2048,384]{1,0:T(8,128)(2,1)} %get-tuple-element.82.own, bf16[2048,384]{1,0:T(8,128)(2,1)} %copy-done.23), custom_call_target="tpu_custom_call" | custom-call | flops 3221225472 | bytes 14680064 | tf_op jit(solution)/shard_map/grad_heads/pallas_call | solution.py:429
  433.1 1.5 collective-permute-start.19
  435.7 1.3 add_convert_fusion.2
  438.2 3.8 all-to-all-start.4
  442.0 22.4 %collective-permute-done.19.y_came = bf16[2,512,512]{2,1,0:T(8,128)(2,1)S(1)} collective-permute-done((bf16[2,512,512]{2,1,0:T(8,128)(2,1)}, bf16[2,512,512]{2,1,0:T(8,128)(2,1)S(1)}, u32[]{:S(2)}, u32[]{:S(2)}) %collective-permute-start.19) | collective-permute-done | bytes 1048608 | tf_op jit(solution)/shard_map/ppermute | solution.py:946
  464.5 11.7 %collective-permute-done.20.z_came = bf16[2,512,512]{2,1,0:T(8,128)(2,1)S(1)} collective-permute-done((bf16[2,512,512]{2,1,0:T(8,128)(2,1)}, bf16[2,512,512]{2,1,0:T(8,128)(2,1)S(1)}, u32[]{:S(2)}, u32[]{:S(2)}) %collective-permute-start.20) | collective-permute-done | bytes 1048608 | tf_op jit(solution)/shard_map/ppermute | solution.py:946
  477.1 4.6 second.1
  482.5 22.7 %collective-permute-done.21.z_second = bf16[512,512]{1,0:T(8,128)(2,1)S(1)} collective-permute-done((bf16[512,512]{1,0:T(8,128)(2,1)}, bf16[512,512]{1,0:T(8,128)(2,1)S(1)}, u32[]{:S(2)}, u32[]{:S(2)}) %collective-permute-start.21) | collective-permute-done | bytes 524320 | tf_op jit(solution)/shard_map/ppermute | solution.py:946
  506.1 6.3 %last.1 = (bf16[512,1024]{1,0:T(8,128)(2,1)}, f32[8,1024]{1,0:T(8,128)}) custom-call(s32[4]{0:T(128)} %pad_add_fusion.1.ids, f32[512,1024]{1,0:T(8,128)} %get-tuple-element.87.first, bf16[2,512,512]{2,1,0:T(8,128)(2,1)} %copy-done.5, bf16[2,512,512]{2,1,0:T(8,128)(2,1)} %copy-done.6, bf16[512,512]{1,0:T(8,128)(2,1)} %copy-done.15, ...), custom_call_target="tpu_custom_call" | custom-call | bytes 16908288 | tf_op jit(solution)/shard_map/last/pallas_call | solution.py:429
  513.2 2.5 collective-permute-done.31
  516.4 2.8 collective-permute-start.32
  520.8 1.8 collective-permute-done.33
  523.5 1.6 collective-permute-done.34
  525.8 7.0 %collective-permute-start.23 = (bf16[512,1024]{1,0:T(8,128)(2,1)}, bf16[512,1024]{1,0:T(8,128)(2,1)}, u32[]{:S(2)}, u32[]{:S(2)}) collective-permute-start(bf16[512,1024]{1,0:T(8,128)(2,1)} %get-tuple-element.95), channel_id=1, source_target_pairs={{0,0},{1,1},{2,2},{3,3},{4,8},{5,9},{6,10},{7,11},{8,4},{9,5},{10,... | collective-permute-start | bytes 3145736 | tf_op jit(solution)/shard_map/ppermute | solution.py:956
  532.8 1.8 collective-permute-start.27
  534.7 5.5 collective-permute-start.26
  540.2 2.9 collective-permute-done.29
  543.1 1.2 add_convert_fusion.3
  544.3 5.0 collective-permute-start.30
  550.9 2.7 collective-permute-start.28
  554.1 2.6 collective-permute-done.23
  557.0 1.6 copy.62
  558.7 2.9 fusion.1
  561.6 1.6 fusion
  563.6 2.0 reshape.260
  565.6 3.2 copy.69
  568.8 2.7 reshape.261
  571.9 1.2 reshape.259
  574.1 2.3 copy.76
  (173 shorter events, 34.9 us)
Async XLA Ops:
  7.2 20.5 %copy-start = (bf16[512,1024]{1,0:T(8,128)(2,1)S(1)}, bf16[512,1024]{1,0:T(8,128)(2,1)}, u32[]{:S(2)}) copy-start(bf16[512,1024]{1,0:T(8,128)(2,1)} %param.22) | copy-start | bytes 3145732
  11.7 51.6 %all-to-all-start = ((bf16[8,144,384]{2,1,0:T(8,128)(2,1)}), bf16[8,144,384]{2,1,0:T(8,128)(2,1)}, u32[]{:S(2)}, u32[]{:S(2)}) async-start(bf16[8,144,384]{2,1,0:T(8,128)(2,1)} %maximum_maximum_fusion), calls=%async_computation | async-start | bytes 1769472 | tf_op jit(solution)/shard_map/all_to_all | solution.py:1028
  18.1 219.5 %all-gather.2.cloned.1.call-start = ((), (), s32[]{:S(2)}) async-start(), calls=%async_computation.7 | async-start | bytes 19464192 | tf_op jit(solution)/shard_map/all_gather | solution.py:1032
  18.1 45.1 %collective-permute-start.1 = (bf16[512,1024]{1,0:T(8,128)(2,1)}, bf16[512,1024]{1,0:T(8,128)(2,1)S(1)}, u32[]{:S(2)}, u32[]{:S(2)}) collective-permute-start(bf16[512,1024]{1,0:T(8,128)(2,1)} %bitcast.15), channel_id=1, source_target_pairs={{0,0},{1,1},{2,2},{3,3},{4,8},{5,9},{6,10},{7,11},{8,4},{9,5},{10,... | collective-permute-start | bytes 3145736 | tf_op jit(solution)/shard_map/ppermute | solution.py:956
  27.7 43.2 %copy-start.19 = (s32[1,4096]{1,0:T(1,128)S(1)}, s32[1,4096]{1,0:T(1,128)}, u32[]{:S(2)}) copy-start(s32[1,4096]{1,0:T(1,128)} %param.17) | copy-start | bytes 49156
  27.8 43.2 %copy-start.21 = (s32[1,4]{1,0:T(1,128)S(1)}, s32[1,4]{1,0:T(1,128)}, u32[]{:S(2)}) copy-start(s32[1,4]{1,0:T(1,128)} %param.16) | copy-start | bytes 52
  63.2 2.1 copy-start.2
  69.9 34.0 %collective-permute-start.3 = (bf16[512,1024]{1,0:T(8,128)(2,1)}, bf16[512,1024]{1,0:T(8,128)(2,1)S(1)}, u32[]{:S(2)}, u32[]{:S(2)}) collective-permute-start(bf16[512,1024]{1,0:T(8,128)(2,1)} %norm.1.own), channel_id=1, source_target_pairs={{0,2},{1,3},{2,0},{3,1},{4,6},{5,7},{6,4},{7,5},{8,10},{9,11},{10,... | collective-permute-start | bytes 3145736 | tf_op jit(solution)/shard_map/ppermute | solution.py:946
  69.9 35.1 %collective-permute-start.2 = (bf16[512,1024]{1,0:T(8,128)(2,1)}, bf16[512,1024]{1,0:T(8,128)(2,1)S(1)}, u32[]{:S(2)}, u32[]{:S(2)}) collective-permute-start(bf16[512,1024]{1,0:T(8,128)(2,1)} %norm.1.own), channel_id=1, source_target_pairs={{0,1},{1,0},{2,3},{3,2},{4,5},{5,4},{6,7},{7,6},{8,9},{9,8},{10,11... | collective-permute-start | bytes 3145736 | tf_op jit(solution)/shard_map/ppermute | solution.py:946
  70.9 34.5 %collective-permute-start.6 = (bf16[8,144,384]{2,1,0:T(8,128)(2,1)}, bf16[8,144,384]{2,1,0:T(8,128)(2,1)}, u32[]{:S(2)}, u32[]{:S(2)}) collective-permute-start(bf16[8,144,384]{2,1,0:T(8,128)(2,1)} %all-to-all-done.w_own), channel_id=1, source_target_pairs={{0,8},{8,0},{16,24},{24,16},{1,9},{9,1},{17,25},{25,17},{2,10},{10... | collective-permute-start | bytes 2654216 | tf_op jit(solution)/shard_map/ppermute | solution.py:941
  71.0 34.2 %collective-permute-start = (s32[33,128]{1,0:T(8,128)S(1)}, s32[33,128]{1,0:T(8,128)S(1)}, u32[]{:S(2)}, u32[]{:S(2)}) collective-permute-start(s32[33,128]{1,0:T(8,128)S(1)} %fusion.3), channel_id=1, source_target_pairs={{0,8},{8,0},{16,24},{24,16},{1,9},{9,1},{17,25},{25,17},{2,10},{10... | collective-permute-start | bytes 50696 | tf_op jit(solution)/shard_map/ppermute | solution.py:941
  103.9 33.2 %copy-start.17 = (bf16[512,1024]{1,0:T(8,128)(2,1)}, bf16[512,1024]{1,0:T(8,128)(2,1)S(1)}, u32[]{:S(2)}) copy-start(bf16[512,1024]{1,0:T(8,128)(2,1)S(1)} %collective-permute-done.3.z_one) | copy-start | bytes 3145732
  103.9 17.0 %collective-permute-start.5 = (bf16[256,1024]{1,0:T(8,128)(2,1)S(1)}, bf16[256,1024]{1,0:T(8,128)(2,1)}, u32[]{:S(2)}, u32[]{:S(2)}) collective-permute-start(bf16[256,1024]{1,0:T(8,128)(2,1)S(1)} %slice.93), channel_id=1, source_target_pairs={{0,1},{1,0},{2,3},{3,2},{4,5},{5,4},{6,7},{7,6},{8,9},{9,8},{10,11... | collective-permute-start | bytes 1572872 | tf_op jit(solution)/shard_map/ppermute | solution.py:946
  105.0 32.1 %copy-start.18 = (bf16[512,1024]{1,0:T(8,128)(2,1)}, bf16[512,1024]{1,0:T(8,128)(2,1)S(1)}, u32[]{:S(2)}) copy-start(bf16[512,1024]{1,0:T(8,128)(2,1)S(1)} %collective-permute-done.2.y_one) | copy-start | bytes 3145732
  105.1 32.0 %collective-permute-start.4 = (bf16[256,1024]{1,0:T(8,128)(2,1)S(1)}, bf16[256,1024]{1,0:T(8,128)(2,1)}, u32[]{:S(2)}, u32[]{:S(2)}) collective-permute-start(bf16[256,1024]{1,0:T(8,128)(2,1)S(1)} %slice.92), channel_id=1, source_target_pairs={{0,2},{1,3},{2,0},{3,1},{4,6},{5,7},{6,4},{7,5},{8,10},{9,11},{10,... | collective-permute-start | bytes 1572872 | tf_op jit(solution)/shard_map/ppermute | solution.py:946
  146.8 5.4 collective-permute-start.7
  152.3 1.1 copy-start.22
  205.5 3.7 copy-start.24
  205.5 18.3 %all-to-all-start.1 = ((bf16[8,512,128]{2,1,0:T(8,128)(2,1)}), bf16[8,512,128]{2,1,0:T(8,128)(2,1)S(1)}, u32[]{:S(2)}, u32[]{:S(2)}) async-start(bf16[8,512,128]{2,1,0:T(8,128)(2,1)} %get-tuple-element.62.attended), calls=%async_computation.1 | async-start | bytes 2097152 | tf_op jit(solution)/shard_map/all_to_all | solution.py:964
  209.2 316.0 %reduce-scatter.5.cloned.1.call-start = ((), (), s32[]{:S(2)}) async-start(), calls=%async_computation.9 | async-start | bytes 4718592 | tf_op jit(solution)/shard_map/reduce_scatter | solution.py:1153
  209.2 28.3 %collective-permute-start.10 = (bf16[512,1024]{1,0:T(8,128)(2,1)S(1)}, bf16[512,1024]{1,0:T(8,128)(2,1)S(1)}, u32[]{:S(2)}, u32[]{:S(2)}) collective-permute-start(bf16[512,1024]{1,0:T(8,128)(2,1)S(1)} %bitcast.147), channel_id=1, source_target_pairs={{0,0},{1,1},{2,2},{3,3},{4,8},{5,9},{6,10},{7,11},{8,4},{9,5},{10,... | collective-permute-start | bytes 3145736 | tf_op jit(solution)/shard_map/ppermute | solution.py:956
  223.8 13.8 %copy-start.7 = (bf16[8,512,128]{2,1,0:T(8,128)(2,1)}, bf16[8,512,128]{2,1,0:T(8,128)(2,1)S(1)}, u32[]{:S(2)}) copy-start(bf16[8,512,128]{2,1,0:T(8,128)(2,1)S(1)} %all-to-all-done.1.own) | copy-start | bytes 3145732
  223.8 13.7 %collective-permute-start.8 = (bf16[8,512,128]{2,1,0:T(8,128)(2,1)S(1)}, bf16[8,512,128]{2,1,0:T(8,128)(2,1)}, u32[]{:S(2)}, u32[]{:S(2)}) collective-permute-start(bf16[8,512,128]{2,1,0:T(8,128)(2,1)S(1)} %all-to-all-done.1.own), channel_id=1, source_target_pairs={{0,8},{8,0},{16,24},{24,16},{1,9},{9,1},{17,25},{25,17},{2,10},{10... | collective-permute-start | bytes 3145736 | tf_op jit(solution)/shard_map/ppermute | solution.py:941
  237.5 6.7 %copy-start.4 = (bf16[512,1024]{1,0:T(8,128)(2,1)}, bf16[512,1024]{1,0:T(8,128)(2,1)S(1)}, u32[]{:S(2)}) copy-start(bf16[512,1024]{1,0:T(8,128)(2,1)S(1)} %collective-permute-done.10.grad_own.cotangent) | copy-start | bytes 3145732
  237.5 7.2 %collective-permute-start.11 = (bf16[512,1024]{1,0:T(8,128)(2,1)S(1)}, bf16[512,1024]{1,0:T(8,128)(2,1)S(1)}, u32[]{:S(2)}, u32[]{:S(2)}) collective-permute-start(bf16[512,1024]{1,0:T(8,128)(2,1)S(1)} %collective-permute-done.10.grad_own.cotangent), channel_id=1, source_target_pairs={{0,8},{8,0},{16,24},{24,16},{1,9},{9,1},{17,25},{25,17},{2,10},{10... | collective-permute-start | bytes 3145736 | tf_op jit(solution)/shard_map/ppermute | solution.py:941
  244.2 3.0 collective-permute-start.9
  244.7 2.5 copy-start.10
  287.4 1.2 copy-start.25
  288.6 2.7 collective-permute-start.14
  306.5 4.6 collective-permute-start.15
  306.8 32.7 %all-to-all-start.2 = ((bf16[8,512,128]{2,1,0:T(8,128)(2,1)}), bf16[8,512,128]{2,1,0:T(8,128)(2,1)}, u32[]{:S(2)}, u32[]{:S(2)}) async-start(bf16[8,512,128]{2,1,0:T(8,128)(2,1)} %get-tuple-element.73), calls=%async_computation.2 | async-start | bytes 2097152 | tf_op jit(solution)/shard_map/all_to_all | solution.py:964
  312.0 28.7 %copy-start.3 = (f32[512,1024]{1,0:T(8,128)S(1)}, f32[512,1024]{1,0:T(8,128)}, u32[]{:S(2)}) copy-start(f32[512,1024]{1,0:T(8,128)} %get-tuple-element.64.middle) | copy-start | bytes 6291460
  322.9 83.2 %collective-permute-start.17 = (bf16[8,128,1280]{2,1,0:T(8,128)(2,1)}, bf16[8,128,1280]{2,1,0:T(8,128)(2,1)}, u32[]{:S(2)}, u32[]{:S(2)}) collective-permute-start(bf16[8,128,1280]{2,1,0:T(8,128)(2,1)} %get-tuple-element.79), channel_id=1, source_target_pairs={{0,16},{8,24},{16,0},{24,8},{1,17},{9,25},{17,1},{25,9},{2,18},{10... | collective-permute-start | bytes 7864328 | tf_op jit(solution)/shard_map/ppermute | solution.py:941
  322.9 17.8 %collective-permute-start.12 = (bf16[512,1024]{1,0:T(8,128)(2,1)}, bf16[512,1024]{1,0:T(8,128)(2,1)S(1)}, u32[]{:S(2)}, u32[]{:S(2)}) collective-permute-start(bf16[512,1024]{1,0:T(8,128)(2,1)} %get-tuple-element.68), channel_id=1, source_target_pairs={{0,8},{8,0},{16,24},{24,16},{1,9},{9,1},{17,25},{25,17},{2,10},{10... | collective-permute-start | bytes 3145736 | tf_op jit(solution)/shard_map/ppermute | solution.py:941
  339.5 12.3 %collective-permute-start.16 = (bf16[8,512,128]{2,1,0:T(8,128)(2,1)}, bf16[8,512,128]{2,1,0:T(8,128)(2,1)}, u32[]{:S(2)}, u32[]{:S(2)}) collective-permute-start(bf16[8,512,128]{2,1,0:T(8,128)(2,1)} %all-to-all-done.2.grad_own), channel_id=1, source_target_pairs={{0,8},{8,0},{16,24},{24,16},{1,9},{9,1},{17,25},{25,17},{2,10},{10... | collective-permute-start | bytes 3145736 | tf_op jit(solution)/shard_map/ppermute | solution.py:941
  340.7 5.4 copy-start.20
  344.0 62.1 %collective-permute-start.13 = (bf16[512,1024]{1,0:T(8,128)(2,1)}, bf16[512,1024]{1,0:T(8,128)(2,1)S(1)}, u32[]{:S(2)}, u32[]{:S(2)}) collective-permute-start(bf16[512,1024]{1,0:T(8,128)(2,1)} %add_convert_fusion.1), channel_id=1, source_target_pairs={{0,0},{1,1},{2,2},{3,3},{4,8},{5,9},{6,10},{7,11},{8,4},{9,5},{10,... | collective-permute-start | bytes 3145736 | tf_op jit(solution)/shard_map/ppermute | solution.py:956
  346.8 59.3 %all-to-all-start.3 = ((f32[32,8,128]{2,1,0:T(8,128)}), f32[32,8,128]{2,1,0:T(8,128)S(1)}, u32[]{:S(2)}, u32[]{:S(2)}) async-start(f32[32,8,128]{2,1,0:T(8,128)} %bitcast.38), calls=%async_computation.3 | async-start | bytes 262144 | tf_op jit(solution)/shard_map/all_to_all | solution.py:1211
  351.5 181.3 %reduce-scatter.3.cloned.1.call-start = ((), (), s32[]{:S(2)}) async-start(), calls=%async_computation.8 | async-start | bytes 2949120 | tf_op jit(solution)/shard_map/reduce_scatter | solution.py:1228
  406.1 5.1 copy-start.12
  406.1 5.1 collective-permute-start.18
  432.9 2.9 collective-permute-start.24
  433.1 31.3 %collective-permute-start.19 = (bf16[2,512,512]{2,1,0:T(8,128)(2,1)}, bf16[2,512,512]{2,1,0:T(8,128)(2,1)S(1)}, u32[]{:S(2)}, u32[]{:S(2)}) collective-permute-start(bf16[2,512,512]{2,1,0:T(8,128)(2,1)} %get-tuple-element.88), channel_id=1, source_target_pairs={{0,1},{1,0},{2,3},{3,2},{4,5},{5,4},{6,7},{7,6},{8,9},{9,8},{10,11... | collective-permute-start | bytes 3145736 | tf_op jit(solution)/shard_map/ppermute | solution.py:946
  434.7 41.4 %collective-permute-start.20 = (bf16[2,512,512]{2,1,0:T(8,128)(2,1)}, bf16[2,512,512]{2,1,0:T(8,128)(2,1)S(1)}, u32[]{:S(2)}, u32[]{:S(2)}) collective-permute-start(bf16[2,512,512]{2,1,0:T(8,128)(2,1)} %get-tuple-element.89), channel_id=1, source_target_pairs={{0,2},{1,3},{2,0},{3,1},{4,6},{5,7},{6,4},{7,5},{8,10},{9,11},{10,... | collective-permute-start | bytes 3145736 | tf_op jit(solution)/shard_map/ppermute | solution.py:946
  438.2 84.4 %all-to-all-start.4 = ((bf16[8,128,384]{1,2,0:T(8,128)(2,1)}), bf16[8,128,384]{1,2,0:T(8,128)(2,1)S(1)}, u32[]{:S(2)}, u32[]{:S(2)}) async-start(bf16[8,128,384]{1,2,0:T(8,128)(2,1)} %copy.58), calls=%async_computation.4 | async-start | bytes 1572864 | tf_op jit(solution)/shard_map/all_to_all | solution.py:1292
  464.5 11.7 %copy-start.5 = (bf16[2,512,512]{2,1,0:T(8,128)(2,1)}, bf16[2,512,512]{2,1,0:T(8,128)(2,1)S(1)}, u32[]{:S(2)}) copy-start(bf16[2,512,512]{2,1,0:T(8,128)(2,1)S(1)} %collective-permute-done.19.y_came) | copy-start | bytes 3145732
  481.7 23.4 %collective-permute-start.21 = (bf16[512,512]{1,0:T(8,128)(2,1)}, bf16[512,512]{1,0:T(8,128)(2,1)S(1)}, u32[]{:S(2)}, u32[]{:S(2)}) collective-permute-start(bf16[512,512]{1,0:T(8,128)(2,1)} %get-tuple-element.92), channel_id=1, source_target_pairs={{0,2},{1,3},{2,0},{3,1},{4,6},{5,7},{6,4},{7,5},{8,10},{9,11},{10,... | collective-permute-start | bytes 1572872 | tf_op jit(solution)/shard_map/ppermute | solution.py:946
  481.7 23.4 %collective-permute-start.22 = (bf16[512,512]{1,0:T(8,128)(2,1)}, bf16[512,512]{1,0:T(8,128)(2,1)S(1)}, u32[]{:S(2)}, u32[]{:S(2)}) collective-permute-start(bf16[512,512]{1,0:T(8,128)(2,1)} %get-tuple-element.93), channel_id=1, source_target_pairs={{0,1},{1,0},{2,3},{3,2},{4,5},{5,4},{6,7},{7,6},{8,9},{9,8},{10,11... | collective-permute-start | bytes 1572872 | tf_op jit(solution)/shard_map/ppermute | solution.py:946
  513.2 2.5 collective-permute-start.31
  516.4 3.7 collective-permute-start.32
  520.1 2.5 collective-permute-start.33
  522.6 2.5 collective-permute-start.34
  522.8 11.8 %collective-permute-start.25 = (bf16[4,128,384]{1,2,0:T(8,128)(2,1)S(1)}, bf16[4,128,384]{1,2,0:T(8,128)(2,1)S(1)}, u32[]{:S(2)}, u32[]{:S(2)}) collective-permute-start(bf16[4,128,384]{1,2,0:T(8,128)(2,1)S(1)} %fusion.2), channel_id=1, source_target_pairs={{0,16},{8,24},{16,0},{24,8},{1,17},{9,25},{17,1},{25,9},{2,18},{10... | collective-permute-start | bytes 1179656 | tf_op jit(solution)/shard_map/ppermute | solution.py:941
  525.1 7.6 %collective-permute-start.35 = (f32[2,1024]{1,0:T(2,128)S(1)}, f32[2,1024]{1,0:T(2,128)S(1)}, u32[]{:S(2)}, u32[]{:S(2)}) collective-permute-start(f32[2,1024]{1,0:T(2,128)S(1)} %add.125), channel_id=1, source_target_pairs={{0,4},{1,5},{2,6},{3,7},{4,0},{5,1},{6,2},{7,3},{8,12},{9,13},{10,... | collective-permute-start | bytes 24584 | tf_op jit(solution)/shard_map/ppermute | solution.py:946
  525.2 17.9 %collective-permute-start.29 = (bf16[256,1024]{1,0:T(8,128)(2,1)}, bf16[256,1024]{1,0:T(8,128)(2,1)}, u32[]{:S(2)}, u32[]{:S(2)}) collective-permute-start(bf16[256,1024]{1,0:T(8,128)(2,1)} %reduce-scatter.5.cloned.1.call-done), channel_id=1, source_target_pairs={{0,16},{8,24},{16,0},{24,8},{1,17},{9,25},{17,1},{25,9},{2,18},{10... | collective-permute-start | bytes 1572872 | tf_op jit(solution)/shard_map/ppermute | solution.py:941
  525.8 31.0 %collective-permute-start.23 = (bf16[512,1024]{1,0:T(8,128)(2,1)}, bf16[512,1024]{1,0:T(8,128)(2,1)}, u32[]{:S(2)}, u32[]{:S(2)}) collective-permute-start(bf16[512,1024]{1,0:T(8,128)(2,1)} %get-tuple-element.95), channel_id=1, source_target_pairs={{0,0},{1,1},{2,2},{3,3},{4,8},{5,9},{6,10},{7,11},{8,4},{9,5},{10,... | collective-permute-start | bytes 3145736 | tf_op jit(solution)/shard_map/ppermute | solution.py:956
  532.8 10.3 %copy-start.14 = (bf16[256,1024]{1,0:T(8,128)(2,1)S(1)}, bf16[256,1024]{1,0:T(8,128)(2,1)}, u32[]{:S(2)}) copy-start(bf16[256,1024]{1,0:T(8,128)(2,1)} %reduce-scatter.5.cloned.1.call-done) | copy-start | bytes 1572868
  532.8 17.2 %copy-start.8 = (bf16[128,1280]{1,0:T(8,128)(2,1)S(1)}, bf16[128,1280]{1,0:T(8,128)(2,1)}, u32[]{:S(2)}) copy-start(bf16[128,1280]{1,0:T(8,128)(2,1)} %reduce-scatter.3.cloned.1.call-done) | copy-start | bytes 983044
  532.8 17.2 %collective-permute-start.27 = (bf16[128,1280]{1,0:T(8,128)(2,1)}, bf16[128,1280]{1,0:T(8,128)(2,1)S(1)}, u32[]{:S(2)}, u32[]{:S(2)}) collective-permute-start(bf16[128,1280]{1,0:T(8,128)(2,1)} %reduce-scatter.3.cloned.1.call-done), channel_id=1, source_target_pairs={{0,16},{8,24},{16,0},{24,8},{1,17},{9,25},{17,1},{25,9},{2,18},{10... | collective-permute-start | bytes 983048 | tf_op jit(solution)/shard_map/ppermute | solution.py:941
  534.7 22.0 %collective-permute-start.26 = (bf16[4,128,384]{1,2,0:T(8,128)(2,1)S(1)}, bf16[4,128,384]{1,2,0:T(8,128)(2,1)S(1)}, u32[]{:S(2)}, u32[]{:S(2)}) collective-permute-start(bf16[4,128,384]{1,2,0:T(8,128)(2,1)S(1)} %add_convert_fusion.4), channel_id=1, source_target_pairs={{0,8},{8,0},{16,24},{24,16},{1,9},{9,1},{17,25},{25,17},{2,10},{10... | collective-permute-start | bytes 1179656 | tf_op jit(solution)/shard_map/ppermute | solution.py:941
  544.3 14.3 %collective-permute-start.30 = (bf16[256,1024]{1,0:T(8,128)(2,1)S(1)}, bf16[256,1024]{1,0:T(8,128)(2,1)}, u32[]{:S(2)}, u32[]{:S(2)}) collective-permute-start(bf16[256,1024]{1,0:T(8,128)(2,1)S(1)} %add_convert_fusion.3), channel_id=1, source_target_pairs={{0,8},{8,0},{16,24},{24,16},{1,9},{9,1},{17,25},{25,17},{2,10},{10... | collective-permute-start | bytes 1572872 | tf_op jit(solution)/shard_map/ppermute | solution.py:941
  550.9 10.7 %collective-permute-start.28 = (bf16[2,128,1280]{2,1,0:T(8,128)(2,1)}, bf16[2,128,1280]{2,1,0:T(8,128)(2,1)}, u32[]{:S(2)}, u32[]{:S(2)}) collective-permute-start(bf16[2,128,1280]{2,1,0:T(8,128)(2,1)} %maximum_select_fusion.4), channel_id=1, source_target_pairs={{0,8},{8,0},{16,24},{24,16},{1,9},{9,1},{17,25},{25,17},{2,10},{10... | collective-permute-start | bytes 1966088 | tf_op jit(solution)/shard_map/ppermute | solution.py:941
  571.5 1.6 copy-start.13
  573.1 3.2 copy-start.1
  (7 other events, 6.8 us)
Sparse Core Ops, SparseCore 0:
  63.4 139.6 all-gather.1
  287.6 101.9 reduce-scatter.4
  411.3 93.6 reduce-scatter.2

commit v2 on v1

--- a/solution.py
+++ b/solution.py
@@ -458,15 +458,17 @@
 
 def project_kernel(ids, own, y_one, z_one, top, bottom, w_own, w_other, out, leaving, natural):
     square = ids[SQUARE]
-    width = own.shape[1]
-    part = width // 8
-    weights = [w[:, 0:part, :].reshape(width, 3 * LANES) for w in (w_own, w_other)]
     corner = jnp.where(pl.program_id(0) < 2, top[...], bottom[...])
-    for j, rows in enumerate((own[...], y_one[...], z_one[...], corner)):
+    pieces = (own[...], y_one[...], z_one[...], corner)
+    rows = jnp.concatenate(pieces, axis=0)
+    size = corner.shape[0]
+    mine = dot_nn(rows, w_own[...]).astype(jnp.bfloat16)
+    other = dot_nn(rows, w_other[...]).astype(jnp.bfloat16)
+    for j in range(4):
         at = pl.ds(square ^ j, 1)
-        natural[at] = rows[None]
-        out[at] = dot_nn(rows, weights[0]).astype(jnp.bfloat16)[None]
-        leaving[at] = dot_nn(rows, weights[1]).astype(jnp.bfloat16)[None]
+        natural[at] = pieces[j][None]
+        out[at] = mine[None, j * size : (j + 1) * size]
+        leaving[at] = other[None, j * size : (j + 1) * size]
 
 
 def head_lanes(block, head):
@@ -486,74 +488,92 @@
 def first_frames(bounds, positions):
     start = jnp.zeros_like(positions)
     for u in range(1, UTTERANCES):
-        start = jnp.where(positions >= bounds[4, u], bounds[4, u], start)
+        start = jnp.where(positions >= bounds[2, u], bounds[2, u], start)
     return start
 
 
-def attend_kernel(ids, bounds, own, came, bias_row, out, lse, qkv, top, total, acc):
+def spread_places(places_row, column):
+    for j in range(places_row.shape[1] // TILE):
+        row = places_row[:, j * TILE : (j + 1) * TILE]
+        column[j * TILE : (j + 1) * TILE, :] = jnp.transpose(
+            jnp.broadcast_to(row, (LANES, TILE))
+        )
+
+
+def allowed_keys(column, at, start, diagonal):
+    places = jnp.concatenate([column[pl.ds(at, TILE), :]] * (TILE // LANES), axis=1)
+    allowed = places >= start
+    if diagonal:
+        key = lax.broadcasted_iota(jnp.int32, (TILE, TILE), 0)
+        query = lax.broadcasted_iota(jnp.int32, (TILE, TILE), 1)
+        allowed = (allowed & (key < query)) | (key == query)
+    return allowed
+
+
+def row_starts(bounds, base):
+    return first_frames(bounds, base + lax.broadcasted_iota(jnp.int32, (1, TILE), 1)).astype(
+        jnp.float32
+    )
+
+
+def attend_kernel(
+    ids, bounds, own, came, places_row, out, lse, qkv, turned, column, scores, top, total, acc
+):
     tile = pl.program_id(0)
     base = pl.multiple_of(tile * TILE, TILE)
 
     @pl.when(tile == 0)
     def _():
         join_heads(ids, own, came, qkv)
+        spread_places(places_row, column)
+        for j in range(qkv.shape[0] // TILE):
+            rows = slice(j * TILE, (j + 1) * TILE)
+            turned[:, rows] = jnp.transpose(qkv[rows, 2 * LANES : 3 * LANES])
 
     queries = [head_lanes(qkv[pl.ds(base, TILE), 0:LANES], head) for head in range(2)]
     top[...] = jnp.full_like(top, NEGATIVE)
     total[...] = jnp.zeros_like(total)
     acc[...] = jnp.zeros_like(acc)
 
-    def step(j, masked):
+    start = row_starts(bounds, base)
+
+    def step(j, diagonal):
         at = pl.multiple_of(j * TILE, TILE)
         keys = qkv[pl.ds(at, TILE), LANES : 2 * LANES]
-        values = qkv[pl.ds(at, TILE), 2 * LANES : 3 * LANES]
-        bias = bias_row[:, pl.ds(at, TILE)]
-        if masked:
-            key_pos = at + lax.broadcasted_iota(jnp.int32, (TILE, TILE), 1)
-            query_pos = base + lax.broadcasted_iota(jnp.int32, (TILE, TILE), 0)
-            column = base + lax.broadcasted_iota(jnp.int32, (TILE, 1), 0)
-            allowed = (
-                (key_pos >= first_frames(bounds, column))
-                & (key_pos <= query_pos)
-                & ((bias == 0.0) | (key_pos == query_pos))
+        allowed = allowed_keys(column, at, start, diagonal)
+        for head in range(2):
+            value = jnp.where(allowed, dot_nt(keys, queries[head]), NEGATIVE)
+            scores[head, j] = value
+            top[head : head + 1, :] = jnp.maximum(
+                top[head : head + 1, :], jnp.max(value, axis=0, keepdims=True)
             )
-        for head in range(2):
-            scores = dot_nt(queries[head], keys)
-            if masked:
-                scores = jnp.where(allowed, scores, NEGATIVE)
-            else:
-                scores = scores + bias
-            old = top[head]
-            new = jnp.maximum(old, jnp.max(scores, axis=1, keepdims=True))
-            probs = jnp.exp(scores - new[:, 0:1])
-            shrink = jnp.exp(old - new)
-            total[head] = total[head] * shrink + jnp.sum(probs, axis=1, keepdims=True)
-            acc[head] = acc[head] * shrink + dot_nn(probs.astype(jnp.bfloat16), values)
-            top[head] = new
-
-    def masked_step(j, carry):
-        step(j, True)
-        return carry
-
-    def free_step(j, carry):
+
+    def first_pass(j, carry):
         step(j, False)
         return carry
 
-    lax.fori_loop(bounds[0, tile], bounds[1, tile], masked_step, 0)
-    lax.fori_loop(bounds[1, tile], tile, free_step, 0)
+    def second_pass(j, carry):
+        at = pl.multiple_of(j * TILE, TILE)
+        for head in range(2):
+            probs = jnp.exp(scores[head, j] - top[head : head + 1, :])
+            total[head : head + 1, :] += jnp.sum(probs, axis=0, keepdims=True)
+            values = turned[head * HEAD_DIM : (head + 1) * HEAD_DIM, pl.ds(at, TILE)]
+            acc[head] += dot_nn(values, probs.astype(jnp.bfloat16))
+        return carry
+
+    lax.fori_loop(bounds[0, tile], tile, first_pass, 0)
     step(tile, True)
-    lane = lax.broadcasted_iota(jnp.int32, (TILE, LANES), 1)
-    out[0] = jnp.where(lane < HEAD_DIM, acc[0] / total[0], acc[1] / total[1]).astype(jnp.bfloat16)
-    for head in range(2):
-        column = top[head] + jnp.log(total[head])
-        lse[head : head + 1, pl.ds(base, TILE)] = jnp.transpose(column)[0:1, :]
+    lax.fori_loop(bounds[0, tile], tile + 1, second_pass, 0)
+    both = jnp.concatenate([acc[0] / total[0:1, :], acc[1] / total[1:2, :]], axis=0)
+    out[0] = jnp.transpose(both).astype(jnp.bfloat16)
+    lse[:, pl.ds(base, TILE)] = top[...] + jnp.log(total[...])
 
 
 def block_order(i):
     return 2 * (i % 4) + i // 4
 
 
-def attend(ids, bounds, own, came, bias_row):
+def attend(ids, bounds, own, came, places):
     rows = 2 * own.shape[0]
     return pl.pallas_call(
         attend_kernel,
@@ -570,15 +590,22 @@
                 pl.BlockSpec((1, TILE, LANES), lambda i, *_: (block_order(i), 0, 0)),
                 whole(2, rows),
             ],
-            scratch_shapes=[pltpu.VMEM((rows, 3 * LANES), jnp.bfloat16)]
-            + [pltpu.VMEM((2, TILE, LANES), jnp.float32)] * 3,
+            scratch_shapes=[
+                pltpu.VMEM((rows, 3 * LANES), jnp.bfloat16),
+                pltpu.VMEM((LANES, rows), jnp.bfloat16),
+                pltpu.VMEM((rows, LANES), jnp.float32),
+                pltpu.VMEM((2, rows // TILE, TILE, TILE), jnp.float32),
+                pltpu.VMEM((2, TILE), jnp.float32),
+                pltpu.VMEM((2, TILE), jnp.float32),
+                pltpu.VMEM((2, HEAD_DIM, TILE), jnp.float32),
+            ],
         ),
         compiler_params=PARAMS,
         cost_estimate=pl.CostEstimate(
             flops=rows * rows * 256 // SHRINK, bytes_accessed=rows * 2400, transcendentals=rows * rows
         ),
         name="attend",
-    )(ids, bounds, own, came, bias_row)
+    )(ids, bounds, own, came, places)
 
 
 def attend_back_kernel(
@@ -589,7 +616,7 @@
     grad_own,
     grad_came,
     attended,
-    bias_row,
+    places_row,
     lse,
     out,
     leaving,
@@ -598,6 +625,7 @@
     delta,
     grad_queries,
     grad_kv,
+    column,
 ):
     tile = pl.program_id(0)
     base = pl.multiple_of(tile * TILE, TILE)
@@ -606,6 +634,7 @@
     @pl.when(tile == 0)
     def _():
         join_heads(ids, own, came, qkv)
+        spread_places(places_row, column)
         grad_queries[...] = jnp.zeros_like(grad_queries)
         for j in range(4):
             for rows, side in ((grad_own, core), (grad_came, 1 - core)):
@@ -622,34 +651,20 @@
     keys = qkv[pl.ds(base, TILE), LANES : 2 * LANES]
     values = qkv[pl.ds(base, TILE), 2 * LANES : 3 * LANES]
     head_keys = [head_lanes(keys, head) for head in range(2)]
-    bias = jnp.broadcast_to(bias_row[:, pl.ds(base, TILE)], (LANES, TILE))
-    bias = jnp.transpose(bias)[:, 0:1]
     grad_kv[...] = jnp.zeros_like(grad_kv)
 
-    def step(i, masked):
+    def step(i, diagonal):
         at = pl.multiple_of(i * TILE, TILE)
         scaled = qkv[pl.ds(at, TILE), 0:LANES]
         grads = grad[pl.ds(at, TILE), :]
-        if masked:
-            key_pos = base + lax.broadcasted_iota(jnp.int32, (TILE, TILE), 0)
-            query_pos = at + lax.broadcasted_iota(jnp.int32, (TILE, TILE), 1)
-            row = at + lax.broadcasted_iota(jnp.int32, (1, TILE), 1)
-            allowed = (
-                (key_pos >= first_frames(bounds, row))
-                & (key_pos <= query_pos)
-                & ((bias == 0.0) | (key_pos == query_pos))
-            )
+        allowed = allowed_keys(column, base, row_starts(bounds, at), diagonal)
         query_part = jnp.zeros((TILE, LANES), jnp.float32)
         key_part = grad_kv[0]
         value_part = grad_kv[1]
         for head in range(2):
             queries = head_lanes(scaled, head)
             head_grads = head_lanes(grads, head)
-            scores = dot_nt(keys, queries)
-            if masked:
-                scores = jnp.where(allowed, scores, NEGATIVE)
-            else:
-                scores = scores + bias
+            scores = jnp.where(allowed, dot_nt(keys, queries), NEGATIVE)
             probs = jnp.exp(scores - lse[head : head + 1, pl.ds(at, TILE)])
             dprobs = dot_nt(values, head_grads)
             dscores = (probs * (dprobs - delta[head : head + 1, pl.ds(at, TILE)])).astype(
@@ -662,17 +677,12 @@
         grad_kv[1] = value_part
         grad_queries[pl.ds(at, TILE), :] += query_part
 
-    def masked_step(i, carry):
-        step(i, True)
-        return carry
-
-    def free_step(i, carry):
+    def later_step(i, carry):
         step(i, False)
         return carry
 
     step(tile, True)
-    lax.fori_loop(tile + 1, bounds[2, tile], free_step, 0)
-    lax.fori_loop(bounds[2, tile], bounds[3, tile], masked_step, 0)
+    lax.fori_loop(tile + 1, bounds[1, tile], later_step, 0)
 
     def store(target):
         at = pl.ds(pl.multiple_of((tile % 4) * TILE, TILE), TILE)
@@ -691,7 +701,7 @@
         store(leaving)
 
 
-def attend_back(ids, bounds, own, came, grad_own, grad_came, attended, bias_row, lse):
+def attend_back(ids, bounds, own, came, grad_own, grad_came, attended, places, lse):
     half = own.shape[0]
     rows = 2 * half
     return pl.pallas_call(
@@ -716,6 +726,7 @@
                 pltpu.VMEM((2, rows), jnp.float32),
                 pltpu.VMEM((rows, LANES), jnp.float32),
                 pltpu.VMEM((2, TILE, LANES), jnp.float32),
+                pltpu.VMEM((rows, LANES), jnp.float32),
             ],
         ),
         compiler_params=PARAMS,
@@ -723,24 +734,16 @@
             flops=rows * rows * 640 // SHRINK, bytes_accessed=rows * 2400, transcendentals=rows * rows
         ),
         name="attend_back",
-    )(ids, bounds, own, came, grad_own, grad_came, attended, bias_row, lse)
+    )(ids, bounds, own, came, grad_own, grad_came, attended, places, lse)
 
 
 def attend_bounds(start, starts, rows):
     tiles = rows // TILE
-    index = jnp.arange(tiles, dtype=jnp.int32)
     first = start[:: TILE]
-    last = start[TILE - 1 :: TILE]
-    low = first // TILE
-    middle = jnp.clip((last + TILE - 1) // TILE, low, index)
-    key_first = index * TILE
-    free_end = jnp.sum((last[None, :] <= key_first[:, None]).astype(jnp.int32), axis=1)
-    free_end = jnp.maximum(free_end, index + 1)
-    far_end = jnp.sum(
-        (first[None, :] <= key_first[:, None] + TILE - 1).astype(jnp.int32), axis=1
-    )
+    key_last = jnp.arange(1, tiles + 1, dtype=jnp.int32) * TILE - 1
+    far_end = jnp.sum((first[None, :] <= key_last[:, None]).astype(jnp.int32), axis=1)
     starts = jnp.pad(starts, (0, tiles - starts.shape[0]))
-    return jnp.stack([low, middle, free_end, far_end, starts]).astype(jnp.int32)
+    return jnp.stack([first // TILE, far_end, starts]).astype(jnp.int32)
 
 
 def out_kernel(ids, own, came, tokens, w_out, vectors, attended, middle, normed):
@@ -883,26 +886,23 @@
     leaving[:, :, half:] = jnp.where(chip_x == 0, more[:, :, cut:], more[:, :, :cut])
 
 
-def back_project_kernel(ids, own, came, w_own, w_other, first, y_out, z_out, keep_left, keep_right):
+def back_project_kernel(
+    ids, own, came, w_own, w_other, first, y_out, z_out, keep_left, keep_right, grads
+):
     square = ids[SQUARE]
-    width = first.shape[1]
-    part = width // 8
+    size, width = first.shape
     half = width // 2
-    weights = [w[:, 0:part, :].reshape(width, 3 * LANES) for w in (w_own, w_other)]
-    for j in range(4):
-        at = square ^ j
-        value = dot_nt(own[at], weights[0]) + dot_nt(came[at], weights[1])
-        if j == 0:
-            first[...] = value
-        if j == 1:
-            y_out[0] = value[:, :half].astype(jnp.bfloat16)
-            keep_right[...] = value[:, half:]
-        if j == 2:
-            z_out[0] = value[:, half:].astype(jnp.bfloat16)
-            keep_left[...] = value[:, :half]
-        if j == 3:
-            y_out[1] = value[:, :half].astype(jnp.bfloat16)
-            z_out[1] = value[:, half:].astype(jnp.bfloat16)
+    rows = 4 * size
+    value = dot_nt(own[...].reshape(rows, 3 * LANES), w_own[...])
+    value = value + dot_nt(came[...].reshape(rows, 3 * LANES), w_other[...])
+    grads[...] = value.reshape(4, size, width)
+    first[...] = grads[square]
+    y_out[0] = grads[square ^ 1, :, :half].astype(jnp.bfloat16)
+    keep_right[...] = grads[square ^ 1, :, half:]
+    z_out[0] = grads[square ^ 2, :, half:].astype(jnp.bfloat16)
+    keep_left[...] = grads[square ^ 2, :, :half]
+    y_out[1] = grads[square ^ 3, :, :half].astype(jnp.bfloat16)
+    z_out[1] = grads[square ^ 3, :, half:].astype(jnp.bfloat16)
 
 
 def second_kernel(ids, keep_left, keep_right, y_came, z_came, z_out, y_out):
@@ -936,6 +936,48 @@
     leaving[...] = dot_tn(normed[...], came[...]).astype(jnp.bfloat16)
 
 
+def spread_kernel(
+    ids,
+    heads,
+    heads_came,
+    down,
+    down_came,
+    mixed,
+    mixed_x,
+    mixed_core,
+    mixed_both,
+    qkv_out,
+    out_out,
+    up_out,
+    down_out,
+):
+    wide = jnp.float32
+    core, chip_x = ids[CORE], ids[CHIP_X]
+
+    def ordered(side, own, other):
+        return jnp.where(side == 0, own, other), jnp.where(side == 0, other, own)
+
+    for side, blocks in enumerate(ordered(core, heads[...], heads_came[...])):
+        for j in range(4):
+            for k in range(3):
+                at = k * 8 * LANES + (4 * side + j) * LANES
+                qkv_out[:, at : at + LANES] = blocks[j, :, k * LANES : (k + 1) * LANES].astype(wide)
+    rows = down.shape[0]
+    for side, block in enumerate(ordered(core, down[...], down_came[...])):
+        down_out[side * rows : (side + 1) * rows, :] = block.astype(wide)
+    own = ordered(chip_x, mixed[...], mixed_x[...])
+    came = ordered(chip_x, mixed_core[...], mixed_both[...])
+    width = out_out.shape[1]
+    step = 2 * LANES
+    for x in range(2):
+        for side, block in enumerate(ordered(core, own[x], came[x])):
+            for j in range(4):
+                at = (4 * x + j) * 2 * step + side * step
+                up_out[:, at : at + step] = block[:, j * step : (j + 1) * step].astype(wide)
+            at = side * 2 * step + x * step
+            out_out[:, at : at + step] = block[:, width:].astype(wide)
+
+
 def hop_batch(block, bit):
     size = lax.axis_size("batch")
     return lax.ppermute(block, "batch", [(i, i ^ bit) for i in range(size)])
@@ -966,14 +1008,6 @@
 
 IN_SQUARE = [[0, 1, 2, 3], [4, 5, 6, 7]]
 ALONG_Z = [[0, 2, 4, 6], [1, 3, 5, 7]]
-
-
-def by_side(side, own, other, axis):
-    return jnp.where(
-        side == 0,
-        jnp.concatenate([own, other], axis=axis),
-        jnp.concatenate([other, own], axis=axis),
-    )
 
 
 def square_shards(
@@ -1013,8 +1047,6 @@
     deep = bundle.shape[0]
 
     tokens_here = swap_halves(tokens[0])
-    heads = lax.dynamic_slice_in_dim(w_qkv.reshape(part, 3, 8, LANES), 4 * core, 4, 2)
-    heads = heads.transpose(2, 0, 1, 3).reshape(4, part, 3 * LANES)
     small = jnp.concatenate(
         [
             jnp.stack([ln1_gain, ln1_bias, ln2_gain, ln2_bias, out_bias, down_bias]),
@@ -1023,15 +1055,15 @@
         ],
         axis=0,
     )
-    small = jnp.broadcast_to(jnp.pad(small, ((0, 0), (0, 2 * part)))[None], (4, 16, 3 * part))
-    heads = jnp.concatenate([heads, small], axis=1)
-    w_heads = lax.all_to_all(
-        jnp.concatenate([heads, heads], axis=0), "seq", 0, 0, tiled=True
-    )
-    tokens_here, w_heads, bundle = lax.optimization_barrier((tokens_here, w_heads, bundle))
-    bundle = lax.all_gather(bundle, ("seq", "batch"), axis=0, tiled=True)
-    bundle = bundle.reshape(8, 4, deep, width)
-    vectors = w_heads[:, part:, :part].astype(wide).transpose(1, 0, 2).reshape(16, width)
+    small = lax.all_to_all(
+        jnp.broadcast_to(small[None], (8, 16, part)), "seq", 0, 0, tiled=True
+    )
+    vectors = small.astype(wide).transpose(1, 0, 2).reshape(16, width)
+
+    heads = lax.dynamic_slice_in_dim(w_qkv.reshape(part, 3, 8, LANES), 4 * core, 4, 2)
+    heads = heads.transpose(2, 0, 1, 3).reshape(4, part, 3 * LANES)
+    heads = after(jnp.concatenate([heads, heads], axis=0), small)
+    w_heads = lax.all_to_all(heads, "seq", 0, 0, tiled=True).reshape(width, 3 * LANES)
     w_other = hop_batch(w_heads, 1)
 
     meta = jnp.concatenate([key_mask[0], jnp.pad(lengths[0], (0, LANES - lengths.shape[1]))])
@@ -1044,7 +1076,7 @@
         jnp.where(starts[None, :] <= positions[:, None], starts[None, :], 0), axis=1
     ).astype(jnp.int32)
     bounds = attend_bounds(start, starts, rows)
-    bias = jnp.where(meta[:rows] == 1, 0.0, NEGATIVE).astype(wide)[None, :]
+    places = jnp.where(meta[:rows] == 1, positions, -1).astype(wide)[None, :]
 
     fourth = frames // 4
     slab = pl.BlockSpec((fourth, width), lambda i, *_: (i, 0))
@@ -1053,6 +1085,8 @@
     )(ids, tokens_here, vectors)
     y_one = hop_seq(normed_one, 1)
     z_one = hop_seq(normed_one, 2)
+    bundle = lax.all_gather(after(bundle, normed_one, w_heads), ("seq", "batch"), axis=0, tiled=True)
+    bundle = bundle.reshape(8, 4, deep, width)
     half = frames // 2
     top, bottom = hop_seq(y_one[:half], 2), hop_seq(z_one[half:], 1)
     heads_shape = (4, frames, 3 * LANES)
@@ -1075,21 +1109,22 @@
     natural = natural.reshape(4 * frames, width)
     cotangent_own = swap_halves(after(cotangent[0], leaving))
 
-    attended_heads, lse = attend(ids, bounds, qkv_own, qkv_came, bias)
+    attended_heads, lse = attend(ids, bounds, qkv_own, qkv_came, places)
     cotangent_came = hop_batch(cotangent_own, 1)
 
     mine = trade(attended_heads, IN_SQUARE)
     mine_came = hop_batch(mine, 1)
-    blocks = pl.BlockSpec((8, fourth, LANES), lambda i, *_: (0, i, 0))
+    blocks = pl.BlockSpec((8, half, LANES), lambda i, *_: (0, i, 0))
+    wide_slab = pl.BlockSpec((half, width), lambda i, *_: (i, 0))
     w_out_spec = pl.BlockSpec(
         (8, 4, part // 4, width), lambda *_: (0, 0, (deep * 4) // part - 1, 0)
     )
     attended, middle, normed_two = call(
         out_kernel,
         "out_project",
-        4,
-        [blocks, blocks, slab, w_out_spec, whole(16, width)],
-        [slab] * 3,
+        2,
+        [blocks, blocks, wide_slab, w_out_spec, whole(16, width)],
+        [wide_slab] * 3,
         (like((frames, width), low), like((frames, width), wide), like((frames, width), low)),
         flops=2 * frames * width * width,
     )(ids, mine, mine_came, tokens_here, bundle, vectors)
@@ -1154,9 +1189,9 @@
     grad_middle, grad_branch, spread, middle_sums = call(
         middle_kernel,
         "middle_back",
-        4,
-        [slab] * 4 + [w_out_spec, whole(16, width)],
-        [slab, slab, blocks, whole(8, width)],
+        2,
+        [wide_slab] * 4 + [w_out_spec, whole(16, width)],
+        [wide_slab, wide_slab, blocks, whole(8, width)],
         (
             like((frames, width), wide),
             like((frames, width), low),
@@ -1200,15 +1235,7 @@
         + hop_batch(result_leaving, 1).astype(wide)
         + vectors[5:6]
     ).astype(low)
-    result_home = swap_halves(result)
-
-    ups = jnp.zeros((4, width), wide)
-    ups = lax.dynamic_update_slice(ups, up_sums[:2], (2 * core, 0))
-    sums = jnp.concatenate([middle_sums[:4], ups])
-    sums = sums.reshape(8, 8, 1, part).transpose(1, 2, 0, 3)
-    early = jnp.broadcast_to(sums, (8, 4, 8, part)).reshape(32, 8, part)
-
-    early = lax.all_to_all(early, ("seq", "batch"), 0, 0, tiled=True)
+    result_home = swap_halves(result[None])
 
     grad_mine = after(grad_mine, result, up_leaving)
     grad_qkv, grad_leaving = attend_back(
@@ -1219,11 +1246,10 @@
         grad_mine,
         grad_mine_came,
         attended_heads,
-        bias,
+        places,
         lse,
     )
-    grad_leaving = after(grad_leaving, up_came, result_home, early)
-    sums = jnp.sum(early, axis=0)
+    grad_leaving = after(grad_leaving, up_came, result_home)
     mixed = (up_kept.astype(wide) + after(up_came, grad_leaving).astype(wide)).astype(low)
     mixed = lax.psum_scatter(
         mixed.reshape(width, width + width // 4), "seq", scatter_dimension=0, tiled=True
@@ -1246,6 +1272,7 @@
             like(pair[1:], wide),
             like(pair[1:], wide),
         ),
+        scratch=[pltpu.VMEM((4, fourth, width), wide)],
         flops=2 * 4 * frames * width * 6 * LANES,
     )(
         ids,
@@ -1256,15 +1283,6 @@
     )
     y_came, z_came = hop_seq(y_out, 1), hop_seq(z_out, 2)
 
-    z_second, y_second = call(
-        second_kernel,
-        "second",
-        4,
-        [half_spec, half_spec, pair_spec, pair_spec],
-        [half_spec, half_spec],
-        (like(pair[1:], low), like(pair[1:], low)),
-    )(ids, keep_left, keep_right, y_came, z_came)
-    z_second, y_second = hop_seq(z_second, 2), hop_seq(y_second, 1)
     heads_out = like((width, 3 * LANES), low)
     heads_kept, heads_leaving = call(
         grad_heads_kernel,
@@ -1277,7 +1295,23 @@
         flops=2 * 4 * frames * width * 6 * LANES,
     )(ids, after(natural, z_out), grad_qkv, grad_qkv_came)
     heads_came = hop_batch(heads_leaving, 1)
-
+    heads_sum = (heads_kept.astype(wide) + heads_came.astype(wide)).astype(low)
+    heads_came = hop_batch(heads_sum, 2)
+    down = after(down, z_out)
+    down_x = hop_batch(down, 2)
+    down = (down.astype(wide) + down_x.astype(wide)).astype(low)
+    y_came = after(y_came, heads_sum, down)
+    down_came = hop_batch(down, 1)
+
+    z_second, y_second = call(
+        second_kernel,
+        "second",
+        1,
+        [whole(*pair[1:])] * 2 + [whole(*pair)] * 2,
+        [whole(*pair[1:])] * 2,
+        (like(pair[1:], low), like(pair[1:], low)),
+    )(ids, keep_left, keep_right, y_came, z_came)
+    z_last, y_last = hop_seq(z_second, 2), hop_seq(y_second, 1)
     grad_inputs, last_sums = call(
         last_kernel,
         "last",
@@ -1285,49 +1319,63 @@
         [slab, pair_spec, pair_spec, half_spec, half_spec, slab, slab, whole(16, width)],
         [slab, whole(8, width)],
         (like((frames, width), low), like((8, width), wide)),
-    )(ids, first, y_came, z_came, z_second, y_second, tokens_here, grad_middle, vectors)
-    grad_inputs = swap_halves(grad_inputs)
-
-    heads_sum = (heads_kept.astype(wide) + heads_came.astype(wide)).astype(low)
+    )(ids, after(first, down_came, mixed), y_came, z_came, z_last, y_last, tokens_here, grad_middle, vectors)
+    mixed_x = hop_batch(mixed, 2)
+    grad_inputs = swap_halves(after(grad_inputs, mixed_x)[None])
+
+    heads_sum = (
+        after(heads_sum, z_last, y_last).astype(wide) + heads_came.astype(wide)
+    ).astype(low)
     heads_sum = lax.all_to_all(
         heads_sum.reshape(8, part, 3 * LANES), "seq", 0, 0, tiled=True
     ).astype(wide)
     heads_sum = (heads_sum[:4] + heads_sum[4:]).astype(low)
-    heads_sum = (heads_sum.astype(wide) + hop_batch(heads_sum, 2).astype(wide)).astype(low)
-    grad_qkv_w = by_side(core, heads_sum, hop_batch(heads_sum, 1), 0).astype(wide)
-    grad_qkv_w = (
-        grad_qkv_w.reshape(8, part, 3, LANES).transpose(1, 2, 0, 3).reshape(part, 3 * width)
-    )
-
-    down = (down.astype(wide) + hop_batch(down, 2).astype(wide)).astype(low)
-    grad_down_w = by_side(core, down, hop_batch(down, 1), 0).astype(wide)
-    mixed = jnp.stack([mixed, hop_batch(mixed, 2)])
-    mixed = by_side(chip_x, mixed[:1], mixed[1:], 0)
-    mixed = by_side(core, mixed[None], hop_batch(mixed, 1)[None], 0).astype(wide)
-    grad_up_w = mixed[..., :width].reshape(2, 2, part, 4, 2 * LANES)
-    grad_up_w = grad_up_w.transpose(2, 1, 3, 0, 4).reshape(part, 4 * width)
-    grad_out_w = mixed[..., width:].transpose(2, 0, 1, 3).reshape(part, width)
-
-    late = last_sums[:2]
-    late = late + hop_batch(late, 2)
-    late = late + hop_batch(late, 1)
+    heads_came = hop_batch(heads_sum, 1)
+    mixed_core, mixed_both = hop_batch(mixed, 1), hop_batch(mixed_x, 1)
+    grad_qkv_w, grad_out_w, grad_up_w, grad_down_w = call(
+        spread_kernel,
+        "spread",
+        1,
+        [whole(4, part, 3 * LANES)] * 2
+        + [whole(2 * part, width)] * 2
+        + [whole(part, width + width // 4)] * 4,
+        [
+            whole(part, 3 * width),
+            whole(part, width),
+            whole(part, 4 * width),
+            whole(4 * part, width),
+        ],
+        (
+            like((part, 3 * width), wide),
+            like((part, width), wide),
+            like((part, 4 * width), wide),
+            like((4 * part, width), wide),
+        ),
+    )(ids, heads_sum, heads_came, down, down_came, mixed, mixed_x, mixed_core, mixed_both)
+
+    ups = jnp.zeros((4, width), wide)
+    ups = lax.dynamic_update_slice(ups, up_sums[:2], (2 * core, 0))
+    sums = jnp.concatenate([last_sums[:2], middle_sums[:4], ups, jnp.zeros((6, width), wide)])
+    sums = sums + hop_batch(sums, 2)
+    sums = sums + hop_batch(sums, 1)
+    sums = after(sums, mixed_x)
     for bits in (1, 2, 4):
-        late = late + hop_seq(late, bits)
-    late = lax.dynamic_slice_in_dim(late, seq_index * part, part, 1)
+        sums = sums + hop_seq(sums, bits)
+    sums = lax.dynamic_slice_in_dim(sums, seq_index * part, part, 1)
     return (
-        result_home[None],
-        grad_inputs[None],
+        result_home,
+        grad_inputs,
         grad_qkv_w,
         grad_out_w,
         grad_up_w,
         grad_down_w,
-        late[0],
-        late[1],
         sums[0],
         sums[1],
         sums[2],
-        sums[4:8].reshape(4 * LANES),
         sums[3],
+        sums[4],
+        sums[6:10].reshape(4 * LANES),
+        sums[5],
     )
 
 

time: 592 us -> 547 us (0.924); the launches traced: 583 us -> 545 us
  Pallas kernels: 223 us -> 177 us
  starting transfers between devices: 68.2 us -> 84.6 us
  other arithmetic: 21.9 us -> 14.9 us
    pallas_call x1, Pallas kernels: 52.1 us -> 23.1 us  [attend(): pl.pallas_call(attend_kernel, out_shape=(like((8, TILE, LANES), jnp.bfloa...]
    all_to_all x2, waiting for transfers between devices: 28.7 us -> 50.3 us  [trade(): lax.all_to_all(block, 'seq', 0, 0, tiled=True, axis_index_groups=groups)]
    ppermute x4, waiting for transfers between devices: 49.9 us -> 28.4 us  [swap_halves(): return lax.ppermute(block, ('batch', 'seq'), route)]
    pallas_call x1, Pallas kernels: 54.3 us -> 36.8 us  [attend_back(): pl.pallas_call(attend_back_kernel, out_shape=(like(own.shape, jnp.bfloat1...]
    ppermute x21 -> x22, waiting for transfers between devices: 15.2 us -> 30.4 us  [hop_batch(): return lax.ppermute(block, 'batch', [(i, i ^ bit) for i in range(size)])]
    ppermute x11, waiting for transfers between devices: 124 us -> 109 us  [hop_seq(): return lax.ppermute(block, 'seq', [(i, i ^ bits) for i in range(size)])]
    reshape x9 -> x2, local copies, waits for them, and re-layouts: 11.8 us -> 1.22 us  [the longest x1 0.64 us: square_shards(): vectors = small.astype(wide).transpose(1, 0, 2).reshape(16, width)]
    ppermute x21 -> x22, starting transfers between devices: 22.4 us -> 27.5 us  [hop_batch(): return lax.ppermute(block, 'batch', [(i, i ^ bit) for i in range(size)])]
  transfers between devices with their start and end apart: 44 -> 45, of which waited for: 20 -> 23; matrix products, arithmetic and copies ran while one was open for 5% -> 5% of each run, Pallas kernels for 32% -> 25%
where the time goes in v2:
time: 547 us; the launch traced here: 545 us
  waiting for transfers between devices  222 us (41%)
  Pallas kernels  177 us (32%)
  starting transfers between devices  84.6 us (15%)
  local copies, waits for them, and re-layouts  32.8 us (6%)
  other arithmetic  14.9 us (3%)
  between operations  14.3 us (3%)
    pallas_call x13, Pallas kernels, run(): pl.pallas_call(kernel, out_shape=out_shape, grid_spec=pltpu.PrefetchScala...  117 us
    ppermute x11, waiting for transfers between devices, hop_seq(): return lax.ppermute(block, 'seq', [(i, i ^ bits) for i in range(size)])  109 us
    all_to_all x2, waiting for transfers between devices, trade(): lax.all_to_all(block, 'seq', 0, 0, tiled=True, axis_index_groups=groups)  50.3 us
    pallas_call x1, Pallas kernels, attend_back(): pl.pallas_call(attend_back_kernel, out_shape=(like(own.shape, jnp.bfloat1...  36.8 us
    ppermute x22, waiting for transfers between devices, hop_batch(): return lax.ppermute(block, 'batch', [(i, i ^ bit) for i in range(size)])  30.4 us
    ppermute x4, waiting for transfers between devices, swap_halves(): return lax.ppermute(block, ('batch', 'seq'), route)  28.4 us
    ppermute x22, starting transfers between devices, hop_batch(): return lax.ppermute(block, 'batch', [(i, i ^ bit) for i in range(size)])  27.5 us
    pallas_call x1, Pallas kernels, attend(): pl.pallas_call(attend_kernel, out_shape=(like((8, TILE, LANES), jnp.bfloa...  23.1 us
  transfers between devices with their start and end apart: 45, of which 23 were waited for; matrix products, arithmetic and copies ran while one was open for 5% of the time, Pallas kernels for 25%

profile of v2, /device:TPU:1, one launch (start us, length us, event | category | flops | bytes accessed | tf_op | source)
XLA Modules:
  0.0 544.9 jit_solution(10730640384247803884)
XLA Ops:
  7.2 1.7 concatenate.16
  9.5 6.4 %all-to-all-start = ((bf16[8,16,128]{2,1,0:T(8,128)(2,1)}), bf16[8,16,128]{2,1,0:T(8,128)(2,1)S(1)}, u32[]{:S(2)}, u32[]{:S(2)}) async-start(bf16[8,16,128]{2,1,0:T(8,128)(2,1)} %broadcast_in_dim.43), calls=%async_computation | async-start | bytes 65536 | tf_op jit(solution)/shard_map/all_to_all | solution.py:1058
  15.9 1.5 copy.42
  18.4 3.0 all-to-all-done
  21.4 3.5 all-to-all-start.1
  25.0 6.4 %collective-permute-start.1 = (bf16[512,1024]{1,0:T(8,128)(2,1)}, bf16[512,1024]{1,0:T(8,128)(2,1)S(1)}, u32[]{:S(2)}, u32[]{:S(2)}) collective-permute-start(bf16[512,1024]{1,0:T(8,128)(2,1)} %bitcast.118), channel_id=1, source_target_pairs={{0,0},{1,1},{2,2},{3,3},{4,8},{5,9},{6,10},{7,11},{8,4},{9,5},{10,... | collective-permute-start | bytes 3145736 | tf_op jit(solution)/shard_map/ppermute | solution.py:998
  31.4 2.6 reshape.152
  34.0 2.8 dynamic-slice_reduce_fusion
  39.9 28.1 %collective-permute-done.1.tokens = bf16[512,1024]{1,0:T(8,128)(2,1)S(1)} collective-permute-done((bf16[512,1024]{1,0:T(8,128)(2,1)}, bf16[512,1024]{1,0:T(8,128)(2,1)S(1)}, u32[]{:S(2)}, u32[]{:S(2)}) %collective-permute-start.1) | collective-permute-done | bytes 1048608 | tf_op jit(solution)/shard_map/ppermute | solution.py:998
  68.9 4.7 norm.1.own
  77.1 31.0 %collective-permute-done.3.z_one = bf16[512,1024]{1,0:T(8,128)(2,1)} collective-permute-done((bf16[512,1024]{1,0:T(8,128)(2,1)S(1)}, bf16[512,1024]{1,0:T(8,128)(2,1)}, u32[]{:S(2)}, u32[]{:S(2)}) %collective-permute-start.3) | collective-permute-done | bytes 1048608 | tf_op jit(solution)/shard_map/ppermute | solution.py:988
  111.9 13.8 %collective-permute-done.5.bottom = bf16[256,1024]{1,0:T(8,128)(2,1)} collective-permute-done((bf16[256,1024]{1,0:T(8,128)(2,1)S(1)}, bf16[256,1024]{1,0:T(8,128)(2,1)}, u32[]{:S(2)}, u32[]{:S(2)}) %collective-permute-start.5) | collective-permute-done | bytes 524320 | tf_op jit(solution)/shard_map/ppermute | solution.py:988
  125.7 17.7 %collective-permute-done.4.top = bf16[256,1024]{1,0:T(8,128)(2,1)S(1)} collective-permute-done((bf16[256,1024]{1,0:T(8,128)(2,1)S(1)}, bf16[256,1024]{1,0:T(8,128)(2,1)S(1)}, u32[]{:S(2)}, u32[]{:S(2)}) %collective-permute-start.4) | collective-permute-done | bytes 524320 | tf_op jit(solution)/shard_map/ppermute | solution.py:988
  144.2 9.9 %project.1 = (bf16[4,512,384]{2,1,0:T(8,128)(2,1)}, bf16[4,512,384]{2,1,0:T(8,128)(2,1)}, bf16[4,512,1024]{2,1,0:T(8,128)(2,1)}) custom-call(s32[4]{0:T(128)} %pad_add_fusion.2.ids, bf16[512,1024]{1,0:T(8,128)(2,1)} %norm.1.own, bf16[512,1024]{1,0:T(8,128)(2,1)} %collective-permute-done.2.y_one, bf16[512,1024]{1,0:T(8,128)(2,1)} %collective-permute-done.3.z_one, ...), custom_call_target="tpu_custom_call" | custom-call | flops 3221225472 | bytes 11534336 | tf_op jit(solution)/shard_map/project/pallas_call | solution.py:429
  155.5 3.3 collective-permute-done.7
  158.9 1.2 copy-done.29
  160.0 23.1 %attend.1 = (bf16[8,512,128]{2,1,0:T(8,128)(2,1)}, f32[2,4096]{1,0:T(2,128)}) custom-call(s32[4]{0:T(128)} %pad_add_fusion.2.ids, s32[3,8]{1,0:T(4,128)} %pad_add_fusion.1.bounds, bf16[2048,384]{1,0:T(8,128)(2,1)} %bitcast.122, bf16[2048,384]{1,0:T(8,128)(2,1)} %bitcast.115, f32[1,4096]{1,0:T(1,128)} %fusion.2.places_row), custom_call_target="tpu_custom_call" | custom-call | flops 4294967296 | bytes 9830400 | tf_op jit(solution)/shard_map/attend/pallas_call | solution.py:578
  183.2 3.6 all-to-all-start.2
  186.9 7.8 %collective-permute-start.10 = (bf16[512,1024]{1,0:T(8,128)(2,1)S(1)}, bf16[512,1024]{1,0:T(8,128)(2,1)S(1)}, u32[]{:S(2)}, u32[]{:S(2)}) collective-permute-start(bf16[512,1024]{1,0:T(8,128)(2,1)S(1)} %bitcast.119), channel_id=1, source_target_pairs={{0,0},{1,1},{2,2},{3,3},{4,8},{5,9},{6,10},{7,11},{8,4},{9,5},{10,... | collective-permute-start | bytes 3145736 | tf_op jit(solution)/shard_map/ppermute | solution.py:998
  194.7 33.6 %all-to-all-done.2.own = bf16[8,512,128]{2,1,0:T(8,128)(2,1)S(1)} async-done(((bf16[8,512,128]{2,1,0:T(8,128)(2,1)}), bf16[8,512,128]{2,1,0:T(8,128)(2,1)S(1)}, u32[]{:S(2)}, u32[]{:S(2)}) %all-to-all-start.2) | async-done | bytes 1048608 | tf_op jit(solution)/shard_map/all_to_all | solution.py:1006
  228.8 2.7 collective-permute-done.8.came
  231.5 5.7 %out_project.1 = (bf16[512,1024]{1,0:T(8,128)(2,1)}, f32[512,1024]{1,0:T(8,128)}, bf16[512,1024]{1,0:T(8,128)(2,1)}) custom-call(s32[4]{0:T(128)} %pad_add_fusion.2.ids, bf16[8,512,128]{2,1,0:T(8,128)(2,1)} %copy-done.7, bf16[8,512,128]{2,1,0:T(8,128)(2,1)} %collective-permute-done.8.came, bf16[512,1024]{1,0:T(8,128)(2,1)} %copy-done.2, ...), custom_call_target="tpu_custom_call" | custom-call | flops 1073741824 | bytes 44171264 | tf_op jit(solution)/shard_map/out_project/pallas_call | solution.py:429
  237.6 2.5 collective-permute-done.9.normed_came
  241.1 30.1 %feed_forward.1 = (bf16[2,512,2048]{2,1,0:T(8,128)(2,1)}, bf16[2,512,2048]{2,1,0:T(8,128)(2,1)}, f32[8,1024]{1,0:T(8,128)}, f32[512,1024]{1,0:T(8,128)}, bf16[51...) custom-call(s32[4]{0:T(128)} %pad_add_fusion.2.ids, ...), custom_call_target="tpu_custom_call" | custom-call | flops 17179869184 | bytes 159514624 | tf_op jit(solution)/shard_map/feed_forward/pallas_call | solution.py:429
  271.2 9.1 %grad_down.1 = bf16[2048,1024]{1,0:T(8,128)(2,1)} custom-call(s32[4]{0:T(128)} %pad_add_fusion.2.ids, bf16[2,512,2048]{2,1,0:T(8,128)(2,1)} %get-tuple-element.78.act, bf16[512,1024]{1,0:T(8,128)(2,1)} %copy-done.4, bf16[512,1024]{1,0:T(8,128)(2,1)} %copy-done.11), custom_call_target="tpu_custom_call" | custom-call | flops 4294967296 | bytes 12582912 | tf_op jit(solution)/shard_map/grad_down/pallas_call | solution.py:429
  280.3 1.2 copy-done.34
  281.9 2.3 collective-permute-done.14.back_came
  285.2 8.2 %middle_back.1 = (f32[512,1024]{1,0:T(8,128)}, bf16[512,1024]{1,0:T(8,128)(2,1)}, bf16[8,512,128]{2,1,0:T(8,128)(2,1)}, f32[8,1024]{1,0:T(8,128)}) custom-call(s32[4]{0:T(128)} %pad_add_fusion.2.ids, f32[512,1024]{1,0:T(8,128)} %get-tuple-element.79.back_own, bf16[512,1024]{1,0:T(8,128)(2,1)} %copy-done.12, f32[512,1024]{1,0:T(8,128)} %get-tuple-element.72.middle, ...), custom_call_target="tpu_custom_call" | custom-call | flops 1073741824 | bytes 50462720 | tf_op jit(solution)/shard_map/middle_back/pallas_call | solution.py:429
  293.3 4.6 grad_out.1
  298.3 4.3 all-to-all-start.3
  303.6 11.1 %grad_up.1 = (bf16[8,128,1280]{2,1,0:T(8,128)(2,1)}, bf16[8,128,1280]{2,1,0:T(8,128)(2,1)}) custom-call(s32[4]{0:T(128)} %pad_add_fusion.2.ids, bf16[512,1024]{1,0:T(8,128)(2,1)} %get-tuple-element.73.normed_own, bf16[512,1024]{1,0:T(8,128)(2,1)} %copy-done.10, bf16[2,512,2048]{2,1,0:T(8,128)(2,1)} %get-tuple-element.82.grad_up, ...), custom_call_target="tpu_custom_call" | custom-call | flops 4294967296 | bytes 16777216 | tf_op jit(solution)/shard_map/grad_up/pallas_call | solution.py:429
  314.7 1.4 collective-permute-start.17
  316.6 16.7 %all-to-all-done.3.grad_own = bf16[8,512,128]{2,1,0:T(8,128)(2,1)} async-done(((bf16[8,512,128]{2,1,0:T(8,128)(2,1)}), bf16[8,512,128]{2,1,0:T(8,128)(2,1)}, u32[]{:S(2)}, u32[]{:S(2)}) %all-to-all-start.3) | async-done | bytes 1048608 | tf_op jit(solution)/shard_map/all_to_all | solution.py:1006
  333.8 2.3 add_convert_fusion.1
  336.1 2.5 collective-permute-start.13
  339.5 36.8 %attend_back.1 = (bf16[2048,384]{1,0:T(8,128)(2,1)}, bf16[2048,384]{1,0:T(8,128)(2,1)}) custom-call(s32[4]{0:T(128)} %pad_add_fusion.2.ids, s32[3,8]{1,0:T(4,128)} %pad_add_fusion.1.bounds, bf16[2048,384]{1,0:T(8,128)(2,1)} %bitcast.123, bf16[2048,384]{1,0:T(8,128)(2,1)} %bitcast.116, bf16[8,512,128]{2,1,0:T(8,128)(2,1)} %all-to-all-done.3.grad_own, ...), custom_call_target="tpu_custom_call" | custom-call | flops 10737418240 | bytes 9830400 | tf_op jit(solution)/shard_map/attend_back/pallas_call | solution.py:707
  376.7 4.2 add_convert_fusion
  380.9 1.4 copy-done.30
  382.3 3.4 collective-permute-done.18.came
  386.9 9.4 %back_project.1 = (f32[512,1024]{1,0:T(8,128)}, bf16[2,512,512]{2,1,0:T(8,128)(2,1)}, bf16[2,512,512]{2,1,0:T(8,128)(2,1)}, f32[512,512]{1,0:T(8,128)}, f32[512,512]{1,0:T(8,128)}) custom-call(s32[4]{0:T(128)} %pad_add_fusion.2.ids, bf16[4,512,384]{2,1,0:T(8,128)(2,1)} %bitcast.124, bf16[4,512,384]{2,1,0:T(8,128)(2,1)} %bitcast.117, ...), custom_call_target="tpu_custom_call" | custom-call | flops 3221225472 | bytes 9437184 | tf_op jit(solution)/shard_map/back_project/pallas_call | solution.py:429
  396.3 8.7 %grad_heads.1 = (bf16[1024,384]{1,0:T(8,128)(2,1)}, bf16[1024,384]{1,0:T(8,128)(2,1)}) custom-call(s32[4]{0:T(128)} %pad_add_fusion.2.ids, bf16[2048,1024]{1,0:T(8,128)(2,1)} %bitcast.121, bf16[2048,384]{1,0:T(8,128)(2,1)} %get-tuple-element.90.own, bf16[2048,384]{1,0:T(8,128)(2,1)} %copy-done.31), custom_call_target="tpu_custom_call" | custom-call | flops 3221225472 | bytes 14680064 | tf_op jit(solution)/shard_map/grad_heads/pallas_call | solution.py:429
  405.1 2.5 collective-permute-start.21
  408.5 4.3 collective-permute-start.19
  413.7 1.6 add_convert_fusion.3
  415.4 9.2 %collective-permute-done.19 = bf16[256,1024]{1,0:T(8,128)(2,1)S(1)} collective-permute-done((bf16[256,1024]{1,0:T(8,128)(2,1)}, bf16[256,1024]{1,0:T(8,128)(2,1)S(1)}, u32[]{:S(2)}, u32[]{:S(2)}) %collective-permute-start.19) | collective-permute-done | bytes 524320 | tf_op jit(solution)/shard_map/ppermute | solution.py:983
  425.5 15.3 %collective-permute-done.21.y_came = bf16[2,512,512]{2,1,0:T(8,128)(2,1)S(1)} collective-permute-done((bf16[2,512,512]{2,1,0:T(8,128)(2,1)}, bf16[2,512,512]{2,1,0:T(8,128)(2,1)S(1)}, u32[]{:S(2)}, u32[]{:S(2)}) %collective-permute-start.21) | collective-permute-done | bytes 1048608 | tf_op jit(solution)/shard_map/ppermute | solution.py:988
  442.1 3.9 second.1
  446.3 1.2 collective-permute-start.25
  447.5 1.2 collective-permute-start.20
  448.7 17.8 %collective-permute-done.24.z_second = bf16[512,512]{1,0:T(8,128)(2,1)S(1)} collective-permute-done((bf16[512,512]{1,0:T(8,128)(2,1)}, bf16[512,512]{1,0:T(8,128)(2,1)S(1)}, u32[]{:S(2)}, u32[]{:S(2)}) %collective-permute-start.24) | collective-permute-done | bytes 524320 | tf_op jit(solution)/shard_map/ppermute | solution.py:988
  466.5 1.2 add_convert_fusion.2
  467.7 8.8 %all-to-all-start.4 = ((bf16[8,128,384]{2,1,0:T(8,128)(2,1)}), bf16[8,128,384]{2,1,0:T(8,128)(2,1)S(1)}, u32[]{:S(2)}, u32[]{:S(2)}) async-start(bf16[8,128,384]{2,1,0:T(8,128)(2,1)} %bitcast.37), calls=%async_computation.6 | async-start | bytes 1572864 | tf_op jit(solution)/shard_map/all_to_all | solution.py:1329
  477.4 6.4 %last.1 = (bf16[512,1024]{1,0:T(8,128)(2,1)}, f32[8,1024]{1,0:T(8,128)}) custom-call(s32[4]{0:T(128)} %pad_add_fusion.2.ids, f32[512,1024]{1,0:T(8,128)} %get-tuple-element.98.first, bf16[2,512,512]{2,1,0:T(8,128)(2,1)} %copy-done.5, bf16[2,512,512]{2,1,0:T(8,128)(2,1)} %copy-done.6, bf16[512,512]{1,0:T(8,128)(2,1)} %copy-done.19, ...), custom_call_target="tpu_custom_call" | custom-call | bytes 16908288 | tf_op jit(solution)/shard_map/last/pallas_call | solution.py:429
  486.2 6.1 %collective-permute-done.32 = f32[16,1024]{1,0:T(8,128)S(1)} collective-permute-done((f32[16,1024]{1,0:T(8,128)S(1)}, f32[16,1024]{1,0:T(8,128)S(1)}, u32[]{:S(2)}, u32[]{:S(2)}) %collective-permute-start.32) | collective-permute-done | bytes 65568 | tf_op jit(solution)/shard_map/ppermute | solution.py:983
  492.3 3.9 collective-permute-start.33
  496.3 4.2 collective-permute-start.27
  500.5 1.2 collective-permute-start.34
  501.7 1.9 collective-permute-done.34
  503.7 1.2 collective-permute-start.35
  504.9 8.9 %collective-permute-done.35 = f32[16,1024]{1,0:T(8,128)S(1)} collective-permute-done((f32[16,1024]{1,0:T(8,128)S(1)}, f32[16,1024]{1,0:T(8,128)S(1)}, u32[]{:S(2)}, u32[]{:S(2)}) %collective-permute-start.35) | collective-permute-done | bytes 65568 | tf_op jit(solution)/shard_map/ppermute | solution.py:988
  513.9 3.5 collective-permute-start.30
  517.5 2.7 collective-permute-done.36
  520.4 8.2 %collective-permute-start.29 = (bf16[4,128,384]{2,1,0:T(8,128)(2,1)S(1)}, bf16[4,128,384]{2,1,0:T(8,128)(2,1)S(1)}, u32[]{:S(2)}, u32[]{:S(2)}) collective-permute-start(bf16[4,128,384]{2,1,0:T(8,128)(2,1)S(1)} %fusion.heads), channel_id=1, source_target_pairs={{0,8},{8,0},{16,24},{24,16},{1,9},{9,1},{17,25},{25,17},{2,10},{10... | collective-permute-start | bytes 1179656 | tf_op jit(solution)/shard_map/ppermute | solution.py:983
  531.1 5.3 spread.1
  (175 shorter events, 36.0 us)
Async XLA Ops:
  7.2 31.2 %copy-start = (bf16[512,1024]{1,0:T(8,128)(2,1)S(1)}, bf16[512,1024]{1,0:T(8,128)(2,1)}, u32[]{:S(2)}) copy-start(bf16[512,1024]{1,0:T(8,128)(2,1)} %param.22) | copy-start | bytes 3145732
  9.5 11.9 %all-to-all-start = ((bf16[8,16,128]{2,1,0:T(8,128)(2,1)}), bf16[8,16,128]{2,1,0:T(8,128)(2,1)S(1)}, u32[]{:S(2)}, u32[]{:S(2)}) async-start(bf16[8,16,128]{2,1,0:T(8,128)(2,1)} %broadcast_in_dim.43), calls=%async_computation | async-start | bytes 65536 | tf_op jit(solution)/shard_map/all_to_all | solution.py:1058
  21.4 52.2 %all-to-all-start.1 = ((bf16[8,128,384]{1,2,0:T(8,128)(2,1)}), bf16[8,128,384]{1,2,0:T(8,128)(2,1)S(1)}, u32[]{:S(2)}, u32[]{:S(2)}) async-start(bf16[8,128,384]{1,2,0:T(8,128)(2,1)} %pad_maximum_fusion), calls=%async_computation.1 | async-start | bytes 1572864 | tf_op jit(solution)/shard_map/all_to_all | solution.py:1066
  25.0 206.5 %all-gather.2.cloned.1.call-start = ((), (), s32[]{:S(2)}) async-start(), calls=%async_computation.7 | async-start | bytes 19464192 | tf_op jit(solution)/shard_map/all_gather | solution.py:1088
  25.0 43.0 %collective-permute-start.1 = (bf16[512,1024]{1,0:T(8,128)(2,1)}, bf16[512,1024]{1,0:T(8,128)(2,1)S(1)}, u32[]{:S(2)}, u32[]{:S(2)}) collective-permute-start(bf16[512,1024]{1,0:T(8,128)(2,1)} %bitcast.118), channel_id=1, source_target_pairs={{0,0},{1,1},{2,2},{3,3},{4,8},{5,9},{6,10},{7,11},{8,4},{9,5},{10,... | collective-permute-start | bytes 3145736 | tf_op jit(solution)/shard_map/ppermute | solution.py:998
  68.9 6.9 %copy-start.26 = (s32[1,4096]{1,0:T(1,128)S(1)}, s32[1,4096]{1,0:T(1,128)}, u32[]{:S(2)}) copy-start(s32[1,4096]{1,0:T(1,128)} %param.17) | copy-start | bytes 49156
  68.9 6.9 %copy-start.28 = (s32[1,4]{1,0:T(1,128)S(1)}, s32[1,4]{1,0:T(1,128)}, u32[]{:S(2)}) copy-start(s32[1,4]{1,0:T(1,128)} %param.16) | copy-start | bytes 52
  74.0 69.5 %copy-start.16 = (bf16[8,128,384]{2,1,0:T(8,128)(2,1)}, bf16[8,128,384]{2,1,0:T(8,128)(2,1)S(1)}, u32[]{:S(2)}) copy-start(bf16[8,128,384]{2,1,0:T(8,128)(2,1)S(1)} %copy.44) | copy-start | bytes 2359300
  74.8 33.4 %collective-permute-start.3 = (bf16[512,1024]{1,0:T(8,128)(2,1)S(1)}, bf16[512,1024]{1,0:T(8,128)(2,1)}, u32[]{:S(2)}, u32[]{:S(2)}) collective-permute-start(bf16[512,1024]{1,0:T(8,128)(2,1)S(1)} %copy-done.13), channel_id=1, source_target_pairs={{0,2},{1,3},{2,0},{3,1},{4,6},{5,7},{6,4},{7,5},{8,10},{9,11},{10,... | collective-permute-start | bytes 3145736 | tf_op jit(solution)/shard_map/ppermute | solution.py:988
  74.8 35.5 %collective-permute-start.2 = (bf16[512,1024]{1,0:T(8,128)(2,1)S(1)}, bf16[512,1024]{1,0:T(8,128)(2,1)}, u32[]{:S(2)}, u32[]{:S(2)}) collective-permute-start(bf16[512,1024]{1,0:T(8,128)(2,1)S(1)} %copy-done.13), channel_id=1, source_target_pairs={{0,1},{1,0},{2,3},{3,2},{4,5},{5,4},{6,7},{7,6},{8,9},{9,8},{10,11... | collective-permute-start | bytes 3145736 | tf_op jit(solution)/shard_map/ppermute | solution.py:988
  75.9 1.3 collective-permute-start
  76.0 35.9 %collective-permute-start.6 = (bf16[1024,384]{1,0:T(8,128)(2,1)S(1)}, bf16[1024,384]{1,0:T(8,128)(2,1)}, u32[]{:S(2)}, u32[]{:S(2)}) collective-permute-start(bf16[1024,384]{1,0:T(8,128)(2,1)S(1)} %bitcast.97), channel_id=1, source_target_pairs={{0,8},{8,0},{16,24},{24,16},{1,9},{9,1},{17,25},{25,17},{2,10},{10... | collective-permute-start | bytes 2359304 | tf_op jit(solution)/shard_map/ppermute | solution.py:983
  109.3 16.5 %collective-permute-start.5 = (bf16[256,1024]{1,0:T(8,128)(2,1)S(1)}, bf16[256,1024]{1,0:T(8,128)(2,1)}, u32[]{:S(2)}, u32[]{:S(2)}) collective-permute-start(bf16[256,1024]{1,0:T(8,128)(2,1)S(1)} %slice.77), channel_id=1, source_target_pairs={{0,1},{1,0},{2,3},{3,2},{4,5},{5,4},{6,7},{7,6},{8,9},{9,8},{10,11... | collective-permute-start | bytes 1572872 | tf_op jit(solution)/shard_map/ppermute | solution.py:988
  111.4 32.1 %collective-permute-start.4 = (bf16[256,1024]{1,0:T(8,128)(2,1)S(1)}, bf16[256,1024]{1,0:T(8,128)(2,1)S(1)}, u32[]{:S(2)}, u32[]{:S(2)}) collective-permute-start(bf16[256,1024]{1,0:T(8,128)(2,1)S(1)} %slice.76), channel_id=1, source_target_pairs={{0,2},{1,3},{2,0},{3,1},{4,6},{5,7},{6,4},{7,5},{8,10},{9,11},{10,... | collective-permute-start | bytes 1572872 | tf_op jit(solution)/shard_map/ppermute | solution.py:988
  154.1 4.8 collective-permute-start.7
  183.2 3.7 copy-start.32
  183.2 45.1 %all-to-all-start.2 = ((bf16[8,512,128]{2,1,0:T(8,128)(2,1)}), bf16[8,512,128]{2,1,0:T(8,128)(2,1)S(1)}, u32[]{:S(2)}, u32[]{:S(2)}) async-start(bf16[8,512,128]{2,1,0:T(8,128)(2,1)} %get-tuple-element.70.attended), calls=%async_computation.2 | async-start | bytes 2097152 | tf_op jit(solution)/shard_map/all_to_all | solution.py:1006
  186.8 221.6 %reduce-scatter.3.cloned.1.call-start = ((), (), s32[]{:S(2)}) async-start(), calls=%async_computation.8 | async-start | bytes 4718592 | tf_op jit(solution)/shard_map/reduce_scatter | solution.py:1188
  186.9 41.8 %collective-permute-start.10 = (bf16[512,1024]{1,0:T(8,128)(2,1)S(1)}, bf16[512,1024]{1,0:T(8,128)(2,1)S(1)}, u32[]{:S(2)}, u32[]{:S(2)}) collective-permute-start(bf16[512,1024]{1,0:T(8,128)(2,1)S(1)} %bitcast.119), channel_id=1, source_target_pairs={{0,0},{1,1},{2,2},{3,3},{4,8},{5,9},{6,10},{7,11},{8,4},{9,5},{10,... | collective-permute-start | bytes 3145736 | tf_op jit(solution)/shard_map/ppermute | solution.py:998
  228.2 3.2 copy-start.7
  228.2 3.2 collective-permute-start.8
  228.7 8.5 %copy-start.4 = (bf16[512,1024]{1,0:T(8,128)(2,1)}, bf16[512,1024]{1,0:T(8,128)(2,1)S(1)}, u32[]{:S(2)}) copy-start(bf16[512,1024]{1,0:T(8,128)(2,1)S(1)} %collective-permute-done.10.grad_own.cotangent) | copy-start | bytes 3145732
  228.7 8.9 %collective-permute-start.11 = (bf16[512,1024]{1,0:T(8,128)(2,1)S(1)}, bf16[512,1024]{1,0:T(8,128)(2,1)S(1)}, u32[]{:S(2)}, u32[]{:S(2)}) collective-permute-start(bf16[512,1024]{1,0:T(8,128)(2,1)S(1)} %collective-permute-done.10.grad_own.cotangent), channel_id=1, source_target_pairs={{0,8},{8,0},{16,24},{24,16},{1,9},{9,1},{17,25},{25,17},{2,10},{10... | collective-permute-start | bytes 3145736 | tf_op jit(solution)/shard_map/ppermute | solution.py:983
  237.2 2.9 collective-permute-start.9
  281.5 2.7 collective-permute-start.14
  297.9 4.7 collective-permute-start.15
  298.3 35.0 %all-to-all-start.3 = ((bf16[8,512,128]{2,1,0:T(8,128)(2,1)}), bf16[8,512,128]{2,1,0:T(8,128)(2,1)}, u32[]{:S(2)}, u32[]{:S(2)}) async-start(bf16[8,512,128]{2,1,0:T(8,128)(2,1)} %get-tuple-element.81), calls=%async_computation.3 | async-start | bytes 2097152 | tf_op jit(solution)/shard_map/all_to_all | solution.py:1006
  302.5 174.9 %reduce-scatter.5.cloned.1.call-start = ((), (), s32[]{:S(2)}) async-start(), calls=%async_computation.9 | async-start | bytes 2949120 | tf_op jit(solution)/shard_map/reduce_scatter | solution.py:1254
  303.6 30.2 %copy-start.3 = (f32[512,1024]{1,0:T(8,128)S(1)}, f32[512,1024]{1,0:T(8,128)}, u32[]{:S(2)}) copy-start(f32[512,1024]{1,0:T(8,128)} %get-tuple-element.72.middle) | copy-start | bytes 6291460
  314.7 62.0 %collective-permute-start.17 = (bf16[8,128,1280]{2,1,0:T(8,128)(2,1)}, bf16[8,128,1280]{2,1,0:T(8,128)(2,1)}, u32[]{:S(2)}, u32[]{:S(2)}) collective-permute-start(bf16[8,128,1280]{2,1,0:T(8,128)(2,1)} %get-tuple-element.87), channel_id=1, source_target_pairs={{0,16},{8,24},{16,0},{24,8},{1,17},{9,25},{17,1},{25,9},{2,18},{10... | collective-permute-start | bytes 7864328 | tf_op jit(solution)/shard_map/ppermute | solution.py:983
  316.1 17.7 %collective-permute-start.12 = (bf16[512,1024]{1,0:T(8,128)(2,1)}, bf16[512,1024]{1,0:T(8,128)(2,1)S(1)}, u32[]{:S(2)}, u32[]{:S(2)}) collective-permute-start(bf16[512,1024]{1,0:T(8,128)(2,1)} %get-tuple-element.76), channel_id=1, source_target_pairs={{0,8},{8,0},{16,24},{24,16},{1,9},{9,1},{17,25},{25,17},{2,10},{10... | collective-permute-start | bytes 3145736 | tf_op jit(solution)/shard_map/ppermute | solution.py:983
  333.2 5.3 collective-permute-start.16
  336.1 40.6 %collective-permute-start.13 = (bf16[1,512,1024]{2,1,0:T(8,128)(2,1)S(1)}, bf16[1,512,1024]{2,1,0:T(8,128)(2,1)S(1)}, u32[]{:S(2)}, u32[]{:S(2)}) collective-permute-start(bf16[1,512,1024]{2,1,0:T(8,128)(2,1)S(1)} %bitcast.96), channel_id=1, source_target_pairs={{0,0},{1,1},{2,2},{3,3},{4,8},{5,9},{6,10},{7,11},{8,4},{9,5},{10,... | collective-permute-start | bytes 3145736 | tf_op jit(solution)/shard_map/ppermute | solution.py:998
  339.5 37.1 %copy-start.8 = (bf16[8,128,1280]{2,1,0:T(8,128)(2,1)S(1)}, bf16[8,128,1280]{2,1,0:T(8,128)(2,1)}, u32[]{:S(2)}) copy-start(bf16[8,128,1280]{2,1,0:T(8,128)(2,1)} %get-tuple-element.96) | copy-start | bytes 7864324
  376.7 4.2 copy-start.14
  382.3 3.4 collective-permute-start.18
  405.0 7.8 %collective-permute-start.22 = (bf16[1024,384]{1,0:T(8,128)(2,1)}, bf16[1024,384]{1,0:T(8,128)(2,1)S(1)}, u32[]{:S(2)}, u32[]{:S(2)}) collective-permute-start(bf16[1024,384]{1,0:T(8,128)(2,1)} %get-tuple-element.103), channel_id=1, source_target_pairs={{0,8},{8,0},{16,24},{24,16},{1,9},{9,1},{17,25},{25,17},{2,10},{10... | collective-permute-start | bytes 2359304 | tf_op jit(solution)/shard_map/ppermute | solution.py:983
  405.1 35.7 %collective-permute-start.21 = (bf16[2,512,512]{2,1,0:T(8,128)(2,1)}, bf16[2,512,512]{2,1,0:T(8,128)(2,1)S(1)}, u32[]{:S(2)}, u32[]{:S(2)}) collective-permute-start(bf16[2,512,512]{2,1,0:T(8,128)(2,1)} %get-tuple-element.99), channel_id=1, source_target_pairs={{0,1},{1,0},{2,3},{3,2},{4,5},{5,4},{6,7},{7,6},{8,9},{9,8},{10,11... | collective-permute-start | bytes 3145736 | tf_op jit(solution)/shard_map/ppermute | solution.py:988
  407.6 33.4 %collective-permute-start.23 = (bf16[2,512,512]{2,1,0:T(8,128)(2,1)}, bf16[2,512,512]{2,1,0:T(8,128)(2,1)S(1)}, u32[]{:S(2)}, u32[]{:S(2)}) collective-permute-start(bf16[2,512,512]{2,1,0:T(8,128)(2,1)} %get-tuple-element.94), channel_id=1, source_target_pairs={{0,2},{1,3},{2,0},{3,1},{4,6},{5,7},{6,4},{7,5},{8,10},{9,11},{10,... | collective-permute-start | bytes 3145736 | tf_op jit(solution)/shard_map/ppermute | solution.py:988
  408.5 16.1 %copy-start.18 = (bf16[256,1024]{1,0:T(8,128)(2,1)S(1)}, bf16[256,1024]{1,0:T(8,128)(2,1)}, u32[]{:S(2)}) copy-start(bf16[256,1024]{1,0:T(8,128)(2,1)} %reduce-scatter.3.cloned.1.call-done) | copy-start | bytes 1572868
  408.5 16.1 %collective-permute-start.19 = (bf16[256,1024]{1,0:T(8,128)(2,1)}, bf16[256,1024]{1,0:T(8,128)(2,1)S(1)}, u32[]{:S(2)}, u32[]{:S(2)}) collective-permute-start(bf16[256,1024]{1,0:T(8,128)(2,1)} %reduce-scatter.3.cloned.1.call-done), channel_id=1, source_target_pairs={{0,16},{8,24},{16,0},{24,8},{1,17},{9,25},{17,1},{25,9},{2,18},{10... | collective-permute-start | bytes 1572872 | tf_op jit(solution)/shard_map/ppermute | solution.py:983
  415.3 51.2 %collective-permute-start.28 = (bf16[1024,384]{1,0:T(8,128)(2,1)S(1)}, bf16[1024,384]{1,0:T(8,128)(2,1)S(1)}, u32[]{:S(2)}, u32[]{:S(2)}) collective-permute-start(bf16[1024,384]{1,0:T(8,128)(2,1)S(1)} %add_convert_fusion.3), channel_id=1, source_target_pairs={{0,16},{8,24},{16,0},{24,8},{1,17},{9,25},{17,1},{25,9},{2,18},{10... | collective-permute-start | bytes 2359304 | tf_op jit(solution)/shard_map/ppermute | solution.py:983
  446.0 31.4 %copy-start.27 = (f32[8,1024]{1,0:T(8,128)S(1)}, f32[8,1024]{1,0:T(8,128)}, u32[]{:S(2)}) copy-start(f32[8,1024]{1,0:T(8,128)} %get-tuple-element.118) | copy-start | bytes 98308
  446.0 20.5 %collective-permute-start.24 = (bf16[512,512]{1,0:T(8,128)(2,1)}, bf16[512,512]{1,0:T(8,128)(2,1)S(1)}, u32[]{:S(2)}, u32[]{:S(2)}) collective-permute-start(bf16[512,512]{1,0:T(8,128)(2,1)} %get-tuple-element.107), channel_id=1, source_target_pairs={{0,2},{1,3},{2,0},{3,1},{4,6},{5,7},{6,4},{7,5},{8,10},{9,11},{10,... | collective-permute-start | bytes 1572872 | tf_op jit(solution)/shard_map/ppermute | solution.py:988
  446.3 20.2 %collective-permute-start.25 = (bf16[512,512]{1,0:T(8,128)(2,1)}, bf16[512,512]{1,0:T(8,128)(2,1)S(1)}, u32[]{:S(2)}, u32[]{:S(2)}) collective-permute-start(bf16[512,512]{1,0:T(8,128)(2,1)} %get-tuple-element.108), channel_id=1, source_target_pairs={{0,1},{1,0},{2,3},{3,2},{4,5},{5,4},{6,7},{7,6},{8,9},{9,8},{10,11... | collective-permute-start | bytes 1572872 | tf_op jit(solution)/shard_map/ppermute | solution.py:988
  447.5 29.9 %collective-permute-start.20 = (bf16[256,1024]{1,0:T(8,128)(2,1)}, bf16[256,1024]{1,0:T(8,128)(2,1)S(1)}, u32[]{:S(2)}, u32[]{:S(2)}) collective-permute-start(bf16[256,1024]{1,0:T(8,128)(2,1)} %add_convert_fusion.4.down), channel_id=1, source_target_pairs={{0,8},{8,0},{16,24},{24,16},{1,9},{9,1},{17,25},{25,17},{2,10},{10... | collective-permute-start | bytes 1572872 | tf_op jit(solution)/shard_map/ppermute | solution.py:983
  466.5 10.9 %copy-start.19 = (bf16[512,512]{1,0:T(8,128)(2,1)}, bf16[512,512]{1,0:T(8,128)(2,1)S(1)}, u32[]{:S(2)}) copy-start(bf16[512,512]{1,0:T(8,128)(2,1)S(1)} %collective-permute-done.24.z_second) | copy-start | bytes 1572868
  466.5 10.9 %copy-start.20 = (bf16[512,512]{1,0:T(8,128)(2,1)}, bf16[512,512]{1,0:T(8,128)(2,1)S(1)}, u32[]{:S(2)}) copy-start(bf16[512,512]{1,0:T(8,128)(2,1)S(1)} %collective-permute-done.25.y_second) | copy-start | bytes 1572868
  467.7 52.4 %all-to-all-start.4 = ((bf16[8,128,384]{2,1,0:T(8,128)(2,1)}), bf16[8,128,384]{2,1,0:T(8,128)(2,1)S(1)}, u32[]{:S(2)}, u32[]{:S(2)}) async-start(bf16[8,128,384]{2,1,0:T(8,128)(2,1)} %bitcast.37), calls=%async_computation.6 | async-start | bytes 1572864 | tf_op jit(solution)/shard_map/all_to_all | solution.py:1329
  477.4 6.5 %copy-start.21 = (bf16[256,1024]{1,0:T(8,128)(2,1)}, bf16[256,1024]{1,0:T(8,128)(2,1)S(1)}, u32[]{:S(2)}) copy-start(bf16[256,1024]{1,0:T(8,128)(2,1)S(1)} %collective-permute-done.20.down_came) | copy-start | bytes 1572868
  477.4 7.2 %copy-start.23 = (bf16[128,1280]{1,0:T(8,128)(2,1)S(1)}, bf16[128,1280]{1,0:T(8,128)(2,1)}, u32[]{:S(2)}) copy-start(bf16[128,1280]{1,0:T(8,128)(2,1)} %reduce-scatter.5.cloned.1.call-done.mixed) | copy-start | bytes 983044
  484.6 11.6 %collective-permute-start.26 = (bf16[128,1280]{1,0:T(8,128)(2,1)S(1)}, bf16[128,1280]{1,0:T(8,128)(2,1)S(1)}, u32[]{:S(2)}, u32[]{:S(2)}) collective-permute-start(bf16[128,1280]{1,0:T(8,128)(2,1)S(1)} %copy-done.23), channel_id=1, source_target_pairs={{0,16},{8,24},{16,0},{24,8},{1,17},{9,25},{17,1},{25,9},{2,18},{10... | collective-permute-start | bytes 983048 | tf_op jit(solution)/shard_map/ppermute | solution.py:983
  485.7 6.5 %collective-permute-start.32 = (f32[16,1024]{1,0:T(8,128)S(1)}, f32[16,1024]{1,0:T(8,128)S(1)}, u32[]{:S(2)}, u32[]{:S(2)}) collective-permute-start(f32[16,1024]{1,0:T(8,128)S(1)} %maximum_maximum_fusion), channel_id=1, source_target_pairs={{0,16},{8,24},{16,0},{24,8},{1,17},{9,25},{17,1},{25,9},{2,18},{10... | collective-permute-start | bytes 196616 | tf_op jit(solution)/shard_map/ppermute | solution.py:983
  492.3 8.1 %collective-permute-start.33 = (f32[16,1024]{1,0:T(8,128)S(1)}, f32[16,1024]{1,0:T(8,128)S(1)}, u32[]{:S(2)}, u32[]{:S(2)}) collective-permute-start(f32[16,1024]{1,0:T(8,128)S(1)} %fusion.5), channel_id=1, source_target_pairs={{0,8},{8,0},{16,24},{24,16},{1,9},{9,1},{17,25},{25,17},{2,10},{10... | collective-permute-start | bytes 196616 | tf_op jit(solution)/shard_map/ppermute | solution.py:983
  496.3 24.1 %copy-start.24 = (bf16[128,1280]{1,0:T(8,128)(2,1)}, bf16[128,1280]{1,0:T(8,128)(2,1)S(1)}, u32[]{:S(2)}) copy-start(bf16[128,1280]{1,0:T(8,128)(2,1)S(1)} %collective-permute-done.26.mixed_x) | copy-start | bytes 983044
  496.3 40.1 %collective-permute-start.27 = (bf16[1,512,1024]{2,1,0:T(8,128)(2,1)}, bf16[1,512,1024]{2,1,0:T(8,128)(2,1)S(1)}, u32[]{:S(2)}, u32[]{:S(2)}) collective-permute-start(bf16[1,512,1024]{2,1,0:T(8,128)(2,1)} %bitcast.120), channel_id=1, source_target_pairs={{0,0},{1,1},{2,2},{3,3},{4,8},{5,9},{6,10},{7,11},{8,4},{9,5},{10,... | collective-permute-start | bytes 3145736 | tf_op jit(solution)/shard_map/ppermute | solution.py:998
  500.5 3.2 collective-permute-start.34
  503.7 10.2 %collective-permute-start.35 = (f32[16,1024]{1,0:T(8,128)S(1)}, f32[16,1024]{1,0:T(8,128)S(1)}, u32[]{:S(2)}, u32[]{:S(2)}) collective-permute-start(f32[16,1024]{1,0:T(8,128)S(1)} %add.108), channel_id=1, source_target_pairs={{0,2},{1,3},{2,0},{3,1},{4,6},{5,7},{6,4},{7,5},{8,10},{9,11},{10,... | collective-permute-start | bytes 196616 | tf_op jit(solution)/shard_map/ppermute | solution.py:988
  513.9 6.2 %collective-permute-start.36 = (f32[16,1024]{1,0:T(8,128)S(1)}, f32[16,1024]{1,0:T(8,128)S(1)}, u32[]{:S(2)}, u32[]{:S(2)}) collective-permute-start(f32[16,1024]{1,0:T(8,128)S(1)} %add.109), channel_id=1, source_target_pairs={{0,4},{1,5},{2,6},{3,7},{4,0},{5,1},{6,2},{7,3},{8,12},{9,13},{10,... | collective-permute-start | bytes 196616 | tf_op jit(solution)/shard_map/ppermute | solution.py:988
  513.9 15.7 %collective-permute-start.30 = (bf16[128,1280]{1,0:T(8,128)(2,1)S(1)}, bf16[128,1280]{1,0:T(8,128)(2,1)S(1)}, u32[]{:S(2)}, u32[]{:S(2)}) collective-permute-start(bf16[128,1280]{1,0:T(8,128)(2,1)S(1)} %copy-done.23), channel_id=1, source_target_pairs={{0,8},{8,0},{16,24},{24,16},{1,9},{9,1},{17,25},{25,17},{2,10},{10... | collective-permute-start | bytes 983048 | tf_op jit(solution)/shard_map/ppermute | solution.py:983
  517.5 12.2 %collective-permute-start.31 = (bf16[128,1280]{1,0:T(8,128)(2,1)S(1)}, bf16[128,1280]{1,0:T(8,128)(2,1)}, u32[]{:S(2)}, u32[]{:S(2)}) collective-permute-start(bf16[128,1280]{1,0:T(8,128)(2,1)S(1)} %collective-permute-done.26.mixed_x), channel_id=1, source_target_pairs={{0,8},{8,0},{16,24},{24,16},{1,9},{9,1},{17,25},{25,17},{2,10},{10... | collective-permute-start | bytes 983048 | tf_op jit(solution)/shard_map/ppermute | solution.py:983
  520.2 16.2 %copy-start.15 = (bf16[1,512,1024]{2,1,0:T(8,128)(2,1)S(1)}, bf16[1,512,1024]{2,1,0:T(8,128)(2,1)}, u32[]{:S(2)}) copy-start(bf16[1,512,1024]{2,1,0:T(8,128)(2,1)} %copy-done.14) | copy-start | bytes 3145732
  520.3 9.5 %copy-start.9 = (bf16[4,128,384]{2,1,0:T(8,128)(2,1)}, bf16[4,128,384]{2,1,0:T(8,128)(2,1)S(1)}, u32[]{:S(2)}) copy-start(bf16[4,128,384]{2,1,0:T(8,128)(2,1)S(1)} %fusion.heads) | copy-start | bytes 1179652
  520.4 9.5 %collective-permute-start.29 = (bf16[4,128,384]{2,1,0:T(8,128)(2,1)S(1)}, bf16[4,128,384]{2,1,0:T(8,128)(2,1)S(1)}, u32[]{:S(2)}, u32[]{:S(2)}) collective-permute-start(bf16[4,128,384]{2,1,0:T(8,128)(2,1)S(1)} %fusion.heads), channel_id=1, source_target_pairs={{0,8},{8,0},{16,24},{24,16},{1,9},{9,1},{17,25},{25,17},{2,10},{10... | collective-permute-start | bytes 1179656 | tf_op jit(solution)/shard_map/ppermute | solution.py:983
  (18 other events, 20.8 us)
Sparse Core Ops, SparseCore 0:
  74.1 154.3 all-gather.1
  280.4 101.7 reduce-scatter.2
  386.1 86.8 reduce-scatter.4

commit v3 on v2

--- a/solution.py
+++ b/solution.py
@@ -650,7 +650,7 @@
 
     keys = qkv[pl.ds(base, TILE), LANES : 2 * LANES]
     values = qkv[pl.ds(base, TILE), 2 * LANES : 3 * LANES]
-    head_keys = [head_lanes(keys, head) for head in range(2)]
+    turned_keys = jnp.transpose(keys)
     grad_kv[...] = jnp.zeros_like(grad_kv)
 
     def step(i, diagonal):
@@ -658,7 +658,6 @@
         scaled = qkv[pl.ds(at, TILE), 0:LANES]
         grads = grad[pl.ds(at, TILE), :]
         allowed = allowed_keys(column, base, row_starts(bounds, at), diagonal)
-        query_part = jnp.zeros((TILE, LANES), jnp.float32)
         key_part = grad_kv[0]
         value_part = grad_kv[1]
         for head in range(2):
@@ -672,10 +671,10 @@
             )
             value_part = value_part + dot_nn(probs.astype(jnp.bfloat16), head_grads)
             key_part = key_part + dot_nn(dscores, queries)
-            query_part = query_part + dot_tn(dscores, head_keys[head])
+            lanes = slice(head * HEAD_DIM, (head + 1) * HEAD_DIM)
+            grad_queries[lanes, pl.ds(at, TILE)] += dot_nn(turned_keys[lanes, :], dscores)
         grad_kv[0] = key_part
         grad_kv[1] = value_part
-        grad_queries[pl.ds(at, TILE), :] += query_part
 
     def later_step(i, carry):
         step(i, False)
@@ -687,7 +686,7 @@
     def store(target):
         at = pl.ds(pl.multiple_of((tile % 4) * TILE, TILE), TILE)
         target[at, 0:LANES] = (
-            grad_queries[pl.ds(base, TILE), :] * HEAD_DIM ** (-0.5)
+            jnp.transpose(grad_queries[:, pl.ds(base, TILE)]) * HEAD_DIM ** (-0.5)
         ).astype(jnp.bfloat16)
         target[at, LANES : 2 * LANES] = grad_kv[0].astype(jnp.bfloat16)
         target[at, 2 * LANES : 3 * LANES] = grad_kv[1].astype(jnp.bfloat16)
@@ -724,7 +723,7 @@
                 pltpu.VMEM((rows, 3 * LANES), jnp.bfloat16),
                 pltpu.VMEM((rows, LANES), jnp.bfloat16),
                 pltpu.VMEM((2, rows), jnp.float32),
-                pltpu.VMEM((rows, LANES), jnp.float32),
+                pltpu.VMEM((LANES, rows), jnp.float32),
                 pltpu.VMEM((2, TILE, LANES), jnp.float32),
                 pltpu.VMEM((rows, LANES), jnp.float32),
             ],
@@ -795,34 +794,42 @@
         result[...] = jnp.zeros_like(result)
         back[...] = jnp.zeros_like(back)
 
-    w_up = jnp.concatenate(
-        [up_a[...].reshape(width, LANES), up_b[...].reshape(width, LANES)], axis=1
-    )
-    w_down = jnp.concatenate(
-        [down_a[...].reshape(LANES, width), down_b[...].reshape(LANES, width)], axis=0
-    )
+    def weave(first, second, axis):
+        parts = []
+        for k in range(2):
+            for block in (first, second):
+                at = [slice(None), slice(None)]
+                at[axis] = slice(k * LANES, (k + 1) * LANES)
+                parts.append(block[tuple(at)])
+        return jnp.concatenate(parts, axis=axis)
+
+    wide_step = 2 * LANES
+    w_up = weave(up_a[...].reshape(width, wide_step), up_b[...].reshape(width, wide_step), 1)
+    w_down = weave(down_a[...].reshape(wide_step, width), down_b[...].reshape(wide_step, width), 0)
     shift = jnp.where(
         core == 0,
-        jnp.concatenate([vectors[6:7, :], vectors[7:8, :]], axis=1),
-        jnp.concatenate([vectors[8:9, :], vectors[9:10, :]], axis=1),
-    )
-    bias = jnp.zeros((1, 2 * LANES), jnp.float32)
-    for side, (normed, grad) in enumerate(((normed_own, grad_own), (normed_came, grad_came))):
-        value = dot_nn(normed[...], w_up) + shift
+        weave(vectors[6:7, :], vectors[7:8, :], 1),
+        weave(vectors[8:9, :], vectors[9:10, :], 1),
+    )
+    sides = ((normed_own, grad_own), (normed_came, grad_came))
+    values = [dot_nn(normed[...], w_up) + shift for normed, _ in sides]
+    slopes = [dot_nt(grad[...], w_down) for _, grad in sides]
+    bias = jnp.zeros((1, 4 * LANES), jnp.float32)
+    for side, (value, slope) in enumerate(zip(values, slopes)):
         half = 0.5 + 0.5 * lax.erf(value * 0.7071067811865476)
         bell = jnp.exp(-0.5 * value * value) * 0.3989422804014327
         activated = (value * half).astype(jnp.bfloat16)
+        change = (slope * (half + value * bell)).astype(jnp.bfloat16)
         act[side] = activated
-        change = dot_nt(grad[...], w_down) * (half + value * bell)
-        bias = bias + jnp.sum(change.astype(jnp.bfloat16).astype(jnp.float32), axis=0, keepdims=True)
-        change = change.astype(jnp.bfloat16)
         grad_up[side] = change
+        bias = bias + jnp.sum(change.astype(jnp.float32), axis=0, keepdims=True)
         result[side] += dot_nn(activated, w_down)
         back[side] += dot_nt(change, w_up)
-    up_bias[0:1, :] = bias[:, 0:LANES]
-    up_bias[1:2, :] = bias[:, LANES:]
-
-    @pl.when(step == 7)
+    for k in range(4):
+        at = slice((k // 2) * LANES, (k // 2 + 1) * LANES)
+        up_bias[k % 2 : k % 2 + 1, at] = bias[:, k * LANES : (k + 1) * LANES]
+
+    @pl.when(step == 3)
     def _():
         result_own[...] = result[0]
         result_came[...] = result[1].astype(jnp.bfloat16)
@@ -887,7 +894,17 @@
 
 
 def back_project_kernel(
-    ids, own, came, w_own, w_other, first, y_out, z_out, keep_left, keep_right, grads
+    ids,
+    own,
+    came,
+    w_own,
+    w_other,
+    first,
+    y_out,
+    z_out,
+    keep_left,
+    keep_right,
+    grads,
 ):
     square = ids[SQUARE]
     size, width = first.shape
@@ -905,15 +922,39 @@
     z_out[1] = grads[square ^ 3, :, half:].astype(jnp.bfloat16)
 
 
+def first_sums_kernel(
+    ids, first, y_out, z_out, keep_left, keep_right, natural, vectors, sums
+):
+    square = ids[SQUARE]
+    half = first.shape[1] // 2
+    wide = jnp.float32
+    parts = (
+        (first[:, :half], first[:, half:]),
+        (y_out[0].astype(wide), keep_right[...]),
+        (keep_left[...], z_out[0].astype(wide)),
+        (y_out[1].astype(wide), z_out[1].astype(wide)),
+    )
+
+    @pl.when(pl.program_id(0) == 0)
+    def _():
+        sums[...] = jnp.zeros_like(sums)
+
+    for j in range(4):
+        for side in range(2):
+            lanes = slice(side * half, (side + 1) * half)
+            value = parts[j][side]
+            rows = natural[square ^ j, :, lanes].astype(wide)
+            normed = (rows - vectors[1:2, lanes]) / vectors[0:1, lanes]
+            sums[0:1, lanes] += jnp.sum(value * normed, axis=0, keepdims=True)
+            sums[1:2, lanes] += jnp.sum(value, axis=0, keepdims=True)
+
+
 def second_kernel(ids, keep_left, keep_right, y_came, z_came, z_out, y_out):
     z_out[...] = (keep_left[...] + y_came[1].astype(jnp.float32)).astype(jnp.bfloat16)
     y_out[...] = (keep_right[...] + z_came[1].astype(jnp.float32)).astype(jnp.bfloat16)
 
 
-def last_kernel(
-    ids, first, y_came, z_came, z_second, y_second, tokens, grad_middle, vectors, out, sums
-):
-    step = pl.program_id(0)
+def last_kernel(ids, first, y_came, z_came, z_second, y_second, tokens, grad_middle, vectors, out):
     wide = jnp.float32
     left = y_came[0].astype(wide) + z_second[...].astype(wide)
     right = z_came[0].astype(wide) + y_second[...].astype(wide)
@@ -923,17 +964,9 @@
         jnp.bfloat16
     )
 
-    @pl.when(step == 0)
-    def _():
-        sums[...] = jnp.zeros_like(sums)
-
-    sums[0:1, :] += jnp.sum(grad * xhat, axis=0, keepdims=True)
-    sums[1:2, :] += jnp.sum(grad, axis=0, keepdims=True)
-
-
-def grad_heads_kernel(ids, normed, own, came, out, leaving):
-    out[...] = dot_tn(normed[...], own[...]).astype(jnp.bfloat16)
-    leaving[...] = dot_tn(normed[...], came[...]).astype(jnp.bfloat16)
+
+def grad_heads_kernel(ids, normed, grads, out):
+    out[...] = dot_tn(normed[...], grads[...]).astype(jnp.bfloat16)
 
 
 def spread_kernel(
@@ -1047,6 +1080,8 @@
     deep = bundle.shape[0]
 
     tokens_here = swap_halves(tokens[0])
+    heads = lax.dynamic_slice_in_dim(w_qkv.reshape(part, 3, 8, LANES), 4 * core, 4, 2)
+    heads = heads.transpose(2, 0, 1, 3).reshape(4, part, 3 * LANES)
     small = jnp.concatenate(
         [
             jnp.stack([ln1_gain, ln1_bias, ln2_gain, ln2_bias, out_bias, down_bias]),
@@ -1055,15 +1090,11 @@
         ],
         axis=0,
     )
-    small = lax.all_to_all(
-        jnp.broadcast_to(small[None], (8, 16, part)), "seq", 0, 0, tiled=True
-    )
-    vectors = small.astype(wide).transpose(1, 0, 2).reshape(16, width)
-
-    heads = lax.dynamic_slice_in_dim(w_qkv.reshape(part, 3, 8, LANES), 4 * core, 4, 2)
-    heads = heads.transpose(2, 0, 1, 3).reshape(4, part, 3 * LANES)
-    heads = after(jnp.concatenate([heads, heads], axis=0), small)
-    w_heads = lax.all_to_all(heads, "seq", 0, 0, tiled=True).reshape(width, 3 * LANES)
+    small = jnp.broadcast_to(jnp.pad(small, ((0, 0), (0, 2 * part)))[None], (4, 16, 3 * part))
+    heads = jnp.concatenate([heads, small], axis=1)
+    came = lax.all_to_all(jnp.concatenate([heads, heads], axis=0), "seq", 0, 0, tiled=True)
+    vectors = came[:, part:, :part].astype(wide).transpose(1, 0, 2).reshape(16, width)
+    w_heads = came[:, :part].reshape(width, 3 * LANES)
     w_other = hop_batch(w_heads, 1)
 
     meta = jnp.concatenate([key_mask[0], jnp.pad(lengths[0], (0, LANES - lengths.shape[1]))])
@@ -1085,7 +1116,7 @@
     )(ids, tokens_here, vectors)
     y_one = hop_seq(normed_one, 1)
     z_one = hop_seq(normed_one, 2)
-    bundle = lax.all_gather(after(bundle, normed_one, w_heads), ("seq", "batch"), axis=0, tiled=True)
+    bundle = lax.all_gather(after(bundle, tokens_here, came), ("seq", "batch"), axis=0, tiled=True)
     bundle = bundle.reshape(8, 4, deep, width)
     half = frames // 2
     top, bottom = hop_seq(y_one[:half], 2), hop_seq(z_one[half:], 1)
@@ -1131,23 +1162,23 @@
     normed_two_came = hop_batch(normed_two, 1)
 
     up_specs = [
-        pl.BlockSpec((8, 1, part, LANES), lambda s, ids, k=k: (0, 2 * k + ids[CORE], 1, s))
+        pl.BlockSpec((8, 1, part, 2 * LANES), lambda s, ids, k=k: (0, 2 * k + ids[CORE], 1, s))
         for k in range(2)
     ]
     down_specs = [
-        pl.BlockSpec((1, 1, part, width), lambda s, ids, k=k: (s, 2 * k + ids[CORE], 0, 0))
+        pl.BlockSpec((2, 1, part, width), lambda s, ids, k=k: (s, 2 * k + ids[CORE], 0, 0))
         for k in range(2)
     ]
-    hidden = pl.BlockSpec((2, frames, 2 * LANES), lambda s, *_: (0, 0, s))
+    hidden = pl.BlockSpec((2, frames, 4 * LANES), lambda s, *_: (0, 0, s))
     act, grad_up, up_sums, result_own, result_leaving, back_own, back_leaving = call(
         forward_kernel,
         "feed_forward",
-        8,
+        4,
         [whole(frames, width)] * 4
         + up_specs
         + down_specs
-        + [pl.BlockSpec((16, LANES), lambda s, *_: (0, s))],
-        [hidden, hidden, pl.BlockSpec((8, LANES), lambda s, *_: (0, s))]
+        + [pl.BlockSpec((16, 2 * LANES), lambda s, *_: (0, s))],
+        [hidden, hidden, pl.BlockSpec((8, 2 * LANES), lambda s, *_: (0, s))]
         + [whole(frames, width)] * 4,
         (
             like((2, frames, 2 * width), low),
@@ -1213,7 +1244,7 @@
         [column, whole(frames, width)],
         [split_spec, split_spec],
         (split, split),
-        flops=2 * frames * width * width,
+        flops=frames * width,
     )(ids, attended, grad_branch)
     out_came = hop_batch(out_leaving, 1)
     broad = like((8, part, width + width // 4), low)
@@ -1225,7 +1256,7 @@
         [column, column, whole(2, frames, 2 * width), split_spec, split_spec],
         [broad_spec, broad_spec],
         (broad, broad),
-        flops=2 * 2 * frames * width * 2 * width,
+        flops=frames * width,
     )(ids, normed_two, normed_two_came, grad_up, out_kept, out_came)
     up_came = hop_batch(up_leaving, 2)
 
@@ -1283,17 +1314,45 @@
     )
     y_came, z_came = hop_seq(y_out, 1), hop_seq(z_out, 2)
 
+    first_sums = call(
+        first_sums_kernel,
+        "first_sums",
+        4,
+        [slab, pair_spec, pair_spec, half_spec, half_spec, natural_slab, whole(16, width)],
+        whole(8, width),
+        like((8, width), wide),
+    )(
+        ids,
+        first,
+        y_out,
+        z_out,
+        keep_left,
+        keep_right,
+        natural.reshape(4, frames, width),
+        vectors,
+    )
+    y_came = after(y_came, first_sums)
+    ups = jnp.zeros((4, width), wide)
+    ups = lax.dynamic_update_slice(ups, up_sums[:2], (2 * core, 0))
+    sums = jnp.concatenate([first_sums[:2], middle_sums[:4], ups, jnp.zeros((6, width), wide)])
+    sums = sums.reshape(16, 8, 1, part).transpose(1, 2, 0, 3)
+    sums = jnp.broadcast_to(sums, (8, 4, 16, part)).reshape(32, 16, part)
+
     heads_out = like((width, 3 * LANES), low)
-    heads_kept, heads_leaving = call(
+    grad_heads = call(
         grad_heads_kernel,
         "grad_heads",
         2,
-        [pl.BlockSpec((4 * frames, 4 * part), lambda i, *_: (0, i))]
-        + [whole(4 * frames, 3 * LANES)] * 2,
-        [pl.BlockSpec((4 * part, 3 * LANES), lambda i, *_: (i, 0))] * 2,
-        (heads_out, heads_out),
-        flops=2 * 4 * frames * width * 6 * LANES,
-    )(ids, after(natural, z_out), grad_qkv, grad_qkv_came)
+        [
+            pl.BlockSpec((4 * frames, 4 * part), lambda i, *_: (0, i)),
+            whole(4 * frames, 3 * LANES),
+        ],
+        pl.BlockSpec((4 * part, 3 * LANES), lambda i, *_: (i, 0)),
+        like((width, 3 * LANES), low),
+        flops=2 * 4 * frames * width * 3 * LANES,
+    )
+    heads_leaving = grad_heads(ids, after(natural, z_out), grad_qkv_came)
+    heads_kept = grad_heads(ids, after(natural, z_out), grad_qkv)
     heads_came = hop_batch(heads_leaving, 1)
     heads_sum = (heads_kept.astype(wide) + heads_came.astype(wide)).astype(low)
     heads_came = hop_batch(heads_sum, 2)
@@ -1312,16 +1371,18 @@
         (like(pair[1:], low), like(pair[1:], low)),
     )(ids, keep_left, keep_right, y_came, z_came)
     z_last, y_last = hop_seq(z_second, 2), hop_seq(y_second, 1)
-    grad_inputs, last_sums = call(
+    sums = lax.all_to_all(after(sums, z_second), ("seq", "batch"), 0, 0, tiled=True)
+    sums = jnp.sum(sums, axis=0)
+    grad_inputs = call(
         last_kernel,
         "last",
         4,
         [slab, pair_spec, pair_spec, half_spec, half_spec, slab, slab, whole(16, width)],
-        [slab, whole(8, width)],
-        (like((frames, width), low), like((8, width), wide)),
-    )(ids, after(first, down_came, mixed), y_came, z_came, z_last, y_last, tokens_here, grad_middle, vectors)
+        slab,
+        like((frames, width), low),
+    )(ids, after(first, mixed, sums), y_came, z_came, z_last, y_last, tokens_here, grad_middle, vectors)
     mixed_x = hop_batch(mixed, 2)
-    grad_inputs = swap_halves(after(grad_inputs, mixed_x)[None])
+    grad_inputs = swap_halves(grad_inputs[None])
 
     heads_sum = (
         after(heads_sum, z_last, y_last).astype(wide) + heads_came.astype(wide)
@@ -1353,15 +1414,7 @@
         ),
     )(ids, heads_sum, heads_came, down, down_came, mixed, mixed_x, mixed_core, mixed_both)
 
-    ups = jnp.zeros((4, width), wide)
-    ups = lax.dynamic_update_slice(ups, up_sums[:2], (2 * core, 0))
-    sums = jnp.concatenate([last_sums[:2], middle_sums[:4], ups, jnp.zeros((6, width), wide)])
-    sums = sums + hop_batch(sums, 2)
-    sums = sums + hop_batch(sums, 1)
-    sums = after(sums, mixed_x)
-    for bits in (1, 2, 4):
-        sums = sums + hop_seq(sums, bits)
-    sums = lax.dynamic_slice_in_dim(sums, seq_index * part, part, 1)
+    grad_inputs = after(grad_inputs, grad_qkv_w)
     return (
         result_home,
         grad_inputs,

time: 547 us -> 522 us (0.954)
  starting transfers between devices: 84.6 us -> 58.9 us
    ppermute x22 -> x20, starting transfers between devices: 27.5 us -> 11.2 us  [hop_batch(): return lax.ppermute(block, 'batch', [(i, i ^ bit) for i in range(size)])]
    ppermute x11 -> x8, waiting for transfers between devices: 109 us -> 93.6 us  [hop_seq(): return lax.ppermute(block, 'seq', [(i, i ^ bits) for i in range(size)])]
    ppermute x22 -> x20, waiting for transfers between devices: 30.4 us -> 18.2 us  [hop_batch(): return lax.ppermute(block, 'batch', [(i, i ^ bit) for i in range(size)])]
    all_to_all x1, waiting for transfers between devices: 0.01 us -> 9.88 us  [square_shards(): lax.all_to_all(heads_sum.reshape(8, part, 3 * LANES), 'seq', 0, 0, tiled=...]
    ppermute x4, waiting for transfers between devices: 28.4 us -> 37.2 us  [swap_halves(): return lax.ppermute(block, ('batch', 'seq'), route)]
    pallas_call x13 -> x15, Pallas kernels: 117 us -> 124 us  [run(): pl.pallas_call(kernel, out_shape=out_shape, grid_spec=pltpu.PrefetchScala...]
    unnamed x78 -> x70, local copies, waits for them, and re-layouts: 18.2 us -> 13.5 us
  transfers between devices with their start and end apart: 45 -> 40, of which waited for: 23 -> 21; matrix products, arithmetic and copies ran while one was open for 5% -> 5% of each run, Pallas kernels for 25% -> 28%
where the time goes in v3:
time: 522 us; the launch traced here: 520 us
  waiting for transfers between devices  220 us (42%)
  Pallas kernels  182 us (35%)
  starting transfers between devices  58.9 us (11%)
  local copies, waits for them, and re-layouts  27.6 us (5%)
  other arithmetic  16.8 us (3%)
  between operations  14.3 us (3%)
    pallas_call x15, Pallas kernels, run(): pl.pallas_call(kernel, out_shape=out_shape, grid_spec=pltpu.PrefetchScala...  124 us
    ppermute x8, waiting for transfers between devices, hop_seq(): return lax.ppermute(block, 'seq', [(i, i ^ bits) for i in range(size)])  93.6 us
    all_to_all x2, waiting for transfers between devices, trade(): lax.all_to_all(block, 'seq', 0, 0, tiled=True, axis_index_groups=groups)  53.1 us
    ppermute x4, waiting for transfers between devices, swap_halves(): return lax.ppermute(block, ('batch', 'seq'), route)  37.2 us
    pallas_call x1, Pallas kernels, attend_back(): pl.pallas_call(attend_back_kernel, out_shape=(like(own.shape, jnp.bfloat1...  34.9 us
    pallas_call x1, Pallas kernels, attend(): pl.pallas_call(attend_kernel, out_shape=(like((8, TILE, LANES), jnp.bfloa...  23.1 us
    ppermute x4, starting transfers between devices, swap_halves(): return lax.ppermute(block, ('batch', 'seq'), route)  18.5 us
    ppermute x20, waiting for transfers between devices, hop_batch(): return lax.ppermute(block, 'batch', [(i, i ^ bit) for i in range(size)])  18.2 us
  transfers between devices with their start and end apart: 40, of which 21 were waited for; matrix products, arithmetic and copies ran while one was open for 5% of the time, Pallas kernels for 28%

profile of v3, /device:TPU:1, one launch (start us, length us, event | category | flops | bytes accessed | tf_op | source)
XLA Modules:
  0.0 519.9 jit_solution(18135935175945400484)
XLA Ops:
  7.2 1.7 concatenate.19
  9.0 1.5 copy.71
  10.8 1.4 copy.74
  12.3 6.4 %all-to-all-start = ((bf16[8,144,384]{2,1,0:T(8,128)(2,1)}), bf16[8,144,384]{2,1,0:T(8,128)(2,1)S(1)}, u32[]{:S(2)}, u32[]{:S(2)}) async-start(bf16[8,144,384]{2,1,0:T(8,128)(2,1)} %copy.74), calls=%async_computation | async-start | bytes 1769472 | tf_op jit(solution)/shard_map/all_to_all | solution.py:1095
  18.7 5.3 %collective-permute-start.1 = (bf16[512,1024]{1,0:T(8,128)(2,1)}, bf16[512,1024]{1,0:T(8,128)(2,1)S(1)}, u32[]{:S(2)}, u32[]{:S(2)}) collective-permute-start(bf16[512,1024]{1,0:T(8,128)(2,1)} %bitcast.134), channel_id=1, source_target_pairs={{0,0},{1,1},{2,2},{3,3},{4,8},{5,9},{6,10},{7,11},{8,4},{9,5},{10,... | collective-permute-start | bytes 3145736 | tf_op jit(solution)/shard_map/ppermute | solution.py:1031
  24.1 2.6 reshape.158
  26.6 2.8 dynamic-slice_reduce_fusion
  31.2 32.6 %collective-permute-done.1.tokens = bf16[512,1024]{1,0:T(8,128)(2,1)S(1)} collective-permute-done((bf16[512,1024]{1,0:T(8,128)(2,1)}, bf16[512,1024]{1,0:T(8,128)(2,1)S(1)}, u32[]{:S(2)}, u32[]{:S(2)}) %collective-permute-start.1) | collective-permute-done | bytes 1048608 | tf_op jit(solution)/shard_map/ppermute | solution.py:1031
  65.3 4.5 norm.1.own
  72.1 32.3 %collective-permute-done.3.z_one = bf16[512,1024]{1,0:T(8,128)(2,1)S(1)} collective-permute-done((bf16[512,1024]{1,0:T(8,128)(2,1)}, bf16[512,1024]{1,0:T(8,128)(2,1)S(1)}, u32[]{:S(2)}, u32[]{:S(2)}) %collective-permute-start.3) | collective-permute-done | bytes 1048608 | tf_op jit(solution)/shard_map/ppermute | solution.py:1021
  104.5 1.1 collective-permute-start.5
  107.2 13.4 %collective-permute-done.5.bottom = bf16[256,1024]{1,0:T(8,128)(2,1)} collective-permute-done((bf16[256,1024]{1,0:T(8,128)(2,1)S(1)}, bf16[256,1024]{1,0:T(8,128)(2,1)}, u32[]{:S(2)}, u32[]{:S(2)}) %collective-permute-start.5) | collective-permute-done | bytes 524320 | tf_op jit(solution)/shard_map/ppermute | solution.py:1021
  120.7 16.9 %collective-permute-done.4.top = bf16[256,1024]{1,0:T(8,128)(2,1)} collective-permute-done((bf16[256,1024]{1,0:T(8,128)(2,1)S(1)}, bf16[256,1024]{1,0:T(8,128)(2,1)}, u32[]{:S(2)}, u32[]{:S(2)}) %collective-permute-start.4) | collective-permute-done | bytes 524320 | tf_op jit(solution)/shard_map/ppermute | solution.py:1021
  137.5 9.9 %project.1 = (bf16[4,512,384]{2,1,0:T(8,128)(2,1)}, bf16[4,512,384]{2,1,0:T(8,128)(2,1)}, bf16[4,512,1024]{2,1,0:T(8,128)(2,1)}) custom-call(s32[4]{0:T(128)} %pad_add_fusion.2.ids, bf16[512,1024]{1,0:T(8,128)(2,1)} %norm.1.own, bf16[512,1024]{1,0:T(8,128)(2,1)} %collective-permute-done.2.y_one, bf16[512,1024]{1,0:T(8,128)(2,1)} %copy-done.24, ...), custom_call_target="tpu_custom_call" | custom-call | flops 3221225472 | bytes 11534336 | tf_op jit(solution)/shard_map/project/pallas_call | solution.py:429
  148.9 2.8 collective-permute-done.7
  151.8 1.2 copy-done.28
  152.9 23.1 %attend.1 = (bf16[8,512,128]{2,1,0:T(8,128)(2,1)}, f32[2,4096]{1,0:T(2,128)}) custom-call(s32[4]{0:T(128)} %pad_add_fusion.2.ids, s32[3,8]{1,0:T(4,128)} %pad_add_fusion.1.bounds, bf16[2048,384]{1,0:T(8,128)(2,1)} %bitcast.136, bf16[2048,384]{1,0:T(8,128)(2,1)} %bitcast.132, f32[1,4096]{1,0:T(1,128)} %fusion.2.places_row), custom_call_target="tpu_custom_call" | custom-call | flops 4294967296 | bytes 9830400 | tf_op jit(solution)/shard_map/attend/pallas_call | solution.py:578
  176.1 3.6 all-to-all-start.1
  179.8 4.9 collective-permute-start.10
  184.7 36.5 %all-to-all-done.1.own = bf16[8,512,128]{2,1,0:T(8,128)(2,1)S(1)} async-done(((bf16[8,512,128]{2,1,0:T(8,128)(2,1)}), bf16[8,512,128]{2,1,0:T(8,128)(2,1)S(1)}, u32[]{:S(2)}, u32[]{:S(2)}) %all-to-all-start.1) | async-done | bytes 1048608 | tf_op jit(solution)/shard_map/all_to_all | solution.py:1039
  221.7 2.9 collective-permute-done.8.came
  224.6 5.7 %out_project.1 = (bf16[512,1024]{1,0:T(8,128)(2,1)}, f32[512,1024]{1,0:T(8,128)}, bf16[512,1024]{1,0:T(8,128)(2,1)}) custom-call(s32[4]{0:T(128)} %pad_add_fusion.2.ids, bf16[8,512,128]{2,1,0:T(8,128)(2,1)} %copy-done.8, bf16[8,512,128]{2,1,0:T(8,128)(2,1)} %collective-permute-done.8.came, bf16[512,1024]{1,0:T(8,128)(2,1)} %copy-done.2, ...), custom_call_target="tpu_custom_call" | custom-call | flops 1073741824 | bytes 44171264 | tf_op jit(solution)/shard_map/out_project/pallas_call | solution.py:429
  230.7 2.5 collective-permute-done.9.normed_came
  234.2 26.8 %feed_forward.1 = (bf16[2,512,2048]{2,1,0:T(8,128)(2,1)}, bf16[2,512,2048]{2,1,0:T(8,128)(2,1)}, f32[8,1024]{1,0:T(8,128)}, f32[512,1024]{1,0:T(8,128)}, bf16[51...) custom-call(s32[4]{0:T(128)} %pad_add_fusion.2.ids, ...), custom_call_target="tpu_custom_call" | custom-call | flops 17179869184 | bytes 159514624 | tf_op jit(solution)/shard_map/feed_forward/pallas_call | solution.py:429
  261.0 9.1 %grad_down.1 = bf16[2048,1024]{1,0:T(8,128)(2,1)} custom-call(s32[4]{0:T(128)} %pad_add_fusion.2.ids, bf16[2,512,2048]{2,1,0:T(8,128)(2,1)} %get-tuple-element.73.act, bf16[512,1024]{1,0:T(8,128)(2,1)} %copy-done.4, bf16[512,1024]{1,0:T(8,128)(2,1)} %copy-done.13), custom_call_target="tpu_custom_call" | custom-call | flops 4294967296 | bytes 12582912 | tf_op jit(solution)/shard_map/grad_down/pallas_call | solution.py:429
  270.1 1.2 copy-done.31
  271.7 2.3 collective-permute-done.14.back_came
  275.0 8.2 %middle_back.1 = (f32[512,1024]{1,0:T(8,128)}, bf16[512,1024]{1,0:T(8,128)(2,1)}, bf16[8,512,128]{2,1,0:T(8,128)(2,1)}, f32[8,1024]{1,0:T(8,128)}) custom-call(s32[4]{0:T(128)} %pad_add_fusion.2.ids, f32[512,1024]{1,0:T(8,128)} %get-tuple-element.74.back_own, bf16[512,1024]{1,0:T(8,128)(2,1)} %copy-done.15, f32[512,1024]{1,0:T(8,128)} %get-tuple-element.67.middle, ...), custom_call_target="tpu_custom_call" | custom-call | flops 1073741824 | bytes 50462720 | tf_op jit(solution)/shard_map/middle_back/pallas_call | solution.py:429
  283.2 4.6 grad_out.1
  288.1 4.3 all-to-all-start.2
  293.4 11.1 %grad_up.1 = (bf16[8,128,1280]{2,1,0:T(8,128)(2,1)}, bf16[8,128,1280]{2,1,0:T(8,128)(2,1)}) custom-call(s32[4]{0:T(128)} %pad_add_fusion.2.ids, bf16[512,1024]{1,0:T(8,128)(2,1)} %get-tuple-element.68.normed_own, bf16[512,1024]{1,0:T(8,128)(2,1)} %copy-done.5, bf16[2,512,2048]{2,1,0:T(8,128)(2,1)} %get-tuple-element.77.grad_up, ...), custom_call_target="tpu_custom_call" | custom-call | flops 524288 | bytes 16777216 | tf_op jit(solution)/shard_map/grad_up/pallas_call | solution.py:429
  304.5 1.3 collective-permute-start.17
  306.2 16.6 %all-to-all-done.2.grad_own = bf16[8,512,128]{2,1,0:T(8,128)(2,1)} async-done(((bf16[8,512,128]{2,1,0:T(8,128)(2,1)}), bf16[8,512,128]{2,1,0:T(8,128)(2,1)}, u32[]{:S(2)}, u32[]{:S(2)}) %all-to-all-start.2) | async-done | bytes 1048608 | tf_op jit(solution)/shard_map/all_to_all | solution.py:1039
  323.5 2.3 add_convert_fusion.1
  325.7 2.5 collective-permute-start.13
  329.3 34.9 %attend_back.1 = (bf16[2048,384]{1,0:T(8,128)(2,1)}, bf16[2048,384]{1,0:T(8,128)(2,1)}) custom-call(s32[4]{0:T(128)} %pad_add_fusion.2.ids, s32[3,8]{1,0:T(4,128)} %pad_add_fusion.1.bounds, bf16[2048,384]{1,0:T(8,128)(2,1)} %bitcast.137, bf16[2048,384]{1,0:T(8,128)(2,1)} %bitcast.133, bf16[8,512,128]{2,1,0:T(8,128)(2,1)} %all-to-all-done.2.grad_own, ...), custom_call_target="tpu_custom_call" | custom-call | flops 10737418240 | bytes 9830400 | tf_op jit(solution)/shard_map/attend_back/pallas_call | solution.py:706
  364.2 2.3 collective-permute-done.13
  366.5 4.2 add_convert_fusion
  370.8 1.1 copy-done.11
  371.9 9.4 %back_project.1 = (f32[512,1024]{1,0:T(8,128)}, bf16[2,512,512]{2,1,0:T(8,128)(2,1)}, bf16[2,512,512]{2,1,0:T(8,128)(2,1)}, f32[512,512]{1,0:T(8,128)}, f32[512,512]{1,0:T(8,128)}) custom-call(s32[4]{0:T(128)} %pad_add_fusion.2.ids, bf16[4,512,384]{2,1,0:T(8,128)(2,1)} %bitcast.107, bf16[4,512,384]{2,1,0:T(8,128)(2,1)} %bitcast.108, ...), custom_call_target="tpu_custom_call" | custom-call | flops 3221225472 | bytes 9437184 | tf_op jit(solution)/shard_map/back_project/pallas_call | solution.py:429
  381.4 6.0 %grad_heads.3 = bf16[1024,384]{1,0:T(8,128)(2,1)} custom-call(s32[4]{0:T(128)} %pad_add_fusion.2.ids, bf16[2048,1024]{1,0:T(8,128)(2,1)} %bitcast.96, bf16[2048,384]{1,0:T(8,128)(2,1)} %copy-done.11), custom_call_target="tpu_custom_call" | custom-call | flops 1610612736 | bytes 11534336 | tf_op jit(solution)/shard_map/grad_heads/pallas_call | solution.py:429
  387.5 2.5 collective-permute-start.19
  390.1 3.1 collective-permute-start.21
  393.2 7.2 %first_sums.1 = f32[8,1024]{1,0:T(8,128)} custom-call(s32[4]{0:T(128)} %pad_add_fusion.2.ids, f32[512,1024]{1,0:T(8,128)} %get-tuple-element.104.first, bf16[2,512,512]{2,1,0:T(8,128)(2,1)} %get-tuple-element.91.y_out, bf16[2,512,512]{2,1,0:T(8,128)(2,1)} %get-tuple-element.92.z_out, f32[512,512]{1,0:T(8,128)} %get-tuple-element.93.keep_left, ...), custom_call_target="tpu_custom_call" | custom-call | bytes 21102592 | tf_op jit(solution)/shard_map/first_sums/pallas_call | solution.py:429
  400.5 6.0 %grad_heads.2 = bf16[1024,384]{1,0:T(8,128)(2,1)} custom-call(s32[4]{0:T(128)} %pad_add_fusion.2.ids, bf16[2048,1024]{1,0:T(8,128)(2,1)} %bitcast.97, bf16[2048,384]{1,0:T(8,128)(2,1)} %get-tuple-element.85.grads), custom_call_target="tpu_custom_call" | custom-call | flops 1610612736 | bytes 11534336 | tf_op jit(solution)/shard_map/grad_heads/pallas_call | solution.py:429
  406.5 1.6 add_convert_fusion.3
  408.3 8.7 %collective-permute-done.19.y_came = bf16[2,512,512]{2,1,0:T(8,128)(2,1)S(1)} collective-permute-done((bf16[2,512,512]{2,1,0:T(8,128)(2,1)}, bf16[2,512,512]{2,1,0:T(8,128)(2,1)S(1)}, u32[]{:S(2)}, u32[]{:S(2)}) %collective-permute-start.19) | collective-permute-done | bytes 1048608 | tf_op jit(solution)/shard_map/ppermute | solution.py:1021
  417.0 2.4 add_convert_fusion.4.down
  419.5 11.1 %collective-permute-done.22.z_came = bf16[2,512,512]{2,1,0:T(8,128)(2,1)S(1)} collective-permute-done((bf16[2,512,512]{2,1,0:T(8,128)(2,1)}, bf16[2,512,512]{2,1,0:T(8,128)(2,1)S(1)}, u32[]{:S(2)}, u32[]{:S(2)}) %collective-permute-start.22) | collective-permute-done | bytes 1048608 | tf_op jit(solution)/shard_map/ppermute | solution.py:1021
  431.5 3.9 second.1
  435.4 1.4 collective-permute-start.24
  438.4 5.1 all-to-all-start.3
  443.5 6.3 %collective-permute-done.24.y_second = bf16[512,512]{1,0:T(8,128)(2,1)S(1)} collective-permute-done((bf16[512,512]{1,0:T(8,128)(2,1)}, bf16[512,512]{1,0:T(8,128)(2,1)S(1)}, u32[]{:S(2)}, u32[]{:S(2)}) %collective-permute-start.24) | collective-permute-done | bytes 524320 | tf_op jit(solution)/shard_map/ppermute | solution.py:1021
  449.8 4.9 collective-permute-done.23.z_second
  454.7 2.4 add_convert_fusion.2
  457.1 7.8 %all-to-all-done.3 = f32[32,16,128]{2,1,0:T(8,128)S(1)} async-done(((f32[32,16,128]{2,1,0:T(8,128)}), f32[32,16,128]{2,1,0:T(8,128)S(1)}, u32[]{:S(2)}, u32[]{:S(2)}) %all-to-all-start.3) | async-done | bytes 262176 | tf_op jit(solution)/shard_map/all_to_all | solution.py:1374
  465.0 3.5 all-to-all-start.4
  468.6 6.4 %last.1 = bf16[512,1024]{1,0:T(8,128)(2,1)} custom-call(s32[4]{0:T(128)} %pad_add_fusion.2.ids, f32[512,1024]{1,0:T(8,128)} %get-tuple-element.104.first, bf16[2,512,512]{2,1,0:T(8,128)(2,1)} %copy-done.6, bf16[2,512,512]{2,1,0:T(8,128)(2,1)} %copy-done.7, bf16[512,512]{1,0:T(8,128)(2,1)} %copy-done.21, bf16[512,512]{1,0:T(8,128)(2,1)} %copy-done.20, ...), custom_call_target="tpu_custom_call" | custom-call | bytes 16908288 | tf_op jit(solution)/shard_map/last/pallas_call | solution.py:429
  475.0 5.8 %collective-permute-start.25 = (bf16[1,512,1024]{2,1,0:T(8,128)(2,1)}, bf16[1,512,1024]{2,1,0:T(8,128)(2,1)S(1)}, u32[]{:S(2)}, u32[]{:S(2)}) collective-permute-start(bf16[1,512,1024]{2,1,0:T(8,128)(2,1)} %bitcast.109), channel_id=1, source_target_pairs={{0,0},{1,1},{2,2},{3,3},{4,8},{5,9},{6,10},{7,11},{8,4},{9,5},{10,... | collective-permute-start | bytes 3145736 | tf_op jit(solution)/shard_map/ppermute | solution.py:1031
  481.5 7.0 %collective-permute-done.29.mixed_x = bf16[128,1280]{1,0:T(8,128)(2,1)} collective-permute-done((bf16[128,1280]{1,0:T(8,128)(2,1)}, bf16[128,1280]{1,0:T(8,128)(2,1)}, u32[]{:S(2)}, u32[]{:S(2)}) %collective-permute-start.29) | collective-permute-done | bytes 327712 | tf_op jit(solution)/shard_map/ppermute | solution.py:1016
  488.5 9.9 %all-to-all-done.4 = bf16[8,128,384]{2,1,0:T(8,128)(2,1)S(1)} async-done(((bf16[8,128,384]{2,1,0:T(8,128)(2,1)}), bf16[8,128,384]{2,1,0:T(8,128)(2,1)S(1)}, u32[]{:S(2)}, u32[]{:S(2)}) %all-to-all-start.4) | async-done | bytes 786464 | tf_op jit(solution)/shard_map/all_to_all | solution.py:1390
  498.6 2.6 collective-permute-start.27
  503.8 5.3 %spread.1 = (f32[128,3072]{1,0:T(8,128)}, f32[128,1024]{1,0:T(8,128)}, f32[128,4096]{1,0:T(8,128)}, f32[512,1024]{1,0:T(8,128)}) custom-call(s32[4]{0:T(128)} %pad_add_fusion.2.ids, bf16[4,128,384]{2,1,0:T(8,128)(2,1)} %copy-done.12, bf16[4,128,384]{2,1,0:T(8,128)(2,1)} %copy-done.23, bf16[256,1024]{1,0:T(8,128)(2,1)} %add_convert_fusion.4.down, ...), custom_call_target="tpu_custom_call" | custom-call | bytes 6291456 | tf_op jit(solution)/shard_map/spread/pallas_call | solution.py:429
  509.1 2.3 collective-permute-done.25
  (160 shorter events, 24.3 us)
Async XLA Ops:
  7.2 23.1 %copy-start = (bf16[512,1024]{1,0:T(8,128)(2,1)S(1)}, bf16[512,1024]{1,0:T(8,128)(2,1)}, u32[]{:S(2)}) copy-start(bf16[512,1024]{1,0:T(8,128)(2,1)} %param.22) | copy-start | bytes 3145732
  12.3 51.6 %all-to-all-start = ((bf16[8,144,384]{2,1,0:T(8,128)(2,1)}), bf16[8,144,384]{2,1,0:T(8,128)(2,1)S(1)}, u32[]{:S(2)}, u32[]{:S(2)}) async-start(bf16[8,144,384]{2,1,0:T(8,128)(2,1)} %copy.74), calls=%async_computation | async-start | bytes 1769472 | tf_op jit(solution)/shard_map/all_to_all | solution.py:1095
  18.7 205.9 %all-gather.2.cloned.1.call-start = ((), (), s32[]{:S(2)}) async-start(), calls=%async_computation.7 | async-start | bytes 19464192 | tf_op jit(solution)/shard_map/all_gather | solution.py:1119
  18.7 45.1 %collective-permute-start.1 = (bf16[512,1024]{1,0:T(8,128)(2,1)}, bf16[512,1024]{1,0:T(8,128)(2,1)S(1)}, u32[]{:S(2)}, u32[]{:S(2)}) collective-permute-start(bf16[512,1024]{1,0:T(8,128)(2,1)} %bitcast.134), channel_id=1, source_target_pairs={{0,0},{1,1},{2,2},{3,3},{4,8},{5,9},{6,10},{7,11},{8,4},{9,5},{10,... | collective-permute-start | bytes 3145736 | tf_op jit(solution)/shard_map/ppermute | solution.py:1031
  30.3 40.5 %copy-start.25 = (s32[1,4096]{1,0:T(1,128)S(1)}, s32[1,4096]{1,0:T(1,128)}, u32[]{:S(2)}) copy-start(s32[1,4096]{1,0:T(1,128)} %param.17) | copy-start | bytes 49156
  30.4 40.5 %copy-start.27 = (s32[1,4]{1,0:T(1,128)S(1)}, s32[1,4]{1,0:T(1,128)}, u32[]{:S(2)}) copy-start(s32[1,4]{1,0:T(1,128)} %param.16) | copy-start | bytes 52
  63.9 1.4 copy-start.2
  69.8 34.7 %collective-permute-start.3 = (bf16[512,1024]{1,0:T(8,128)(2,1)}, bf16[512,1024]{1,0:T(8,128)(2,1)S(1)}, u32[]{:S(2)}, u32[]{:S(2)}) collective-permute-start(bf16[512,1024]{1,0:T(8,128)(2,1)} %norm.1.own), channel_id=1, source_target_pairs={{0,2},{1,3},{2,0},{3,1},{4,6},{5,7},{6,4},{7,5},{8,10},{9,11},{10,... | collective-permute-start | bytes 3145736 | tf_op jit(solution)/shard_map/ppermute | solution.py:1021
  69.8 35.8 %collective-permute-start.2 = (bf16[512,1024]{1,0:T(8,128)(2,1)}, bf16[512,1024]{1,0:T(8,128)(2,1)}, u32[]{:S(2)}, u32[]{:S(2)}) collective-permute-start(bf16[512,1024]{1,0:T(8,128)(2,1)} %norm.1.own), channel_id=1, source_target_pairs={{0,1},{1,0},{2,3},{3,2},{4,5},{5,4},{6,7},{7,6},{8,9},{9,8},{10,11... | collective-permute-start | bytes 3145736 | tf_op jit(solution)/shard_map/ppermute | solution.py:1021
  70.9 1.3 collective-permute-start
  71.1 66.5 %copy-start.18 = (bf16[8,128,384]{2,1,0:T(8,128)(2,1)}, bf16[8,128,384]{2,1,0:T(8,128)(2,1)S(1)}, u32[]{:S(2)}) copy-start(bf16[8,128,384]{2,1,0:T(8,128)(2,1)S(1)} %slice.87) | copy-start | bytes 2359300
  71.1 36.1 %collective-permute-start.6 = (bf16[1024,384]{1,0:T(8,128)(2,1)S(1)}, bf16[1024,384]{1,0:T(8,128)(2,1)}, u32[]{:S(2)}, u32[]{:S(2)}) collective-permute-start(bf16[1024,384]{1,0:T(8,128)(2,1)S(1)} %bitcast.113), channel_id=1, source_target_pairs={{0,8},{8,0},{16,24},{24,16},{1,9},{9,1},{17,25},{25,17},{2,10},{10... | collective-permute-start | bytes 2359304 | tf_op jit(solution)/shard_map/ppermute | solution.py:1016
  104.5 33.1 %copy-start.24 = (bf16[512,1024]{1,0:T(8,128)(2,1)}, bf16[512,1024]{1,0:T(8,128)(2,1)S(1)}, u32[]{:S(2)}) copy-start(bf16[512,1024]{1,0:T(8,128)(2,1)S(1)} %collective-permute-done.3.z_one) | copy-start | bytes 3145732
  104.5 16.1 %collective-permute-start.5 = (bf16[256,1024]{1,0:T(8,128)(2,1)S(1)}, bf16[256,1024]{1,0:T(8,128)(2,1)}, u32[]{:S(2)}, u32[]{:S(2)}) collective-permute-start(bf16[256,1024]{1,0:T(8,128)(2,1)S(1)} %slice.86), channel_id=1, source_target_pairs={{0,1},{1,0},{2,3},{3,2},{4,5},{5,4},{6,7},{7,6},{8,9},{9,8},{10,11... | collective-permute-start | bytes 1572872 | tf_op jit(solution)/shard_map/ppermute | solution.py:1021
  106.7 30.8 %collective-permute-start.4 = (bf16[256,1024]{1,0:T(8,128)(2,1)S(1)}, bf16[256,1024]{1,0:T(8,128)(2,1)}, u32[]{:S(2)}, u32[]{:S(2)}) collective-permute-start(bf16[256,1024]{1,0:T(8,128)(2,1)S(1)} %slice.85), channel_id=1, source_target_pairs={{0,2},{1,3},{2,0},{3,1},{4,6},{5,7},{6,4},{7,5},{8,10},{9,11},{10,... | collective-permute-start | bytes 1572872 | tf_op jit(solution)/shard_map/ppermute | solution.py:1021
  147.5 4.3 collective-permute-start.7
  176.0 3.7 copy-start.29
  176.1 45.1 %all-to-all-start.1 = ((bf16[8,512,128]{2,1,0:T(8,128)(2,1)}), bf16[8,512,128]{2,1,0:T(8,128)(2,1)S(1)}, u32[]{:S(2)}, u32[]{:S(2)}) async-start(bf16[8,512,128]{2,1,0:T(8,128)(2,1)} %get-tuple-element.65.attended), calls=%async_computation.1 | async-start | bytes 2097152 | tf_op jit(solution)/shard_map/all_to_all | solution.py:1039
  179.7 210.4 %reduce-scatter.5.cloned.1.call-start = ((), (), s32[]{:S(2)}) async-start(), calls=%async_computation.9 | async-start | bytes 4718592 | tf_op jit(solution)/shard_map/reduce_scatter | solution.py:1219
  179.8 41.8 %collective-permute-start.10 = (bf16[512,1024]{1,0:T(8,128)(2,1)S(1)}, bf16[512,1024]{1,0:T(8,128)(2,1)S(1)}, u32[]{:S(2)}, u32[]{:S(2)}) collective-permute-start(bf16[512,1024]{1,0:T(8,128)(2,1)S(1)} %bitcast.135), channel_id=1, source_target_pairs={{0,0},{1,1},{2,2},{3,3},{4,8},{5,9},{6,10},{7,11},{8,4},{9,5},{10,... | collective-permute-start | bytes 3145736 | tf_op jit(solution)/shard_map/ppermute | solution.py:1031
  221.2 3.4 copy-start.8
  221.2 3.4 collective-permute-start.8
  221.6 8.7 %copy-start.4 = (bf16[512,1024]{1,0:T(8,128)(2,1)}, bf16[512,1024]{1,0:T(8,128)(2,1)S(1)}, u32[]{:S(2)}) copy-start(bf16[512,1024]{1,0:T(8,128)(2,1)S(1)} %collective-permute-done.10.grad_own.cotangent) | copy-start | bytes 3145732
  221.6 9.1 %collective-permute-start.11 = (bf16[512,1024]{1,0:T(8,128)(2,1)S(1)}, bf16[512,1024]{1,0:T(8,128)(2,1)S(1)}, u32[]{:S(2)}, u32[]{:S(2)}) collective-permute-start(bf16[512,1024]{1,0:T(8,128)(2,1)S(1)} %collective-permute-done.10.grad_own.cotangent), channel_id=1, source_target_pairs={{0,8},{8,0},{16,24},{24,16},{1,9},{9,1},{17,25},{25,17},{2,10},{10... | collective-permute-start | bytes 3145736 | tf_op jit(solution)/shard_map/ppermute | solution.py:1016
  230.3 2.9 collective-permute-start.9
  230.7 2.5 copy-start.13
  270.1 1.2 copy-start.31
  271.3 2.7 collective-permute-start.14
  287.8 4.6 collective-permute-start.15
  288.1 34.7 %all-to-all-start.2 = ((bf16[8,512,128]{2,1,0:T(8,128)(2,1)}), bf16[8,512,128]{2,1,0:T(8,128)(2,1)}, u32[]{:S(2)}, u32[]{:S(2)}) async-start(bf16[8,512,128]{2,1,0:T(8,128)(2,1)} %get-tuple-element.76), calls=%async_computation.2 | async-start | bytes 2097152 | tf_op jit(solution)/shard_map/all_to_all | solution.py:1039
  292.4 176.2 %reduce-scatter.3.cloned.1.call-start = ((), (), s32[]{:S(2)}) async-start(), calls=%async_computation.8 | async-start | bytes 2949120 | tf_op jit(solution)/shard_map/reduce_scatter | solution.py:1285
  293.4 30.1 %copy-start.3 = (f32[512,1024]{1,0:T(8,128)S(1)}, f32[512,1024]{1,0:T(8,128)}, u32[]{:S(2)}) copy-start(f32[512,1024]{1,0:T(8,128)} %get-tuple-element.67.middle) | copy-start | bytes 6291460
  304.5 62.0 %collective-permute-start.17 = (bf16[8,128,1280]{2,1,0:T(8,128)(2,1)}, bf16[8,128,1280]{2,1,0:T(8,128)(2,1)}, u32[]{:S(2)}, u32[]{:S(2)}) collective-permute-start(bf16[8,128,1280]{2,1,0:T(8,128)(2,1)} %get-tuple-element.82), channel_id=1, source_target_pairs={{0,16},{8,24},{16,0},{24,8},{1,17},{9,25},{17,1},{25,9},{2,18},{10... | collective-permute-start | bytes 7864328 | tf_op jit(solution)/shard_map/ppermute | solution.py:1016
  305.8 17.7 %collective-permute-start.12 = (bf16[512,1024]{1,0:T(8,128)(2,1)}, bf16[512,1024]{1,0:T(8,128)(2,1)S(1)}, u32[]{:S(2)}, u32[]{:S(2)}) collective-permute-start(bf16[512,1024]{1,0:T(8,128)(2,1)} %get-tuple-element.71), channel_id=1, source_target_pairs={{0,8},{8,0},{16,24},{24,16},{1,9},{9,1},{17,25},{25,17},{2,10},{10... | collective-permute-start | bytes 3145736 | tf_op jit(solution)/shard_map/ppermute | solution.py:1016
  322.8 5.5 %collective-permute-start.16 = (bf16[8,512,128]{2,1,0:T(8,128)(2,1)}, bf16[8,512,128]{2,1,0:T(8,128)(2,1)S(1)}, u32[]{:S(2)}, u32[]{:S(2)}) collective-permute-start(bf16[8,512,128]{2,1,0:T(8,128)(2,1)} %all-to-all-done.2.grad_own), channel_id=1, source_target_pairs={{0,8},{8,0},{16,24},{24,16},{1,9},{9,1},{17,25},{25,17},{2,10},{10... | collective-permute-start | bytes 3145736 | tf_op jit(solution)/shard_map/ppermute | solution.py:1016
  325.7 40.8 %collective-permute-start.13 = (bf16[1,512,1024]{2,1,0:T(8,128)(2,1)S(1)}, bf16[1,512,1024]{2,1,0:T(8,128)(2,1)S(1)}, u32[]{:S(2)}, u32[]{:S(2)}) collective-permute-start(bf16[1,512,1024]{2,1,0:T(8,128)(2,1)S(1)} %bitcast.112), channel_id=1, source_target_pairs={{0,0},{1,1},{2,2},{3,3},{4,8},{5,9},{6,10},{7,11},{8,4},{9,5},{10,... | collective-permute-start | bytes 3145736 | tf_op jit(solution)/shard_map/ppermute | solution.py:1031
  329.3 37.2 %copy-start.9 = (bf16[8,128,1280]{2,1,0:T(8,128)(2,1)S(1)}, bf16[8,128,1280]{2,1,0:T(8,128)(2,1)}, u32[]{:S(2)}) copy-start(bf16[8,128,1280]{2,1,0:T(8,128)(2,1)} %get-tuple-element.89) | copy-start | bytes 7864324
  366.5 4.3 copy-start.16
  366.5 4.3 collective-permute-start.18
  387.4 19.1 %collective-permute-start.20 = (bf16[1024,384]{1,0:T(8,128)(2,1)}, bf16[1024,384]{1,0:T(8,128)(2,1)}, u32[]{:S(2)}, u32[]{:S(2)}) collective-permute-start(bf16[1024,384]{1,0:T(8,128)(2,1)} %grad_heads.3), channel_id=1, source_target_pairs={{0,8},{8,0},{16,24},{24,16},{1,9},{9,1},{17,25},{25,17},{2,10},{10... | collective-permute-start | bytes 2359304 | tf_op jit(solution)/shard_map/ppermute | solution.py:1016
  387.5 29.5 %collective-permute-start.19 = (bf16[2,512,512]{2,1,0:T(8,128)(2,1)}, bf16[2,512,512]{2,1,0:T(8,128)(2,1)S(1)}, u32[]{:S(2)}, u32[]{:S(2)}) collective-permute-start(bf16[2,512,512]{2,1,0:T(8,128)(2,1)} %get-tuple-element.91.y_out), channel_id=1, source_target_pairs={{0,1},{1,0},{2,3},{3,2},{4,5},{5,4},{6,7},{7,6},{8,9},{9,8},{10,11... | collective-permute-start | bytes 3145736 | tf_op jit(solution)/shard_map/ppermute | solution.py:1021
  390.1 40.5 %collective-permute-start.22 = (bf16[2,512,512]{2,1,0:T(8,128)(2,1)}, bf16[2,512,512]{2,1,0:T(8,128)(2,1)S(1)}, u32[]{:S(2)}, u32[]{:S(2)}) collective-permute-start(bf16[2,512,512]{2,1,0:T(8,128)(2,1)} %get-tuple-element.92.z_out), channel_id=1, source_target_pairs={{0,2},{1,3},{2,0},{3,1},{4,6},{5,7},{6,4},{7,5},{8,10},{9,11},{10,... | collective-permute-start | bytes 3145736 | tf_op jit(solution)/shard_map/ppermute | solution.py:1021
  390.1 27.0 %collective-permute-start.21 = (bf16[256,1024]{1,0:T(8,128)(2,1)}, bf16[256,1024]{1,0:T(8,128)(2,1)}, u32[]{:S(2)}, u32[]{:S(2)}) collective-permute-start(bf16[256,1024]{1,0:T(8,128)(2,1)} %reduce-scatter.5.cloned.1.call-done), channel_id=1, source_target_pairs={{0,16},{8,24},{16,0},{24,8},{1,17},{9,25},{17,1},{25,9},{2,18},{10... | collective-permute-start | bytes 1572872 | tf_op jit(solution)/shard_map/ppermute | solution.py:1016
  406.5 10.5 %copy-start.19 = (bf16[256,1024]{1,0:T(8,128)(2,1)S(1)}, bf16[256,1024]{1,0:T(8,128)(2,1)}, u32[]{:S(2)}) copy-start(bf16[256,1024]{1,0:T(8,128)(2,1)} %reduce-scatter.5.cloned.1.call-done) | copy-start | bytes 1572868
  408.2 46.6 %collective-permute-start.26 = (bf16[1024,384]{1,0:T(8,128)(2,1)S(1)}, bf16[1024,384]{1,0:T(8,128)(2,1)}, u32[]{:S(2)}, u32[]{:S(2)}) collective-permute-start(bf16[1024,384]{1,0:T(8,128)(2,1)S(1)} %add_convert_fusion.3), channel_id=1, source_target_pairs={{0,16},{8,24},{16,0},{24,8},{1,17},{9,25},{17,1},{25,9},{2,18},{10... | collective-permute-start | bytes 2359304 | tf_op jit(solution)/shard_map/ppermute | solution.py:1016
  417.0 13.5 %copy-start.6 = (bf16[2,512,512]{2,1,0:T(8,128)(2,1)}, bf16[2,512,512]{2,1,0:T(8,128)(2,1)S(1)}, u32[]{:S(2)}) copy-start(bf16[2,512,512]{2,1,0:T(8,128)(2,1)S(1)} %collective-permute-done.19.y_came) | copy-start | bytes 3145732
  419.5 18.1 %copy-start.26 = (f32[8,1024]{1,0:T(8,128)S(1)}, f32[8,1024]{1,0:T(8,128)}, u32[]{:S(2)}) copy-start(f32[8,1024]{1,0:T(8,128)} %get-tuple-element.96) | copy-start | bytes 98308
  419.5 18.1 %slice-start = ((f32[8,1024]{1,0:T(8,128)}), f32[2,1024]{1,0:T(2,128)S(1)}, s32[]{:S(2)}) async-start(f32[8,1024]{1,0:T(8,128)} %first_sums.1), calls=%async_computation.10 | async-start | bytes 16384 | tf_op jit(solution)/shard_map/slice | solution.py:1337
  435.4 14.4 %collective-permute-start.24 = (bf16[512,512]{1,0:T(8,128)(2,1)}, bf16[512,512]{1,0:T(8,128)(2,1)S(1)}, u32[]{:S(2)}, u32[]{:S(2)}) collective-permute-start(bf16[512,512]{1,0:T(8,128)(2,1)} %get-tuple-element.105), channel_id=1, source_target_pairs={{0,1},{1,0},{2,3},{3,2},{4,5},{5,4},{6,7},{7,6},{8,9},{9,8},{10,11... | collective-permute-start | bytes 1572872 | tf_op jit(solution)/shard_map/ppermute | solution.py:1021
  436.8 18.0 %collective-permute-start.23 = (bf16[512,512]{1,0:T(8,128)(2,1)}, bf16[512,512]{1,0:T(8,128)(2,1)S(1)}, u32[]{:S(2)}, u32[]{:S(2)}) collective-permute-start(bf16[512,512]{1,0:T(8,128)(2,1)} %get-tuple-element.102), channel_id=1, source_target_pairs={{0,2},{1,3},{2,0},{3,1},{4,6},{5,7},{6,4},{7,5},{8,10},{9,11},{10,... | collective-permute-start | bytes 1572872 | tf_op jit(solution)/shard_map/ppermute | solution.py:1021
  438.4 26.5 %all-to-all-start.3 = ((f32[32,16,128]{2,1,0:T(8,128)}), f32[32,16,128]{2,1,0:T(8,128)S(1)}, u32[]{:S(2)}, u32[]{:S(2)}) async-start(f32[32,16,128]{2,1,0:T(8,128)} %bitcast.37), calls=%async_computation.5 | async-start | bytes 524288 | tf_op jit(solution)/shard_map/all_to_all | solution.py:1374
  449.8 18.7 %copy-start.20 = (bf16[512,512]{1,0:T(8,128)(2,1)}, bf16[512,512]{1,0:T(8,128)(2,1)S(1)}, u32[]{:S(2)}) copy-start(bf16[512,512]{1,0:T(8,128)(2,1)S(1)} %collective-permute-done.24.y_second) | copy-start | bytes 1572868
  454.7 13.8 %copy-start.21 = (bf16[512,512]{1,0:T(8,128)(2,1)}, bf16[512,512]{1,0:T(8,128)(2,1)S(1)}, u32[]{:S(2)}) copy-start(bf16[512,512]{1,0:T(8,128)(2,1)S(1)} %collective-permute-done.23.z_second) | copy-start | bytes 1572868
  465.0 33.4 %all-to-all-start.4 = ((bf16[8,128,384]{2,1,0:T(8,128)(2,1)}), bf16[8,128,384]{2,1,0:T(8,128)(2,1)S(1)}, u32[]{:S(2)}, u32[]{:S(2)}) async-start(bf16[8,128,384]{2,1,0:T(8,128)(2,1)} %bitcast.40), calls=%async_computation.6 | async-start | bytes 1572864 | tf_op jit(solution)/shard_map/all_to_all | solution.py:1390
  468.6 12.4 %copy-start.10 = (bf16[256,1024]{1,0:T(8,128)(2,1)S(1)}, bf16[256,1024]{1,0:T(8,128)(2,1)}, u32[]{:S(2)}) copy-start(bf16[256,1024]{1,0:T(8,128)(2,1)} %add_convert_fusion.4.down) | copy-start | bytes 1572868
  475.0 36.4 %collective-permute-start.25 = (bf16[1,512,1024]{2,1,0:T(8,128)(2,1)}, bf16[1,512,1024]{2,1,0:T(8,128)(2,1)S(1)}, u32[]{:S(2)}, u32[]{:S(2)}) collective-permute-start(bf16[1,512,1024]{2,1,0:T(8,128)(2,1)} %bitcast.109), channel_id=1, source_target_pairs={{0,0},{1,1},{2,2},{3,3},{4,8},{5,9},{6,10},{7,11},{8,4},{9,5},{10,... | collective-permute-start | bytes 3145736 | tf_op jit(solution)/shard_map/ppermute | solution.py:1031
  480.8 7.7 %collective-permute-start.29 = (bf16[128,1280]{1,0:T(8,128)(2,1)}, bf16[128,1280]{1,0:T(8,128)(2,1)}, u32[]{:S(2)}, u32[]{:S(2)}) collective-permute-start(bf16[128,1280]{1,0:T(8,128)(2,1)} %reduce-scatter.3.cloned.1.call-done.mixed), channel_id=1, source_target_pairs={{0,16},{8,24},{16,0},{24,8},{1,17},{9,25},{17,1},{25,9},{2,18},{10... | collective-permute-start | bytes 983048 | tf_op jit(solution)/shard_map/ppermute | solution.py:1016
  481.0 21.3 %collective-permute-start.28 = (bf16[256,1024]{1,0:T(8,128)(2,1)S(1)}, bf16[256,1024]{1,0:T(8,128)(2,1)S(1)}, u32[]{:S(2)}, u32[]{:S(2)}) collective-permute-start(bf16[256,1024]{1,0:T(8,128)(2,1)S(1)} %copy-done.10), channel_id=1, source_target_pairs={{0,8},{8,0},{16,24},{24,16},{1,9},{9,1},{17,25},{25,17},{2,10},{10... | collective-permute-start | bytes 1572872 | tf_op jit(solution)/shard_map/ppermute | solution.py:1016
  481.0 21.3 %collective-permute-start.30 = (bf16[128,1280]{1,0:T(8,128)(2,1)}, bf16[128,1280]{1,0:T(8,128)(2,1)}, u32[]{:S(2)}, u32[]{:S(2)}) collective-permute-start(bf16[128,1280]{1,0:T(8,128)(2,1)} %reduce-scatter.3.cloned.1.call-done.mixed), channel_id=1, source_target_pairs={{0,8},{8,0},{16,24},{24,16},{1,9},{9,1},{17,25},{25,17},{2,10},{10... | collective-permute-start | bytes 983048 | tf_op jit(solution)/shard_map/ppermute | solution.py:1016
  488.5 13.8 %collective-permute-start.31 = (bf16[128,1280]{1,0:T(8,128)(2,1)}, bf16[128,1280]{1,0:T(8,128)(2,1)}, u32[]{:S(2)}, u32[]{:S(2)}) collective-permute-start(bf16[128,1280]{1,0:T(8,128)(2,1)} %collective-permute-done.29.mixed_x), channel_id=1, source_target_pairs={{0,8},{8,0},{16,24},{24,16},{1,9},{9,1},{17,25},{25,17},{2,10},{10... | collective-permute-start | bytes 983048 | tf_op jit(solution)/shard_map/ppermute | solution.py:1016
  498.5 13.0 %copy-start.17 = (bf16[1,512,1024]{2,1,0:T(8,128)(2,1)S(1)}, bf16[1,512,1024]{2,1,0:T(8,128)(2,1)}, u32[]{:S(2)}) copy-start(bf16[1,512,1024]{2,1,0:T(8,128)(2,1)} %copy-done.16) | copy-start | bytes 3145732
  498.6 3.9 copy-start.12
  498.6 3.9 collective-permute-start.27
  511.4 1.9 copy-start.1
  (9 other events, 8.8 us)
Sparse Core Ops, SparseCore 0:
  64.0 157.3 all-gather.1
  270.2 101.6 reduce-scatter.4
  375.9 90.6 reduce-scatter.2

commit v4 on v3

--- a/solution.py
+++ b/solution.py
@@ -1371,8 +1371,6 @@
         (like(pair[1:], low), like(pair[1:], low)),
     )(ids, keep_left, keep_right, y_came, z_came)
     z_last, y_last = hop_seq(z_second, 2), hop_seq(y_second, 1)
-    sums = lax.all_to_all(after(sums, z_second), ("seq", "batch"), 0, 0, tiled=True)
-    sums = jnp.sum(sums, axis=0)
     grad_inputs = call(
         last_kernel,
         "last",
@@ -1380,7 +1378,7 @@
         [slab, pair_spec, pair_spec, half_spec, half_spec, slab, slab, whole(16, width)],
         slab,
         like((frames, width), low),
-    )(ids, after(first, mixed, sums), y_came, z_came, z_last, y_last, tokens_here, grad_middle, vectors)
+    )(ids, after(first, mixed), y_came, z_came, z_last, y_last, tokens_here, grad_middle, vectors)
     mixed_x = hop_batch(mixed, 2)
     grad_inputs = swap_halves(grad_inputs[None])
 
@@ -1391,6 +1389,8 @@
         heads_sum.reshape(8, part, 3 * LANES), "seq", 0, 0, tiled=True
     ).astype(wide)
     heads_sum = (heads_sum[:4] + heads_sum[4:]).astype(low)
+    sums = lax.all_to_all(after(sums, heads_sum), ("seq", "batch"), 0, 0, tiled=True)
+    sums = jnp.sum(sums, axis=0)
     heads_came = hop_batch(heads_sum, 1)
     mixed_core, mixed_both = hop_batch(mixed, 1), hop_batch(mixed_x, 1)
     grad_qkv_w, grad_out_w, grad_up_w, grad_down_w = call(

time: 522 us -> 522 us (level)
  Pallas kernels: 182 us -> 190 us
    all_to_all x1, waiting for transfers between devices: 7.8 us -> 2.2 us  [square_shards(): lax.all_to_all(after(sums, heads_sum), ('seq', 'batch'), 0, 0, tiled=True)]
    unnamed x70 -> x76, local copies, waits for them, and re-layouts: 13.5 us -> 15 us
  transfers between devices with their start and end apart: 40 -> 40, of which waited for: 21 -> 20; matrix products, arithmetic and copies ran while one was open for 5% -> 4% of each run, Pallas kernels for 28% -> 30%
where the time goes in v4:
time: 522 us; the launch traced here: 520 us
  waiting for transfers between devices  215 us (41%)
  Pallas kernels  190 us (36%)
  starting transfers between devices  57.9 us (11%)
  local copies, waits for them, and re-layouts  29.1 us (6%)
  between operations  14.3 us (3%)
  other arithmetic  13.3 us (3%)
    pallas_call x15, Pallas kernels, run(): pl.pallas_call(kernel, out_shape=out_shape, grid_spec=pltpu.PrefetchScala...  124 us
    ppermute x8, waiting for transfers between devices, hop_seq(): return lax.ppermute(block, 'seq', [(i, i ^ bits) for i in range(size)])  97.8 us
    all_to_all x2, waiting for transfers between devices, trade(): lax.all_to_all(block, 'seq', 0, 0, tiled=True, axis_index_groups=groups)  52.9 us
    pallas_call x1, Pallas kernels, attend_back(): pl.pallas_call(attend_back_kernel, out_shape=(like(own.shape, jnp.bfloat1...  39.3 us
    ppermute x4, waiting for transfers between devices, swap_halves(): return lax.ppermute(block, ('batch', 'seq'), route)  33 us
    pallas_call x1, Pallas kernels, attend(): pl.pallas_call(attend_kernel, out_shape=(like((8, TILE, LANES), jnp.bfloa...  25.9 us
    ppermute x4, starting transfers between devices, swap_halves(): return lax.ppermute(block, ('batch', 'seq'), route)  17.4 us
    ppermute x20, waiting for transfers between devices, hop_batch(): return lax.ppermute(block, 'batch', [(i, i ^ bit) for i in range(size)])  16.7 us
  transfers between devices with their start and end apart: 40, of which 20 were waited for; matrix products, arithmetic and copies ran while one was open for 4% of the time, Pallas kernels for 30%

profile of v4, /device:TPU:1, one launch (start us, length us, event | category | flops | bytes accessed | tf_op | source)
XLA Modules:
  0.0 519.7 jit_solution(13364691144449934657)
XLA Ops:
  7.2 1.7 concatenate.19
  9.0 1.5 copy.71
  10.8 1.4 copy.74
  12.3 6.4 %all-to-all-start = ((bf16[8,144,384]{2,1,0:T(8,128)(2,1)}), bf16[8,144,384]{2,1,0:T(8,128)(2,1)S(1)}, u32[]{:S(2)}, u32[]{:S(2)}) async-start(bf16[8,144,384]{2,1,0:T(8,128)(2,1)} %copy.74), calls=%async_computation | async-start | bytes 1769472 | tf_op jit(solution)/shard_map/all_to_all | solution.py:1095
  18.7 5.3 %collective-permute-start.1 = (bf16[512,1024]{1,0:T(8,128)(2,1)}, bf16[512,1024]{1,0:T(8,128)(2,1)S(1)}, u32[]{:S(2)}, u32[]{:S(2)}) collective-permute-start(bf16[512,1024]{1,0:T(8,128)(2,1)} %bitcast.134), channel_id=1, source_target_pairs={{0,0},{1,1},{2,2},{3,3},{4,8},{5,9},{6,10},{7,11},{8,4},{9,5},{10,... | collective-permute-start | bytes 3145736 | tf_op jit(solution)/shard_map/ppermute | solution.py:1031
  24.1 2.6 reshape.158
  26.6 2.8 dynamic-slice_reduce_fusion
  31.2 32.7 %collective-permute-done.1.tokens = bf16[512,1024]{1,0:T(8,128)(2,1)S(1)} collective-permute-done((bf16[512,1024]{1,0:T(8,128)(2,1)}, bf16[512,1024]{1,0:T(8,128)(2,1)S(1)}, u32[]{:S(2)}, u32[]{:S(2)}) %collective-permute-start.1) | collective-permute-done | bytes 1048608 | tf_op jit(solution)/shard_map/ppermute | solution.py:1031
  65.2 4.5 norm.1.own
  69.8 1.0 collective-permute-start.2
  72.1 32.4 %collective-permute-done.3.z_one = bf16[512,1024]{1,0:T(8,128)(2,1)S(1)} collective-permute-done((bf16[512,1024]{1,0:T(8,128)(2,1)}, bf16[512,1024]{1,0:T(8,128)(2,1)S(1)}, u32[]{:S(2)}, u32[]{:S(2)}) %collective-permute-start.3) | collective-permute-done | bytes 1048608 | tf_op jit(solution)/shard_map/ppermute | solution.py:1021
  104.5 1.1 collective-permute-start.5
  105.6 1.1 slice.85
  107.2 13.4 %collective-permute-done.5.bottom = bf16[256,1024]{1,0:T(8,128)(2,1)} collective-permute-done((bf16[256,1024]{1,0:T(8,128)(2,1)S(1)}, bf16[256,1024]{1,0:T(8,128)(2,1)}, u32[]{:S(2)}, u32[]{:S(2)}) %collective-permute-start.5) | collective-permute-done | bytes 524320 | tf_op jit(solution)/shard_map/ppermute | solution.py:1021
  120.6 16.8 %collective-permute-done.4.top = bf16[256,1024]{1,0:T(8,128)(2,1)} collective-permute-done((bf16[256,1024]{1,0:T(8,128)(2,1)S(1)}, bf16[256,1024]{1,0:T(8,128)(2,1)}, u32[]{:S(2)}, u32[]{:S(2)}) %collective-permute-start.4) | collective-permute-done | bytes 524320 | tf_op jit(solution)/shard_map/ppermute | solution.py:1021
  137.5 9.9 %project.1 = (bf16[4,512,384]{2,1,0:T(8,128)(2,1)}, bf16[4,512,384]{2,1,0:T(8,128)(2,1)}, bf16[4,512,1024]{2,1,0:T(8,128)(2,1)}) custom-call(s32[4]{0:T(128)} %pad_add_fusion.2.ids, bf16[512,1024]{1,0:T(8,128)(2,1)} %norm.1.own, bf16[512,1024]{1,0:T(8,128)(2,1)} %collective-permute-done.2.y_one, bf16[512,1024]{1,0:T(8,128)(2,1)} %copy-done.26, ...), custom_call_target="tpu_custom_call" | custom-call | flops 3221225472 | bytes 11534336 | tf_op jit(solution)/shard_map/project/pallas_call | solution.py:429
  148.8 2.9 collective-permute-done.7
  151.7 1.2 copy-done.30
  152.9 25.9 %attend.1 = (bf16[8,512,128]{2,1,0:T(8,128)(2,1)}, f32[2,4096]{1,0:T(2,128)}) custom-call(s32[4]{0:T(128)} %pad_add_fusion.2.ids, s32[3,8]{1,0:T(4,128)} %pad_add_fusion.1.bounds, bf16[2048,384]{1,0:T(8,128)(2,1)} %bitcast.136, bf16[2048,384]{1,0:T(8,128)(2,1)} %bitcast.132, f32[1,4096]{1,0:T(1,128)} %fusion.2.places_row), custom_call_target="tpu_custom_call" | custom-call | flops 4294967296 | bytes 9830400 | tf_op jit(solution)/shard_map/attend/pallas_call | solution.py:578
  178.7 3.7 all-to-all-start.1
  182.5 2.1 collective-permute-start.10
  184.6 36.4 %all-to-all-done.1.own = bf16[8,512,128]{2,1,0:T(8,128)(2,1)S(1)} async-done(((bf16[8,512,128]{2,1,0:T(8,128)(2,1)}), bf16[8,512,128]{2,1,0:T(8,128)(2,1)S(1)}, u32[]{:S(2)}, u32[]{:S(2)}) %all-to-all-start.1) | async-done | bytes 1048608 | tf_op jit(solution)/shard_map/all_to_all | solution.py:1039
  221.6 3.0 collective-permute-done.8.came
  224.6 5.7 %out_project.1 = (bf16[512,1024]{1,0:T(8,128)(2,1)}, f32[512,1024]{1,0:T(8,128)}, bf16[512,1024]{1,0:T(8,128)(2,1)}) custom-call(s32[4]{0:T(128)} %pad_add_fusion.2.ids, bf16[8,512,128]{2,1,0:T(8,128)(2,1)} %copy-done.8, bf16[8,512,128]{2,1,0:T(8,128)(2,1)} %collective-permute-done.8.came, bf16[512,1024]{1,0:T(8,128)(2,1)} %copy-done.2, ...), custom_call_target="tpu_custom_call" | custom-call | flops 1073741824 | bytes 44171264 | tf_op jit(solution)/shard_map/out_project/pallas_call | solution.py:429
  230.7 2.5 collective-permute-done.9.normed_came
  233.2 1.0 copy-done.5
  234.2 26.8 %feed_forward.1 = (bf16[2,512,2048]{2,1,0:T(8,128)(2,1)}, bf16[2,512,2048]{2,1,0:T(8,128)(2,1)}, f32[8,1024]{1,0:T(8,128)}, f32[512,1024]{1,0:T(8,128)}, bf16[51...) custom-call(s32[4]{0:T(128)} %pad_add_fusion.2.ids, ...), custom_call_target="tpu_custom_call" | custom-call | flops 17179869184 | bytes 159514624 | tf_op jit(solution)/shard_map/feed_forward/pallas_call | solution.py:429
  261.0 9.1 %grad_down.1 = bf16[2048,1024]{1,0:T(8,128)(2,1)} custom-call(s32[4]{0:T(128)} %pad_add_fusion.2.ids, bf16[2,512,2048]{2,1,0:T(8,128)(2,1)} %get-tuple-element.73.act, bf16[512,1024]{1,0:T(8,128)(2,1)} %copy-done.4, bf16[512,1024]{1,0:T(8,128)(2,1)} %copy-done.13), custom_call_target="tpu_custom_call" | custom-call | flops 4294967296 | bytes 12582912 | tf_op jit(solution)/shard_map/grad_down/pallas_call | solution.py:429
  270.2 1.2 copy-done.34
  271.7 2.3 collective-permute-done.14.back_came
  275.0 8.2 %middle_back.1 = (f32[512,1024]{1,0:T(8,128)}, bf16[512,1024]{1,0:T(8,128)(2,1)}, bf16[8,512,128]{2,1,0:T(8,128)(2,1)}, f32[8,1024]{1,0:T(8,128)}) custom-call(s32[4]{0:T(128)} %pad_add_fusion.2.ids, f32[512,1024]{1,0:T(8,128)} %get-tuple-element.74.back_own, bf16[512,1024]{1,0:T(8,128)(2,1)} %copy-done.15, f32[512,1024]{1,0:T(8,128)} %get-tuple-element.67.middle, ...), custom_call_target="tpu_custom_call" | custom-call | flops 1073741824 | bytes 50462720 | tf_op jit(solution)/shard_map/middle_back/pallas_call | solution.py:429
  283.2 4.6 grad_out.1
  288.1 4.3 all-to-all-start.2
  293.4 11.1 %grad_up.1 = (bf16[8,128,1280]{2,1,0:T(8,128)(2,1)}, bf16[8,128,1280]{2,1,0:T(8,128)(2,1)}) custom-call(s32[4]{0:T(128)} %pad_add_fusion.2.ids, bf16[512,1024]{1,0:T(8,128)(2,1)} %get-tuple-element.68.normed_own, bf16[512,1024]{1,0:T(8,128)(2,1)} %copy-done.5, bf16[2,512,2048]{2,1,0:T(8,128)(2,1)} %get-tuple-element.77.grad_up, ...), custom_call_target="tpu_custom_call" | custom-call | flops 524288 | bytes 16777216 | tf_op jit(solution)/shard_map/grad_up/pallas_call | solution.py:429
  304.5 1.2 collective-permute-start.17
  306.2 16.5 %all-to-all-done.2.grad_own = bf16[8,512,128]{2,1,0:T(8,128)(2,1)} async-done(((bf16[8,512,128]{2,1,0:T(8,128)(2,1)}), bf16[8,512,128]{2,1,0:T(8,128)(2,1)}, u32[]{:S(2)}, u32[]{:S(2)}) %all-to-all-start.2) | async-done | bytes 1048608 | tf_op jit(solution)/shard_map/all_to_all | solution.py:1039
  323.4 2.3 add_convert_fusion.1
  325.6 2.2 collective-permute-start.13
  328.9 39.3 %attend_back.1 = (bf16[2048,384]{1,0:T(8,128)(2,1)}, bf16[2048,384]{1,0:T(8,128)(2,1)}) custom-call(s32[4]{0:T(128)} %pad_add_fusion.2.ids, s32[3,8]{1,0:T(4,128)} %pad_add_fusion.1.bounds, bf16[2048,384]{1,0:T(8,128)(2,1)} %bitcast.137, bf16[2048,384]{1,0:T(8,128)(2,1)} %bitcast.133, bf16[8,512,128]{2,1,0:T(8,128)(2,1)} %all-to-all-done.2.grad_own, ...), custom_call_target="tpu_custom_call" | custom-call | flops 10737418240 | bytes 9830400 | tf_op jit(solution)/shard_map/attend_back/pallas_call | solution.py:706
  368.2 4.2 add_convert_fusion
  372.4 1.4 copy-done.31
  373.8 3.4 collective-permute-done.18.grads
  377.2 1.1 copy-done.11
  378.4 9.4 %back_project.1 = (f32[512,1024]{1,0:T(8,128)}, bf16[2,512,512]{2,1,0:T(8,128)(2,1)}, bf16[2,512,512]{2,1,0:T(8,128)(2,1)}, f32[512,512]{1,0:T(8,128)}, f32[512,512]{1,0:T(8,128)}) custom-call(s32[4]{0:T(128)} %pad_add_fusion.2.ids, bf16[4,512,384]{2,1,0:T(8,128)(2,1)} %bitcast.107, bf16[4,512,384]{2,1,0:T(8,128)(2,1)} %bitcast.108, ...), custom_call_target="tpu_custom_call" | custom-call | flops 3221225472 | bytes 9437184 | tf_op jit(solution)/shard_map/back_project/pallas_call | solution.py:429
  387.8 6.2 %grad_heads.3 = bf16[1024,384]{1,0:T(8,128)(2,1)} custom-call(s32[4]{0:T(128)} %pad_add_fusion.2.ids, bf16[2048,1024]{1,0:T(8,128)(2,1)} %bitcast.96, bf16[2048,384]{1,0:T(8,128)(2,1)} %copy-done.11), custom_call_target="tpu_custom_call" | custom-call | flops 1610612736 | bytes 11534336 | tf_op jit(solution)/shard_map/grad_heads/pallas_call | solution.py:429
  394.1 1.7 collective-permute-start.19
  395.8 2.2 collective-permute-start.22
  398.1 7.2 %first_sums.1 = f32[8,1024]{1,0:T(8,128)} custom-call(s32[4]{0:T(128)} %pad_add_fusion.2.ids, f32[512,1024]{1,0:T(8,128)} %get-tuple-element.91.first, bf16[2,512,512]{2,1,0:T(8,128)(2,1)} %get-tuple-element.92.y_out, bf16[2,512,512]{2,1,0:T(8,128)(2,1)} %get-tuple-element.93.z_out, f32[512,512]{1,0:T(8,128)} %get-tuple-element.94.keep_left, ...), custom_call_target="tpu_custom_call" | custom-call | bytes 21102592 | tf_op jit(solution)/shard_map/first_sums/pallas_call | solution.py:429
  405.3 6.1 %grad_heads.2 = bf16[1024,384]{1,0:T(8,128)(2,1)} custom-call(s32[4]{0:T(128)} %pad_add_fusion.2.ids, bf16[2048,1024]{1,0:T(8,128)(2,1)} %bitcast.97, bf16[2048,384]{1,0:T(8,128)(2,1)} %get-tuple-element.85.grads), custom_call_target="tpu_custom_call" | custom-call | flops 1610612736 | bytes 11534336 | tf_op jit(solution)/shard_map/grad_heads/pallas_call | solution.py:429
  411.3 1.7 add_convert_fusion.3
  413.0 1.5 collective-permute-start.26
  414.5 13.8 %collective-permute-done.19.y_came = bf16[2,512,512]{2,1,0:T(8,128)(2,1)S(1)} collective-permute-done((bf16[2,512,512]{2,1,0:T(8,128)(2,1)S(1)}, bf16[2,512,512]{2,1,0:T(8,128)(2,1)S(1)}, u32[]{:S(2)}, u32[]{:S(2)}) %collective-permute-start.19) | collective-permute-done | bytes 1048608 | tf_op jit(solution)/shard_map/ppermute | solution.py:1021
  430.2 3.9 second.1
  434.2 1.2 collective-permute-start.24
  435.3 20.6 %collective-permute-done.23.z_second = bf16[512,512]{1,0:T(8,128)(2,1)S(1)} collective-permute-done((bf16[512,512]{1,0:T(8,128)(2,1)}, bf16[512,512]{1,0:T(8,128)(2,1)S(1)}, u32[]{:S(2)}, u32[]{:S(2)}) %collective-permute-start.23) | collective-permute-done | bytes 524320 | tf_op jit(solution)/shard_map/ppermute | solution.py:1021
  456.0 1.2 add_convert_fusion.2
  457.2 3.5 all-to-all-start.3
  460.8 6.4 %last.1 = bf16[512,1024]{1,0:T(8,128)(2,1)} custom-call(s32[4]{0:T(128)} %pad_add_fusion.2.ids, f32[512,1024]{1,0:T(8,128)} %get-tuple-element.91.first, bf16[2,512,512]{2,1,0:T(8,128)(2,1)} %copy-done.6, bf16[2,512,512]{2,1,0:T(8,128)(2,1)} %copy-done.7, bf16[512,512]{1,0:T(8,128)(2,1)} %copy-done.21, bf16[512,512]{1,0:T(8,128)(2,1)} %copy-done.22, ...), custom_call_target="tpu_custom_call" | custom-call | bytes 16908288 | tf_op jit(solution)/shard_map/last/pallas_call | solution.py:429
  467.3 7.7 %collective-permute-start.25 = (bf16[1,512,1024]{2,1,0:T(8,128)(2,1)}, bf16[1,512,1024]{2,1,0:T(8,128)(2,1)S(1)}, u32[]{:S(2)}, u32[]{:S(2)}) collective-permute-start(bf16[1,512,1024]{2,1,0:T(8,128)(2,1)} %bitcast.109), channel_id=1, source_target_pairs={{0,0},{1,1},{2,2},{3,3},{4,8},{5,9},{6,10},{7,11},{8,4},{9,5},{10,... | collective-permute-start | bytes 3145736 | tf_op jit(solution)/shard_map/ppermute | solution.py:1031
  477.0 12.7 %all-to-all-done.3 = bf16[8,128,384]{2,1,0:T(8,128)(2,1)S(1)} async-done(((bf16[8,128,384]{2,1,0:T(8,128)(2,1)}), bf16[8,128,384]{2,1,0:T(8,128)(2,1)S(1)}, u32[]{:S(2)}, u32[]{:S(2)}) %all-to-all-start.3) | async-done | bytes 786464 | tf_op jit(solution)/shard_map/all_to_all | solution.py:1388
  490.6 7.2 %all-to-all-start.4 = ((f32[32,16,128]{2,1,0:T(8,128)}), f32[32,16,128]{2,1,0:T(8,128)S(1)}, u32[]{:S(2)}, u32[]{:S(2)}) async-start(f32[32,16,128]{2,1,0:T(8,128)} %bitcast.40), calls=%async_computation.6 | async-start | bytes 524288 | tf_op jit(solution)/shard_map/all_to_all | solution.py:1392
  498.7 1.6 collective-permute-done.30.mixed_core
  502.3 5.3 %spread.1 = (f32[128,3072]{1,0:T(8,128)}, f32[128,1024]{1,0:T(8,128)}, f32[128,4096]{1,0:T(8,128)}, f32[512,1024]{1,0:T(8,128)}) custom-call(s32[4]{0:T(128)} %pad_add_fusion.2.ids, bf16[4,128,384]{2,1,0:T(8,128)(2,1)} %copy-done.12, bf16[4,128,384]{2,1,0:T(8,128)(2,1)} %copy-done.23, bf16[256,1024]{1,0:T(8,128)(2,1)} %copy-done.10, ...), custom_call_target="tpu_custom_call" | custom-call | bytes 6291456 | tf_op jit(solution)/shard_map/spread/pallas_call | solution.py:429
  507.8 2.2 all-to-all-done.4
  (166 shorter events, 23.9 us)
Async XLA Ops:
  7.2 23.1 %copy-start = (bf16[512,1024]{1,0:T(8,128)(2,1)S(1)}, bf16[512,1024]{1,0:T(8,128)(2,1)}, u32[]{:S(2)}) copy-start(bf16[512,1024]{1,0:T(8,128)(2,1)} %param.22) | copy-start | bytes 3145732
  12.3 51.6 %all-to-all-start = ((bf16[8,144,384]{2,1,0:T(8,128)(2,1)}), bf16[8,144,384]{2,1,0:T(8,128)(2,1)S(1)}, u32[]{:S(2)}, u32[]{:S(2)}) async-start(bf16[8,144,384]{2,1,0:T(8,128)(2,1)} %copy.74), calls=%async_computation | async-start | bytes 1769472 | tf_op jit(solution)/shard_map/all_to_all | solution.py:1095
  18.7 205.9 %all-gather.2.cloned.1.call-start = ((), (), s32[]{:S(2)}) async-start(), calls=%async_computation.7 | async-start | bytes 19464192 | tf_op jit(solution)/shard_map/all_gather | solution.py:1119
  18.7 45.1 %collective-permute-start.1 = (bf16[512,1024]{1,0:T(8,128)(2,1)}, bf16[512,1024]{1,0:T(8,128)(2,1)S(1)}, u32[]{:S(2)}, u32[]{:S(2)}) collective-permute-start(bf16[512,1024]{1,0:T(8,128)(2,1)} %bitcast.134), channel_id=1, source_target_pairs={{0,0},{1,1},{2,2},{3,3},{4,8},{5,9},{6,10},{7,11},{8,4},{9,5},{10,... | collective-permute-start | bytes 3145736 | tf_op jit(solution)/shard_map/ppermute | solution.py:1031
  30.3 40.5 %copy-start.27 = (s32[1,4096]{1,0:T(1,128)S(1)}, s32[1,4096]{1,0:T(1,128)}, u32[]{:S(2)}) copy-start(s32[1,4096]{1,0:T(1,128)} %param.17) | copy-start | bytes 49156
  30.4 40.5 %copy-start.29 = (s32[1,4]{1,0:T(1,128)S(1)}, s32[1,4]{1,0:T(1,128)}, u32[]{:S(2)}) copy-start(s32[1,4]{1,0:T(1,128)} %param.16) | copy-start | bytes 52
  63.9 1.4 copy-start.2
  69.8 34.7 %collective-permute-start.3 = (bf16[512,1024]{1,0:T(8,128)(2,1)}, bf16[512,1024]{1,0:T(8,128)(2,1)S(1)}, u32[]{:S(2)}, u32[]{:S(2)}) collective-permute-start(bf16[512,1024]{1,0:T(8,128)(2,1)} %norm.1.own), channel_id=1, source_target_pairs={{0,2},{1,3},{2,0},{3,1},{4,6},{5,7},{6,4},{7,5},{8,10},{9,11},{10,... | collective-permute-start | bytes 3145736 | tf_op jit(solution)/shard_map/ppermute | solution.py:1021
  69.8 35.9 %collective-permute-start.2 = (bf16[512,1024]{1,0:T(8,128)(2,1)}, bf16[512,1024]{1,0:T(8,128)(2,1)}, u32[]{:S(2)}, u32[]{:S(2)}) collective-permute-start(bf16[512,1024]{1,0:T(8,128)(2,1)} %norm.1.own), channel_id=1, source_target_pairs={{0,1},{1,0},{2,3},{3,2},{4,5},{5,4},{6,7},{7,6},{8,9},{9,8},{10,11... | collective-permute-start | bytes 3145736 | tf_op jit(solution)/shard_map/ppermute | solution.py:1021
  70.8 1.3 collective-permute-start
  71.0 66.4 %copy-start.19 = (bf16[8,128,384]{2,1,0:T(8,128)(2,1)}, bf16[8,128,384]{2,1,0:T(8,128)(2,1)S(1)}, u32[]{:S(2)}) copy-start(bf16[8,128,384]{2,1,0:T(8,128)(2,1)S(1)} %slice.87) | copy-start | bytes 2359300
  71.0 36.2 %collective-permute-start.6 = (bf16[1024,384]{1,0:T(8,128)(2,1)S(1)}, bf16[1024,384]{1,0:T(8,128)(2,1)}, u32[]{:S(2)}, u32[]{:S(2)}) collective-permute-start(bf16[1024,384]{1,0:T(8,128)(2,1)S(1)} %bitcast.113), channel_id=1, source_target_pairs={{0,8},{8,0},{16,24},{24,16},{1,9},{9,1},{17,25},{25,17},{2,10},{10... | collective-permute-start | bytes 2359304 | tf_op jit(solution)/shard_map/ppermute | solution.py:1016
  104.5 33.0 %copy-start.26 = (bf16[512,1024]{1,0:T(8,128)(2,1)}, bf16[512,1024]{1,0:T(8,128)(2,1)S(1)}, u32[]{:S(2)}) copy-start(bf16[512,1024]{1,0:T(8,128)(2,1)S(1)} %collective-permute-done.3.z_one) | copy-start | bytes 3145732
  104.5 16.1 %collective-permute-start.5 = (bf16[256,1024]{1,0:T(8,128)(2,1)S(1)}, bf16[256,1024]{1,0:T(8,128)(2,1)}, u32[]{:S(2)}, u32[]{:S(2)}) collective-permute-start(bf16[256,1024]{1,0:T(8,128)(2,1)S(1)} %slice.86), channel_id=1, source_target_pairs={{0,1},{1,0},{2,3},{3,2},{4,5},{5,4},{6,7},{7,6},{8,9},{9,8},{10,11... | collective-permute-start | bytes 1572872 | tf_op jit(solution)/shard_map/ppermute | solution.py:1021
  106.7 30.7 %collective-permute-start.4 = (bf16[256,1024]{1,0:T(8,128)(2,1)S(1)}, bf16[256,1024]{1,0:T(8,128)(2,1)}, u32[]{:S(2)}, u32[]{:S(2)}) collective-permute-start(bf16[256,1024]{1,0:T(8,128)(2,1)S(1)} %slice.85), channel_id=1, source_target_pairs={{0,2},{1,3},{2,0},{3,1},{4,6},{5,7},{6,4},{7,5},{8,10},{9,11},{10,... | collective-permute-start | bytes 1572872 | tf_op jit(solution)/shard_map/ppermute | solution.py:1021
  147.3 4.4 collective-permute-start.7
  178.7 3.7 copy-start.32
  178.7 42.3 %all-to-all-start.1 = ((bf16[8,512,128]{2,1,0:T(8,128)(2,1)}), bf16[8,512,128]{2,1,0:T(8,128)(2,1)S(1)}, u32[]{:S(2)}, u32[]{:S(2)}) async-start(bf16[8,512,128]{2,1,0:T(8,128)(2,1)} %get-tuple-element.65.attended), calls=%async_computation.1 | async-start | bytes 2097152 | tf_op jit(solution)/shard_map/all_to_all | solution.py:1039
  182.4 215.6 %reduce-scatter.5.cloned.1.call-start = ((), (), s32[]{:S(2)}) async-start(), calls=%async_computation.9 | async-start | bytes 4718592 | tf_op jit(solution)/shard_map/reduce_scatter | solution.py:1219
  182.5 39.1 %collective-permute-start.10 = (bf16[512,1024]{1,0:T(8,128)(2,1)S(1)}, bf16[512,1024]{1,0:T(8,128)(2,1)S(1)}, u32[]{:S(2)}, u32[]{:S(2)}) collective-permute-start(bf16[512,1024]{1,0:T(8,128)(2,1)S(1)} %bitcast.135), channel_id=1, source_target_pairs={{0,0},{1,1},{2,2},{3,3},{4,8},{5,9},{6,10},{7,11},{8,4},{9,5},{10,... | collective-permute-start | bytes 3145736 | tf_op jit(solution)/shard_map/ppermute | solution.py:1031
  221.0 3.6 copy-start.8
  221.0 3.6 collective-permute-start.8
  221.5 8.8 %copy-start.4 = (bf16[512,1024]{1,0:T(8,128)(2,1)}, bf16[512,1024]{1,0:T(8,128)(2,1)S(1)}, u32[]{:S(2)}) copy-start(bf16[512,1024]{1,0:T(8,128)(2,1)S(1)} %collective-permute-done.10.grad_own.cotangent) | copy-start | bytes 3145732
  221.5 9.2 %collective-permute-start.11 = (bf16[512,1024]{1,0:T(8,128)(2,1)S(1)}, bf16[512,1024]{1,0:T(8,128)(2,1)S(1)}, u32[]{:S(2)}, u32[]{:S(2)}) collective-permute-start(bf16[512,1024]{1,0:T(8,128)(2,1)S(1)} %collective-permute-done.10.grad_own.cotangent), channel_id=1, source_target_pairs={{0,8},{8,0},{16,24},{24,16},{1,9},{9,1},{17,25},{25,17},{2,10},{10... | collective-permute-start | bytes 3145736 | tf_op jit(solution)/shard_map/ppermute | solution.py:1016
  230.3 2.9 collective-permute-start.9
  230.7 2.5 copy-start.13
  271.4 2.7 collective-permute-start.14
  287.8 4.6 collective-permute-start.15
  288.1 34.6 %all-to-all-start.2 = ((bf16[8,512,128]{2,1,0:T(8,128)(2,1)}), bf16[8,512,128]{2,1,0:T(8,128)(2,1)}, u32[]{:S(2)}, u32[]{:S(2)}) async-start(bf16[8,512,128]{2,1,0:T(8,128)(2,1)} %get-tuple-element.76), calls=%async_computation.2 | async-start | bytes 2097152 | tf_op jit(solution)/shard_map/all_to_all | solution.py:1039
  292.4 168.5 %reduce-scatter.3.cloned.1.call-start = ((), (), s32[]{:S(2)}) async-start(), calls=%async_computation.8 | async-start | bytes 2949120 | tf_op jit(solution)/shard_map/reduce_scatter | solution.py:1285
  293.4 30.0 %copy-start.3 = (f32[512,1024]{1,0:T(8,128)S(1)}, f32[512,1024]{1,0:T(8,128)}, u32[]{:S(2)}) copy-start(f32[512,1024]{1,0:T(8,128)} %get-tuple-element.67.middle) | copy-start | bytes 6291460
  304.5 63.6 %collective-permute-start.17 = (bf16[8,128,1280]{2,1,0:T(8,128)(2,1)}, bf16[8,128,1280]{2,1,0:T(8,128)(2,1)}, u32[]{:S(2)}, u32[]{:S(2)}) collective-permute-start(bf16[8,128,1280]{2,1,0:T(8,128)(2,1)} %get-tuple-element.82), channel_id=1, source_target_pairs={{0,16},{8,24},{16,0},{24,8},{1,17},{9,25},{17,1},{25,9},{2,18},{10... | collective-permute-start | bytes 7864328 | tf_op jit(solution)/shard_map/ppermute | solution.py:1016
  305.7 17.6 %collective-permute-start.12 = (bf16[512,1024]{1,0:T(8,128)(2,1)}, bf16[512,1024]{1,0:T(8,128)(2,1)S(1)}, u32[]{:S(2)}, u32[]{:S(2)}) collective-permute-start(bf16[512,1024]{1,0:T(8,128)(2,1)} %get-tuple-element.71), channel_id=1, source_target_pairs={{0,8},{8,0},{16,24},{24,16},{1,9},{9,1},{17,25},{25,17},{2,10},{10... | collective-permute-start | bytes 3145736 | tf_op jit(solution)/shard_map/ppermute | solution.py:1016
  322.7 5.2 %collective-permute-start.16 = (bf16[8,512,128]{2,1,0:T(8,128)(2,1)}, bf16[8,512,128]{2,1,0:T(8,128)(2,1)S(1)}, u32[]{:S(2)}, u32[]{:S(2)}) collective-permute-start(bf16[8,512,128]{2,1,0:T(8,128)(2,1)} %all-to-all-done.2.grad_own), channel_id=1, source_target_pairs={{0,8},{8,0},{16,24},{24,16},{1,9},{9,1},{17,25},{25,17},{2,10},{10... | collective-permute-start | bytes 3145736 | tf_op jit(solution)/shard_map/ppermute | solution.py:1016
  325.6 42.5 %collective-permute-start.13 = (bf16[1,512,1024]{2,1,0:T(8,128)(2,1)S(1)}, bf16[1,512,1024]{2,1,0:T(8,128)(2,1)S(1)}, u32[]{:S(2)}, u32[]{:S(2)}) collective-permute-start(bf16[1,512,1024]{2,1,0:T(8,128)(2,1)S(1)} %bitcast.112), channel_id=1, source_target_pairs={{0,0},{1,1},{2,2},{3,3},{4,8},{5,9},{6,10},{7,11},{8,4},{9,5},{10,... | collective-permute-start | bytes 3145736 | tf_op jit(solution)/shard_map/ppermute | solution.py:1031
  328.9 39.3 %copy-start.9 = (bf16[8,128,1280]{2,1,0:T(8,128)(2,1)S(1)}, bf16[8,128,1280]{2,1,0:T(8,128)(2,1)}, u32[]{:S(2)}) copy-start(bf16[8,128,1280]{2,1,0:T(8,128)(2,1)} %get-tuple-element.89) | copy-start | bytes 7864324
  368.2 4.3 copy-start.16
  372.4 1.4 copy-start.31
  373.8 3.4 collective-permute-start.18
  387.8 6.3 %copy-start.18 = (bf16[2,512,512]{2,1,0:T(8,128)(2,1)S(1)}, bf16[2,512,512]{2,1,0:T(8,128)(2,1)}, u32[]{:S(2)}) copy-start(bf16[2,512,512]{2,1,0:T(8,128)(2,1)} %get-tuple-element.92.y_out) | copy-start | bytes 3145732
  394.0 17.3 %collective-permute-start.20 = (bf16[1024,384]{1,0:T(8,128)(2,1)}, bf16[1024,384]{1,0:T(8,128)(2,1)}, u32[]{:S(2)}, u32[]{:S(2)}) collective-permute-start(bf16[1024,384]{1,0:T(8,128)(2,1)} %grad_heads.3), channel_id=1, source_target_pairs={{0,8},{8,0},{16,24},{24,16},{1,9},{9,1},{17,25},{25,17},{2,10},{10... | collective-permute-start | bytes 2359304 | tf_op jit(solution)/shard_map/ppermute | solution.py:1016
  394.1 34.1 %collective-permute-start.19 = (bf16[2,512,512]{2,1,0:T(8,128)(2,1)S(1)}, bf16[2,512,512]{2,1,0:T(8,128)(2,1)S(1)}, u32[]{:S(2)}, u32[]{:S(2)}) collective-permute-start(bf16[2,512,512]{2,1,0:T(8,128)(2,1)S(1)} %copy-done.18), channel_id=1, source_target_pairs={{0,1},{1,0},{2,3},{3,2},{4,5},{5,4},{6,7},{7,6},{8,9},{9,8},{10,11... | collective-permute-start | bytes 3145736 | tf_op jit(solution)/shard_map/ppermute | solution.py:1021
  395.8 33.4 %collective-permute-start.22 = (bf16[2,512,512]{2,1,0:T(8,128)(2,1)}, bf16[2,512,512]{2,1,0:T(8,128)(2,1)S(1)}, u32[]{:S(2)}, u32[]{:S(2)}) collective-permute-start(bf16[2,512,512]{2,1,0:T(8,128)(2,1)} %get-tuple-element.93.z_out), channel_id=1, source_target_pairs={{0,2},{1,3},{2,0},{3,1},{4,6},{5,7},{6,4},{7,5},{8,10},{9,11},{10,... | collective-permute-start | bytes 3145736 | tf_op jit(solution)/shard_map/ppermute | solution.py:1021
  398.1 30.2 %collective-permute-start.21 = (bf16[256,1024]{1,0:T(8,128)(2,1)}, bf16[256,1024]{1,0:T(8,128)(2,1)S(1)}, u32[]{:S(2)}, u32[]{:S(2)}) collective-permute-start(bf16[256,1024]{1,0:T(8,128)(2,1)} %reduce-scatter.5.cloned.1.call-done), channel_id=1, source_target_pairs={{0,16},{8,24},{16,0},{24,8},{1,17},{9,25},{17,1},{25,9},{2,18},{10... | collective-permute-start | bytes 1572872 | tf_op jit(solution)/shard_map/ppermute | solution.py:1016
  411.3 17.0 %copy-start.20 = (bf16[256,1024]{1,0:T(8,128)(2,1)S(1)}, bf16[256,1024]{1,0:T(8,128)(2,1)}, u32[]{:S(2)}) copy-start(bf16[256,1024]{1,0:T(8,128)(2,1)} %reduce-scatter.5.cloned.1.call-done) | copy-start | bytes 1572868
  413.0 43.0 %collective-permute-start.26 = (bf16[1024,384]{1,0:T(8,128)(2,1)S(1)}, bf16[1024,384]{1,0:T(8,128)(2,1)S(1)}, u32[]{:S(2)}, u32[]{:S(2)}) collective-permute-start(bf16[1024,384]{1,0:T(8,128)(2,1)S(1)} %add_convert_fusion.3), channel_id=1, source_target_pairs={{0,16},{8,24},{16,0},{24,8},{1,17},{9,25},{17,1},{25,9},{2,18},{10... | collective-permute-start | bytes 2359304 | tf_op jit(solution)/shard_map/ppermute | solution.py:1016
  428.5 47.4 %copy-start.10 = (bf16[256,1024]{1,0:T(8,128)(2,1)}, bf16[256,1024]{1,0:T(8,128)(2,1)S(1)}, u32[]{:S(2)}) copy-start(bf16[256,1024]{1,0:T(8,128)(2,1)S(1)} %add_convert_fusion.4.down) | copy-start | bytes 1572868
  434.2 21.8 %collective-permute-start.23 = (bf16[512,512]{1,0:T(8,128)(2,1)}, bf16[512,512]{1,0:T(8,128)(2,1)S(1)}, u32[]{:S(2)}, u32[]{:S(2)}) collective-permute-start(bf16[512,512]{1,0:T(8,128)(2,1)} %get-tuple-element.101), channel_id=1, source_target_pairs={{0,2},{1,3},{2,0},{3,1},{4,6},{5,7},{6,4},{7,5},{8,10},{9,11},{10,... | collective-permute-start | bytes 1572872 | tf_op jit(solution)/shard_map/ppermute | solution.py:1021
  434.2 21.8 %collective-permute-start.24 = (bf16[512,512]{1,0:T(8,128)(2,1)}, bf16[512,512]{1,0:T(8,128)(2,1)S(1)}, u32[]{:S(2)}, u32[]{:S(2)}) collective-permute-start(bf16[512,512]{1,0:T(8,128)(2,1)} %get-tuple-element.102), channel_id=1, source_target_pairs={{0,1},{1,0},{2,3},{3,2},{4,5},{5,4},{6,7},{7,6},{8,9},{9,8},{10,11... | collective-permute-start | bytes 1572872 | tf_op jit(solution)/shard_map/ppermute | solution.py:1021
  456.0 4.9 copy-start.21
  456.0 4.9 copy-start.22
  457.2 32.5 %all-to-all-start.3 = ((bf16[8,128,384]{2,1,0:T(8,128)(2,1)}), bf16[8,128,384]{2,1,0:T(8,128)(2,1)S(1)}, u32[]{:S(2)}, u32[]{:S(2)}) async-start(bf16[8,128,384]{2,1,0:T(8,128)(2,1)} %bitcast.37), calls=%async_computation.5 | async-start | bytes 1572864 | tf_op jit(solution)/shard_map/all_to_all | solution.py:1388
  460.8 14.9 %copy-start.28 = (f32[8,1024]{1,0:T(8,128)S(1)}, f32[8,1024]{1,0:T(8,128)}, u32[]{:S(2)}) copy-start(f32[8,1024]{1,0:T(8,128)} %get-tuple-element.110) | copy-start | bytes 98308
  460.8 14.9 %slice-start = ((f32[8,1024]{1,0:T(8,128)}), f32[2,1024]{1,0:T(2,128)S(1)}, s32[]{:S(2)}) async-start(f32[8,1024]{1,0:T(8,128)} %first_sums.1), calls=%async_computation.10 | async-start | bytes 16384 | tf_op jit(solution)/shard_map/slice | solution.py:1337
  467.3 40.6 %collective-permute-start.25 = (bf16[1,512,1024]{2,1,0:T(8,128)(2,1)}, bf16[1,512,1024]{2,1,0:T(8,128)(2,1)S(1)}, u32[]{:S(2)}, u32[]{:S(2)}) collective-permute-start(bf16[1,512,1024]{2,1,0:T(8,128)(2,1)} %bitcast.109), channel_id=1, source_target_pairs={{0,0},{1,1},{2,2},{3,3},{4,8},{5,9},{6,10},{7,11},{8,4},{9,5},{10,... | collective-permute-start | bytes 3145736 | tf_op jit(solution)/shard_map/ppermute | solution.py:1031
  475.9 22.8 %collective-permute-start.28 = (bf16[256,1024]{1,0:T(8,128)(2,1)S(1)}, bf16[256,1024]{1,0:T(8,128)(2,1)}, u32[]{:S(2)}, u32[]{:S(2)}) collective-permute-start(bf16[256,1024]{1,0:T(8,128)(2,1)S(1)} %add_convert_fusion.4.down), channel_id=1, source_target_pairs={{0,8},{8,0},{16,24},{24,16},{1,9},{9,1},{17,25},{25,17},{2,10},{10... | collective-permute-start | bytes 1572872 | tf_op jit(solution)/shard_map/ppermute | solution.py:1016
  476.0 22.4 %collective-permute-start.29 = (bf16[128,1280]{1,0:T(8,128)(2,1)}, bf16[128,1280]{1,0:T(8,128)(2,1)}, u32[]{:S(2)}, u32[]{:S(2)}) collective-permute-start(bf16[128,1280]{1,0:T(8,128)(2,1)} %reduce-scatter.3.cloned.1.call-done.mixed), channel_id=1, source_target_pairs={{0,16},{8,24},{16,0},{24,8},{1,17},{9,25},{17,1},{25,9},{2,18},{10... | collective-permute-start | bytes 983048 | tf_op jit(solution)/shard_map/ppermute | solution.py:1016
  489.9 10.9 %copy-start.12 = (bf16[4,128,384]{2,1,0:T(8,128)(2,1)}, bf16[4,128,384]{2,1,0:T(8,128)(2,1)S(1)}, u32[]{:S(2)}) copy-start(bf16[4,128,384]{2,1,0:T(8,128)(2,1)S(1)} %fusion.heads) | copy-start | bytes 1179652
  489.9 21.3 %copy-start.17 = (bf16[1,512,1024]{2,1,0:T(8,128)(2,1)S(1)}, bf16[1,512,1024]{2,1,0:T(8,128)(2,1)}, u32[]{:S(2)}) copy-start(bf16[1,512,1024]{2,1,0:T(8,128)(2,1)} %copy-done.16) | copy-start | bytes 3145732
  490.6 19.4 %all-to-all-start.4 = ((f32[32,16,128]{2,1,0:T(8,128)}), f32[32,16,128]{2,1,0:T(8,128)S(1)}, u32[]{:S(2)}, u32[]{:S(2)}) async-start(f32[32,16,128]{2,1,0:T(8,128)} %bitcast.40), calls=%async_computation.6 | async-start | bytes 524288 | tf_op jit(solution)/shard_map/all_to_all | solution.py:1392
  497.8 2.9 collective-permute-start.27
  498.2 2.1 collective-permute-start.30
  498.4 2.4 collective-permute-start.31
  511.2 1.9 copy-start.1
  (12 other events, 11.7 us)
Sparse Core Ops, SparseCore 0:
  64.0 155.6 all-gather.1
  270.3 101.4 reduce-scatter.4
  375.7 83.6 reduce-scatter.2

commit v5 on v3

--- a/solution.py
+++ b/solution.py
@@ -1111,8 +1111,15 @@
 
     fourth = frames // 4
     slab = pl.BlockSpec((fourth, width), lambda i, *_: (i, 0))
+    half = frames // 2
+    wide_slab = pl.BlockSpec((half, width), lambda i, *_: (i, 0))
     normed_one = call(
-        norm_kernel, "norm", 4, [slab, whole(16, width)], slab, like((frames, width), low)
+        norm_kernel,
+        "norm",
+        2,
+        [wide_slab, whole(16, width)],
+        wide_slab,
+        like((frames, width), low),
     )(ids, tokens_here, vectors)
     y_one = hop_seq(normed_one, 1)
     z_one = hop_seq(normed_one, 2)
@@ -1146,7 +1153,6 @@
     mine = trade(attended_heads, IN_SQUARE)
     mine_came = hop_batch(mine, 1)
     blocks = pl.BlockSpec((8, half, LANES), lambda i, *_: (0, i, 0))
-    wide_slab = pl.BlockSpec((half, width), lambda i, *_: (i, 0))
     w_out_spec = pl.BlockSpec(
         (8, 4, part // 4, width), lambda *_: (0, 0, (deep * 4) // part - 1, 0)
     )
@@ -1288,14 +1294,17 @@
     grad_qkv_came = hop_batch(grad_leaving, 1)
 
     pair = (2, frames, width // 2)
+    wide_half = pl.BlockSpec((half, width // 2), lambda i, *_: (i, 0))
+    wide_pair = pl.BlockSpec((2, half, width // 2), lambda i, *_: (0, i, 0))
+    wide_heads = pl.BlockSpec((4, half, 3 * LANES), lambda i, *_: (0, i, 0))
     half_spec = pl.BlockSpec((fourth, width // 2), lambda i, *_: (i, 0))
     pair_spec = pl.BlockSpec((2, fourth, width // 2), lambda i, *_: (0, i, 0))
     first, y_out, z_out, keep_left, keep_right = call(
         back_project_kernel,
         "back_project",
-        4,
-        [heads_slab] * 2 + [whole(*w_heads.shape)] * 2,
-        [slab, pair_spec, pair_spec, half_spec, half_spec],
+        2,
+        [wide_heads] * 2 + [whole(*w_heads.shape)] * 2,
+        [wide_slab, wide_pair, wide_pair, wide_half, wide_half],
         (
             like((frames, width), wide),
             like(pair, low),
@@ -1303,7 +1312,7 @@
             like(pair[1:], wide),
             like(pair[1:], wide),
         ),
-        scratch=[pltpu.VMEM((4, fourth, width), wide)],
+        scratch=[pltpu.VMEM((4, half, width), wide)],
         flops=2 * 4 * frames * width * 6 * LANES,
     )(
         ids,
@@ -1376,9 +1385,10 @@
     grad_inputs = call(
         last_kernel,
         "last",
-        4,
-        [slab, pair_spec, pair_spec, half_spec, half_spec, slab, slab, whole(16, width)],
-        slab,
+        2,
+        [wide_slab, wide_pair, wide_pair, wide_half, wide_half]
+        + [wide_slab, wide_slab, whole(16, width)],
+        wide_slab,
         like((frames, width), low),
     )(ids, after(first, mixed, sums), y_came, z_came, z_last, y_last, tokens_here, grad_middle, vectors)
     mixed_x = hop_batch(mixed, 2)

time: 522 us -> 527 us (level); the launches traced: 520 us -> 519 us
  transfers between devices with their start and end apart: 40 -> 40, of which waited for: 21 -> 20; matrix products, arithmetic and copies ran while one was open for 5% -> 5% of each run, Pallas kernels for 28% -> 29%
where the time goes in v5:
time: 527 us; the launch traced here: 519 us
  waiting for transfers between devices  215 us (41%)
  Pallas kernels  185 us (35%)
  starting transfers between devices  59.8 us (11%)
  local copies, waits for them, and re-layouts  27.6 us (5%)
  other arithmetic  16.7 us (3%)
  between operations  14.7 us (3%)
    pallas_call x15, Pallas kernels, run(): pl.pallas_call(kernel, out_shape=out_shape, grid_spec=pltpu.PrefetchScala...  123 us
    ppermute x8, waiting for transfers between devices, hop_seq(): return lax.ppermute(block, 'seq', [(i, i ^ bits) for i in range(size)])  91.8 us
    all_to_all x2, waiting for transfers between devices, trade(): lax.all_to_all(block, 'seq', 0, 0, tiled=True, axis_index_groups=groups)  53.2 us
    pallas_call x1, Pallas kernels, attend_back(): pl.pallas_call(attend_back_kernel, out_shape=(like(own.shape, jnp.bfloat1...  37.8 us
    ppermute x4, waiting for transfers between devices, swap_halves(): return lax.ppermute(block, ('batch', 'seq'), route)  34.9 us
    pallas_call x1, Pallas kernels, attend(): pl.pallas_call(attend_kernel, out_shape=(like((8, TILE, LANES), jnp.bfloa...  25 us
    ppermute x20, waiting for transfers between devices, hop_batch(): return lax.ppermute(block, 'batch', [(i, i ^ bit) for i in range(size)])  17.5 us
    ppermute x4, starting transfers between devices, swap_halves(): return lax.ppermute(block, ('batch', 'seq'), route)  16.5 us
  transfers between devices with their start and end apart: 40, of which 20 were waited for; matrix products, arithmetic and copies ran while one was open for 5% of the time, Pallas kernels for 29%

profile of v5, /device:TPU:1, one launch (start us, length us, event | category | flops | bytes accessed | tf_op | source)
XLA Modules:
  0.0 518.8 jit_solution(10317209838588255937)
XLA Ops:
  7.2 1.7 concatenate.19
  9.0 1.5 copy.71
  10.8 1.4 copy.74
  12.3 6.4 %all-to-all-start = ((bf16[8,144,384]{2,1,0:T(8,128)(2,1)}), bf16[8,144,384]{2,1,0:T(8,128)(2,1)S(1)}, u32[]{:S(2)}, u32[]{:S(2)}) async-start(bf16[8,144,384]{2,1,0:T(8,128)(2,1)} %copy.74), calls=%async_computation | async-start | bytes 1769472 | tf_op jit(solution)/shard_map/all_to_all | solution.py:1095
  18.7 5.3 %collective-permute-start.1 = (bf16[512,1024]{1,0:T(8,128)(2,1)}, bf16[512,1024]{1,0:T(8,128)(2,1)S(1)}, u32[]{:S(2)}, u32[]{:S(2)}) collective-permute-start(bf16[512,1024]{1,0:T(8,128)(2,1)} %bitcast.134), channel_id=1, source_target_pairs={{0,0},{1,1},{2,2},{3,3},{4,8},{5,9},{6,10},{7,11},{8,4},{9,5},{10,... | collective-permute-start | bytes 3145736 | tf_op jit(solution)/shard_map/ppermute | solution.py:1031
  24.1 2.6 reshape.158
  26.6 2.8 dynamic-slice_reduce_fusion
  31.2 32.6 %collective-permute-done.1.tokens = bf16[512,1024]{1,0:T(8,128)(2,1)S(1)} collective-permute-done((bf16[512,1024]{1,0:T(8,128)(2,1)}, bf16[512,1024]{1,0:T(8,128)(2,1)S(1)}, u32[]{:S(2)}, u32[]{:S(2)}) %collective-permute-start.1) | collective-permute-done | bytes 1048608 | tf_op jit(solution)/shard_map/ppermute | solution.py:1031
  65.3 3.3 norm.1.own
  70.9 33.7 %collective-permute-done.3.z_one = bf16[512,1024]{1,0:T(8,128)(2,1)S(1)} collective-permute-done((bf16[512,1024]{1,0:T(8,128)(2,1)}, bf16[512,1024]{1,0:T(8,128)(2,1)S(1)}, u32[]{:S(2)}, u32[]{:S(2)}) %collective-permute-start.3) | collective-permute-done | bytes 1048608 | tf_op jit(solution)/shard_map/ppermute | solution.py:1021
  104.7 1.4 collective-permute-start.5
  106.0 1.1 slice.85
  107.6 11.7 %collective-permute-done.5.bottom = bf16[256,1024]{1,0:T(8,128)(2,1)} collective-permute-done((bf16[256,1024]{1,0:T(8,128)(2,1)S(1)}, bf16[256,1024]{1,0:T(8,128)(2,1)}, u32[]{:S(2)}, u32[]{:S(2)}) %collective-permute-start.5) | collective-permute-done | bytes 524320 | tf_op jit(solution)/shard_map/ppermute | solution.py:1021
  119.4 16.6 %collective-permute-done.4.top = bf16[256,1024]{1,0:T(8,128)(2,1)} collective-permute-done((bf16[256,1024]{1,0:T(8,128)(2,1)S(1)}, bf16[256,1024]{1,0:T(8,128)(2,1)}, u32[]{:S(2)}, u32[]{:S(2)}) %collective-permute-start.4) | collective-permute-done | bytes 524320 | tf_op jit(solution)/shard_map/ppermute | solution.py:1021
  136.0 9.9 %project.1 = (bf16[4,512,384]{2,1,0:T(8,128)(2,1)}, bf16[4,512,384]{2,1,0:T(8,128)(2,1)}, bf16[4,512,1024]{2,1,0:T(8,128)(2,1)}) custom-call(s32[4]{0:T(128)} %pad_add_fusion.2.ids, bf16[512,1024]{1,0:T(8,128)(2,1)} %norm.1.own, bf16[512,1024]{1,0:T(8,128)(2,1)} %collective-permute-done.2.y_one, bf16[512,1024]{1,0:T(8,128)(2,1)} %copy-done.24, ...), custom_call_target="tpu_custom_call" | custom-call | flops 3221225472 | bytes 11534336 | tf_op jit(solution)/shard_map/project/pallas_call | solution.py:429
  147.3 3.1 collective-permute-done.7
  150.4 1.2 copy-done.28
  151.6 25.0 %attend.1 = (bf16[8,512,128]{2,1,0:T(8,128)(2,1)}, f32[2,4096]{1,0:T(2,128)}) custom-call(s32[4]{0:T(128)} %pad_add_fusion.2.ids, s32[3,8]{1,0:T(4,128)} %pad_add_fusion.1.bounds, bf16[2048,384]{1,0:T(8,128)(2,1)} %bitcast.136, bf16[2048,384]{1,0:T(8,128)(2,1)} %bitcast.132, f32[1,4096]{1,0:T(1,128)} %fusion.2.places_row), custom_call_target="tpu_custom_call" | custom-call | flops 4294967296 | bytes 9830400 | tf_op jit(solution)/shard_map/attend/pallas_call | solution.py:578
  176.6 3.7 all-to-all-start.1
  180.4 3.1 collective-permute-start.10
  183.4 36.3 %all-to-all-done.1.own = bf16[8,512,128]{2,1,0:T(8,128)(2,1)S(1)} async-done(((bf16[8,512,128]{2,1,0:T(8,128)(2,1)}), bf16[8,512,128]{2,1,0:T(8,128)(2,1)S(1)}, u32[]{:S(2)}, u32[]{:S(2)}) %all-to-all-start.1) | async-done | bytes 1048608 | tf_op jit(solution)/shard_map/all_to_all | solution.py:1039
  220.4 3.0 collective-permute-done.8.came
  223.4 5.7 %out_project.1 = (bf16[512,1024]{1,0:T(8,128)(2,1)}, f32[512,1024]{1,0:T(8,128)}, bf16[512,1024]{1,0:T(8,128)(2,1)}) custom-call(s32[4]{0:T(128)} %pad_add_fusion.2.ids, bf16[8,512,128]{2,1,0:T(8,128)(2,1)} %copy-done.8, bf16[8,512,128]{2,1,0:T(8,128)(2,1)} %collective-permute-done.8.came, bf16[512,1024]{1,0:T(8,128)(2,1)} %copy-done.2, ...), custom_call_target="tpu_custom_call" | custom-call | flops 1073741824 | bytes 44171264 | tf_op jit(solution)/shard_map/out_project/pallas_call | solution.py:429
  229.5 2.5 collective-permute-done.9.normed_came
  233.0 26.8 %feed_forward.1 = (bf16[2,512,2048]{2,1,0:T(8,128)(2,1)}, bf16[2,512,2048]{2,1,0:T(8,128)(2,1)}, f32[8,1024]{1,0:T(8,128)}, f32[512,1024]{1,0:T(8,128)}, bf16[51...) custom-call(s32[4]{0:T(128)} %pad_add_fusion.2.ids, ...), custom_call_target="tpu_custom_call" | custom-call | flops 17179869184 | bytes 159514624 | tf_op jit(solution)/shard_map/feed_forward/pallas_call | solution.py:429
  259.8 9.1 %grad_down.1 = bf16[2048,1024]{1,0:T(8,128)(2,1)} custom-call(s32[4]{0:T(128)} %pad_add_fusion.2.ids, bf16[2,512,2048]{2,1,0:T(8,128)(2,1)} %get-tuple-element.73.act, bf16[512,1024]{1,0:T(8,128)(2,1)} %copy-done.4, bf16[512,1024]{1,0:T(8,128)(2,1)} %copy-done.13), custom_call_target="tpu_custom_call" | custom-call | flops 4294967296 | bytes 12582912 | tf_op jit(solution)/shard_map/grad_down/pallas_call | solution.py:429
  268.9 1.2 copy-done.31
  270.5 2.3 collective-permute-done.14.back_came
  273.8 8.2 %middle_back.1 = (f32[512,1024]{1,0:T(8,128)}, bf16[512,1024]{1,0:T(8,128)(2,1)}, bf16[8,512,128]{2,1,0:T(8,128)(2,1)}, f32[8,1024]{1,0:T(8,128)}) custom-call(s32[4]{0:T(128)} %pad_add_fusion.2.ids, f32[512,1024]{1,0:T(8,128)} %get-tuple-element.74.back_own, bf16[512,1024]{1,0:T(8,128)(2,1)} %copy-done.15, f32[512,1024]{1,0:T(8,128)} %get-tuple-element.67.middle, ...), custom_call_target="tpu_custom_call" | custom-call | flops 1073741824 | bytes 50462720 | tf_op jit(solution)/shard_map/middle_back/pallas_call | solution.py:429
  281.9 4.6 grad_out.1
  286.8 4.3 all-to-all-start.2
  292.1 11.1 %grad_up.1 = (bf16[8,128,1280]{2,1,0:T(8,128)(2,1)}, bf16[8,128,1280]{2,1,0:T(8,128)(2,1)}) custom-call(s32[4]{0:T(128)} %pad_add_fusion.2.ids, bf16[512,1024]{1,0:T(8,128)(2,1)} %get-tuple-element.68.normed_own, bf16[512,1024]{1,0:T(8,128)(2,1)} %copy-done.5, bf16[2,512,2048]{2,1,0:T(8,128)(2,1)} %get-tuple-element.77.grad_up, ...), custom_call_target="tpu_custom_call" | custom-call | flops 524288 | bytes 16777216 | tf_op jit(solution)/shard_map/grad_up/pallas_call | solution.py:429
  304.5 16.9 %all-to-all-done.2.grad_own = bf16[8,512,128]{2,1,0:T(8,128)(2,1)} async-done(((bf16[8,512,128]{2,1,0:T(8,128)(2,1)}), bf16[8,512,128]{2,1,0:T(8,128)(2,1)}, u32[]{:S(2)}, u32[]{:S(2)}) %all-to-all-start.2) | async-done | bytes 1048608 | tf_op jit(solution)/shard_map/all_to_all | solution.py:1039
  322.1 2.3 add_convert_fusion.1
  324.4 2.5 collective-permute-start.13
  327.9 37.8 %attend_back.1 = (bf16[2048,384]{1,0:T(8,128)(2,1)}, bf16[2048,384]{1,0:T(8,128)(2,1)}) custom-call(s32[4]{0:T(128)} %pad_add_fusion.2.ids, s32[3,8]{1,0:T(4,128)} %pad_add_fusion.1.bounds, bf16[2048,384]{1,0:T(8,128)(2,1)} %bitcast.137, bf16[2048,384]{1,0:T(8,128)(2,1)} %bitcast.133, bf16[8,512,128]{2,1,0:T(8,128)(2,1)} %all-to-all-done.2.grad_own, ...), custom_call_target="tpu_custom_call" | custom-call | flops 10737418240 | bytes 9830400 | tf_op jit(solution)/shard_map/attend_back/pallas_call | solution.py:706
  365.8 4.1 add_convert_fusion
  370.0 1.1 copy-done.11
  371.1 9.5 %back_project.1 = (f32[512,1024]{1,0:T(8,128)}, bf16[2,512,512]{2,1,0:T(8,128)(2,1)}, bf16[2,512,512]{2,1,0:T(8,128)(2,1)}, f32[512,512]{1,0:T(8,128)}, f32[512,512]{1,0:T(8,128)}) custom-call(s32[4]{0:T(128)} %pad_add_fusion.2.ids, bf16[4,512,384]{2,1,0:T(8,128)(2,1)} %bitcast.107, bf16[4,512,384]{2,1,0:T(8,128)(2,1)} %bitcast.108, ...), custom_call_target="tpu_custom_call" | custom-call | flops 3221225472 | bytes 9437184 | tf_op jit(solution)/shard_map/back_project/pallas_call | solution.py:429
  380.6 6.1 %grad_heads.3 = bf16[1024,384]{1,0:T(8,128)(2,1)} custom-call(s32[4]{0:T(128)} %pad_add_fusion.2.ids, bf16[2048,1024]{1,0:T(8,128)(2,1)} %bitcast.96, bf16[2048,384]{1,0:T(8,128)(2,1)} %copy-done.11), custom_call_target="tpu_custom_call" | custom-call | flops 1610612736 | bytes 11534336 | tf_op jit(solution)/shard_map/grad_heads/pallas_call | solution.py:429
  386.9 1.8 collective-permute-start.19
  388.7 1.8 collective-permute-start.22
  390.5 4.0 collective-permute-start.21
  394.6 7.2 %first_sums.1 = f32[8,1024]{1,0:T(8,128)} custom-call(s32[4]{0:T(128)} %pad_add_fusion.2.ids, f32[512,1024]{1,0:T(8,128)} %get-tuple-element.104.first, bf16[2,512,512]{2,1,0:T(8,128)(2,1)} %get-tuple-element.91.y_out, bf16[2,512,512]{2,1,0:T(8,128)(2,1)} %get-tuple-element.92.z_out, f32[512,512]{1,0:T(8,128)} %get-tuple-element.93.keep_left, ...), custom_call_target="tpu_custom_call" | custom-call | bytes 21102592 | tf_op jit(solution)/shard_map/first_sums/pallas_call | solution.py:429
  401.8 6.1 %grad_heads.2 = bf16[1024,384]{1,0:T(8,128)(2,1)} custom-call(s32[4]{0:T(128)} %pad_add_fusion.2.ids, bf16[2048,1024]{1,0:T(8,128)(2,1)} %bitcast.97, bf16[2048,384]{1,0:T(8,128)(2,1)} %get-tuple-element.85.grads), custom_call_target="tpu_custom_call" | custom-call | flops 1610612736 | bytes 11534336 | tf_op jit(solution)/shard_map/grad_heads/pallas_call | solution.py:429
  407.9 1.6 add_convert_fusion.3
  409.7 6.5 %collective-permute-done.19.y_came = bf16[2,512,512]{2,1,0:T(8,128)(2,1)S(1)} collective-permute-done((bf16[2,512,512]{2,1,0:T(8,128)(2,1)}, bf16[2,512,512]{2,1,0:T(8,128)(2,1)S(1)}, u32[]{:S(2)}, u32[]{:S(2)}) %collective-permute-start.19) | collective-permute-done | bytes 1048608 | tf_op jit(solution)/shard_map/ppermute | solution.py:1021
  416.2 2.4 add_convert_fusion.4.down
  418.7 8.8 %collective-permute-done.22.z_came = bf16[2,512,512]{2,1,0:T(8,128)(2,1)S(1)} collective-permute-done((bf16[2,512,512]{2,1,0:T(8,128)(2,1)}, bf16[2,512,512]{2,1,0:T(8,128)(2,1)S(1)}, u32[]{:S(2)}, u32[]{:S(2)}) %collective-permute-start.22) | collective-permute-done | bytes 1048608 | tf_op jit(solution)/shard_map/ppermute | solution.py:1021
  428.5 3.9 second.1
  435.5 4.6 all-to-all-start.3
  440.1 9.0 %collective-permute-done.24.y_second = bf16[512,512]{1,0:T(8,128)(2,1)S(1)} collective-permute-done((bf16[512,512]{1,0:T(8,128)(2,1)}, bf16[512,512]{1,0:T(8,128)(2,1)S(1)}, u32[]{:S(2)}, u32[]{:S(2)}) %collective-permute-start.24) | collective-permute-done | bytes 524320 | tf_op jit(solution)/shard_map/ppermute | solution.py:1021
  449.1 5.4 %collective-permute-done.23.z_second = bf16[512,512]{1,0:T(8,128)(2,1)S(1)} collective-permute-done((bf16[512,512]{1,0:T(8,128)(2,1)}, bf16[512,512]{1,0:T(8,128)(2,1)S(1)}, u32[]{:S(2)}, u32[]{:S(2)}) %collective-permute-start.23) | collective-permute-done | bytes 524320 | tf_op jit(solution)/shard_map/ppermute | solution.py:1021
  454.5 2.4 add_convert_fusion.2
  456.9 6.3 %all-to-all-done.3 = f32[32,16,128]{2,1,0:T(8,128)S(1)} async-done(((f32[32,16,128]{2,1,0:T(8,128)}), f32[32,16,128]{2,1,0:T(8,128)S(1)}, u32[]{:S(2)}, u32[]{:S(2)}) %all-to-all-start.3) | async-done | bytes 262176 | tf_op jit(solution)/shard_map/all_to_all | solution.py:1383
  463.2 3.8 all-to-all-start.4
  467.1 5.9 %last.1 = bf16[512,1024]{1,0:T(8,128)(2,1)} custom-call(s32[4]{0:T(128)} %pad_add_fusion.2.ids, f32[512,1024]{1,0:T(8,128)} %get-tuple-element.104.first, bf16[2,512,512]{2,1,0:T(8,128)(2,1)} %copy-done.6, bf16[2,512,512]{2,1,0:T(8,128)(2,1)} %copy-done.7, bf16[512,512]{1,0:T(8,128)(2,1)} %copy-done.21, bf16[512,512]{1,0:T(8,128)(2,1)} %copy-done.20, ...), custom_call_target="tpu_custom_call" | custom-call | bytes 16908288 | tf_op jit(solution)/shard_map/last/pallas_call | solution.py:429
  473.0 5.6 %collective-permute-start.25 = (bf16[1,512,1024]{2,1,0:T(8,128)(2,1)}, bf16[1,512,1024]{2,1,0:T(8,128)(2,1)S(1)}, u32[]{:S(2)}, u32[]{:S(2)}) collective-permute-start(bf16[1,512,1024]{2,1,0:T(8,128)(2,1)} %bitcast.109), channel_id=1, source_target_pairs={{0,0},{1,1},{2,2},{3,3},{4,8},{5,9},{6,10},{7,11},{8,4},{9,5},{10,... | collective-permute-start | bytes 3145736 | tf_op jit(solution)/shard_map/ppermute | solution.py:1031
  478.6 1.3 collective-permute-start.29
  480.4 5.8 %collective-permute-done.29.mixed_x = bf16[128,1280]{1,0:T(8,128)(2,1)} collective-permute-done((bf16[128,1280]{1,0:T(8,128)(2,1)}, bf16[128,1280]{1,0:T(8,128)(2,1)}, u32[]{:S(2)}, u32[]{:S(2)}) %collective-permute-start.29) | collective-permute-done | bytes 327712 | tf_op jit(solution)/shard_map/ppermute | solution.py:1016
  486.3 10.8 %all-to-all-done.4 = bf16[8,128,384]{2,1,0:T(8,128)(2,1)S(1)} async-done(((bf16[8,128,384]{2,1,0:T(8,128)(2,1)}), bf16[8,128,384]{2,1,0:T(8,128)(2,1)S(1)}, u32[]{:S(2)}, u32[]{:S(2)}) %all-to-all-start.4) | async-done | bytes 786464 | tf_op jit(solution)/shard_map/all_to_all | solution.py:1400
  497.3 2.4 collective-permute-start.27
  502.3 5.3 %spread.1 = (f32[128,3072]{1,0:T(8,128)}, f32[128,1024]{1,0:T(8,128)}, f32[128,4096]{1,0:T(8,128)}, f32[512,1024]{1,0:T(8,128)}) custom-call(s32[4]{0:T(128)} %pad_add_fusion.2.ids, bf16[4,128,384]{2,1,0:T(8,128)(2,1)} %copy-done.12, bf16[4,128,384]{2,1,0:T(8,128)(2,1)} %copy-done.23, bf16[256,1024]{1,0:T(8,128)(2,1)} %add_convert_fusion.4.down, ...), custom_call_target="tpu_custom_call" | custom-call | bytes 6291456 | tf_op jit(solution)/shard_map/spread/pallas_call | solution.py:429
  507.6 2.3 collective-permute-done.25
  (160 shorter events, 25.6 us)
Async XLA Ops:
  7.2 23.1 %copy-start = (bf16[512,1024]{1,0:T(8,128)(2,1)S(1)}, bf16[512,1024]{1,0:T(8,128)(2,1)}, u32[]{:S(2)}) copy-start(bf16[512,1024]{1,0:T(8,128)(2,1)} %param.22) | copy-start | bytes 3145732
  12.3 51.6 %all-to-all-start = ((bf16[8,144,384]{2,1,0:T(8,128)(2,1)}), bf16[8,144,384]{2,1,0:T(8,128)(2,1)S(1)}, u32[]{:S(2)}, u32[]{:S(2)}) async-start(bf16[8,144,384]{2,1,0:T(8,128)(2,1)} %copy.74), calls=%async_computation | async-start | bytes 1769472 | tf_op jit(solution)/shard_map/all_to_all | solution.py:1095
  18.7 204.7 %all-gather.2.cloned.1.call-start = ((), (), s32[]{:S(2)}) async-start(), calls=%async_computation.7 | async-start | bytes 19464192 | tf_op jit(solution)/shard_map/all_gather | solution.py:1126
  18.7 45.1 %collective-permute-start.1 = (bf16[512,1024]{1,0:T(8,128)(2,1)}, bf16[512,1024]{1,0:T(8,128)(2,1)S(1)}, u32[]{:S(2)}, u32[]{:S(2)}) collective-permute-start(bf16[512,1024]{1,0:T(8,128)(2,1)} %bitcast.134), channel_id=1, source_target_pairs={{0,0},{1,1},{2,2},{3,3},{4,8},{5,9},{6,10},{7,11},{8,4},{9,5},{10,... | collective-permute-start | bytes 3145736 | tf_op jit(solution)/shard_map/ppermute | solution.py:1031
  30.3 39.3 %copy-start.25 = (s32[1,4096]{1,0:T(1,128)S(1)}, s32[1,4096]{1,0:T(1,128)}, u32[]{:S(2)}) copy-start(s32[1,4096]{1,0:T(1,128)} %param.17) | copy-start | bytes 49156
  30.4 39.3 %copy-start.27 = (s32[1,4]{1,0:T(1,128)S(1)}, s32[1,4]{1,0:T(1,128)}, u32[]{:S(2)}) copy-start(s32[1,4]{1,0:T(1,128)} %param.16) | copy-start | bytes 52
  63.9 1.4 copy-start.2
  68.6 36.0 %collective-permute-start.3 = (bf16[512,1024]{1,0:T(8,128)(2,1)}, bf16[512,1024]{1,0:T(8,128)(2,1)S(1)}, u32[]{:S(2)}, u32[]{:S(2)}) collective-permute-start(bf16[512,1024]{1,0:T(8,128)(2,1)} %norm.1.own), channel_id=1, source_target_pairs={{0,2},{1,3},{2,0},{3,1},{4,6},{5,7},{6,4},{7,5},{8,10},{9,11},{10,... | collective-permute-start | bytes 3145736 | tf_op jit(solution)/shard_map/ppermute | solution.py:1021
  68.6 37.4 %collective-permute-start.2 = (bf16[512,1024]{1,0:T(8,128)(2,1)}, bf16[512,1024]{1,0:T(8,128)(2,1)}, u32[]{:S(2)}, u32[]{:S(2)}) collective-permute-start(bf16[512,1024]{1,0:T(8,128)(2,1)} %norm.1.own), channel_id=1, source_target_pairs={{0,1},{1,0},{2,3},{3,2},{4,5},{5,4},{6,7},{7,6},{8,9},{9,8},{10,11... | collective-permute-start | bytes 3145736 | tf_op jit(solution)/shard_map/ppermute | solution.py:1021
  69.7 1.3 collective-permute-start
  69.8 66.1 %copy-start.18 = (bf16[8,128,384]{2,1,0:T(8,128)(2,1)}, bf16[8,128,384]{2,1,0:T(8,128)(2,1)S(1)}, u32[]{:S(2)}) copy-start(bf16[8,128,384]{2,1,0:T(8,128)(2,1)S(1)} %slice.87) | copy-start | bytes 2359300
  69.9 37.8 %collective-permute-start.6 = (bf16[1024,384]{1,0:T(8,128)(2,1)S(1)}, bf16[1024,384]{1,0:T(8,128)(2,1)}, u32[]{:S(2)}, u32[]{:S(2)}) collective-permute-start(bf16[1024,384]{1,0:T(8,128)(2,1)S(1)} %bitcast.113), channel_id=1, source_target_pairs={{0,8},{8,0},{16,24},{24,16},{1,9},{9,1},{17,25},{25,17},{2,10},{10... | collective-permute-start | bytes 2359304 | tf_op jit(solution)/shard_map/ppermute | solution.py:1016
  104.6 31.3 %copy-start.24 = (bf16[512,1024]{1,0:T(8,128)(2,1)}, bf16[512,1024]{1,0:T(8,128)(2,1)S(1)}, u32[]{:S(2)}) copy-start(bf16[512,1024]{1,0:T(8,128)(2,1)S(1)} %collective-permute-done.3.z_one) | copy-start | bytes 3145732
  104.7 14.7 %collective-permute-start.5 = (bf16[256,1024]{1,0:T(8,128)(2,1)S(1)}, bf16[256,1024]{1,0:T(8,128)(2,1)}, u32[]{:S(2)}, u32[]{:S(2)}) collective-permute-start(bf16[256,1024]{1,0:T(8,128)(2,1)S(1)} %slice.86), channel_id=1, source_target_pairs={{0,1},{1,0},{2,3},{3,2},{4,5},{5,4},{6,7},{7,6},{8,9},{9,8},{10,11... | collective-permute-start | bytes 1572872 | tf_op jit(solution)/shard_map/ppermute | solution.py:1021
  107.1 28.8 %collective-permute-start.4 = (bf16[256,1024]{1,0:T(8,128)(2,1)S(1)}, bf16[256,1024]{1,0:T(8,128)(2,1)}, u32[]{:S(2)}, u32[]{:S(2)}) collective-permute-start(bf16[256,1024]{1,0:T(8,128)(2,1)S(1)} %slice.85), channel_id=1, source_target_pairs={{0,2},{1,3},{2,0},{3,1},{4,6},{5,7},{6,4},{7,5},{8,10},{9,11},{10,... | collective-permute-start | bytes 1572872 | tf_op jit(solution)/shard_map/ppermute | solution.py:1021
  145.9 4.6 collective-permute-start.7
  176.6 3.8 copy-start.29
  176.6 43.1 %all-to-all-start.1 = ((bf16[8,512,128]{2,1,0:T(8,128)(2,1)}), bf16[8,512,128]{2,1,0:T(8,128)(2,1)S(1)}, u32[]{:S(2)}, u32[]{:S(2)}) async-start(bf16[8,512,128]{2,1,0:T(8,128)(2,1)} %get-tuple-element.65.attended), calls=%async_computation.1 | async-start | bytes 2097152 | tf_op jit(solution)/shard_map/all_to_all | solution.py:1039
  180.3 210.2 %reduce-scatter.5.cloned.1.call-start = ((), (), s32[]{:S(2)}) async-start(), calls=%async_computation.9 | async-start | bytes 4718592 | tf_op jit(solution)/shard_map/reduce_scatter | solution.py:1225
  180.4 39.9 %collective-permute-start.10 = (bf16[512,1024]{1,0:T(8,128)(2,1)S(1)}, bf16[512,1024]{1,0:T(8,128)(2,1)S(1)}, u32[]{:S(2)}, u32[]{:S(2)}) collective-permute-start(bf16[512,1024]{1,0:T(8,128)(2,1)S(1)} %bitcast.135), channel_id=1, source_target_pairs={{0,0},{1,1},{2,2},{3,3},{4,8},{5,9},{6,10},{7,11},{8,4},{9,5},{10,... | collective-permute-start | bytes 3145736 | tf_op jit(solution)/shard_map/ppermute | solution.py:1031
  219.7 3.7 copy-start.8
  219.7 3.7 collective-permute-start.8
  220.3 8.8 %copy-start.4 = (bf16[512,1024]{1,0:T(8,128)(2,1)}, bf16[512,1024]{1,0:T(8,128)(2,1)S(1)}, u32[]{:S(2)}) copy-start(bf16[512,1024]{1,0:T(8,128)(2,1)S(1)} %collective-permute-done.10.grad_own.cotangent) | copy-start | bytes 3145732
  220.3 9.2 %collective-permute-start.11 = (bf16[512,1024]{1,0:T(8,128)(2,1)S(1)}, bf16[512,1024]{1,0:T(8,128)(2,1)S(1)}, u32[]{:S(2)}, u32[]{:S(2)}) collective-permute-start(bf16[512,1024]{1,0:T(8,128)(2,1)S(1)} %collective-permute-done.10.grad_own.cotangent), channel_id=1, source_target_pairs={{0,8},{8,0},{16,24},{24,16},{1,9},{9,1},{17,25},{25,17},{2,10},{10... | collective-permute-start | bytes 3145736 | tf_op jit(solution)/shard_map/ppermute | solution.py:1016
  229.1 2.9 collective-permute-start.9
  229.5 2.5 copy-start.13
  268.9 1.2 copy-start.31
  270.1 2.7 collective-permute-start.14
  286.5 4.6 collective-permute-start.15
  286.8 34.6 %all-to-all-start.2 = ((bf16[8,512,128]{2,1,0:T(8,128)(2,1)}), bf16[8,512,128]{2,1,0:T(8,128)(2,1)}, u32[]{:S(2)}, u32[]{:S(2)}) async-start(bf16[8,512,128]{2,1,0:T(8,128)(2,1)} %get-tuple-element.76), calls=%async_computation.2 | async-start | bytes 2097152 | tf_op jit(solution)/shard_map/all_to_all | solution.py:1039
  291.1 176.0 %reduce-scatter.3.cloned.1.call-start = ((), (), s32[]{:S(2)}) async-start(), calls=%async_computation.8 | async-start | bytes 2949120 | tf_op jit(solution)/shard_map/reduce_scatter | solution.py:1291
  292.1 30.0 %copy-start.3 = (f32[512,1024]{1,0:T(8,128)S(1)}, f32[512,1024]{1,0:T(8,128)}, u32[]{:S(2)}) copy-start(f32[512,1024]{1,0:T(8,128)} %get-tuple-element.67.middle) | copy-start | bytes 6291460
  303.2 62.5 %collective-permute-start.17 = (bf16[8,128,1280]{2,1,0:T(8,128)(2,1)}, bf16[8,128,1280]{2,1,0:T(8,128)(2,1)}, u32[]{:S(2)}, u32[]{:S(2)}) collective-permute-start(bf16[8,128,1280]{2,1,0:T(8,128)(2,1)} %get-tuple-element.82), channel_id=1, source_target_pairs={{0,16},{8,24},{16,0},{24,8},{1,17},{9,25},{17,1},{25,9},{2,18},{10... | collective-permute-start | bytes 7864328 | tf_op jit(solution)/shard_map/ppermute | solution.py:1016
  304.1 18.0 %collective-permute-start.12 = (bf16[512,1024]{1,0:T(8,128)(2,1)}, bf16[512,1024]{1,0:T(8,128)(2,1)S(1)}, u32[]{:S(2)}, u32[]{:S(2)}) collective-permute-start(bf16[512,1024]{1,0:T(8,128)(2,1)} %get-tuple-element.71), channel_id=1, source_target_pairs={{0,8},{8,0},{16,24},{24,16},{1,9},{9,1},{17,25},{25,17},{2,10},{10... | collective-permute-start | bytes 3145736 | tf_op jit(solution)/shard_map/ppermute | solution.py:1016
  321.4 5.4 %collective-permute-start.16 = (bf16[8,512,128]{2,1,0:T(8,128)(2,1)}, bf16[8,512,128]{2,1,0:T(8,128)(2,1)S(1)}, u32[]{:S(2)}, u32[]{:S(2)}) collective-permute-start(bf16[8,512,128]{2,1,0:T(8,128)(2,1)} %all-to-all-done.2.grad_own), channel_id=1, source_target_pairs={{0,8},{8,0},{16,24},{24,16},{1,9},{9,1},{17,25},{25,17},{2,10},{10... | collective-permute-start | bytes 3145736 | tf_op jit(solution)/shard_map/ppermute | solution.py:1016
  324.4 41.4 %collective-permute-start.13 = (bf16[1,512,1024]{2,1,0:T(8,128)(2,1)S(1)}, bf16[1,512,1024]{2,1,0:T(8,128)(2,1)S(1)}, u32[]{:S(2)}, u32[]{:S(2)}) collective-permute-start(bf16[1,512,1024]{2,1,0:T(8,128)(2,1)S(1)} %bitcast.112), channel_id=1, source_target_pairs={{0,0},{1,1},{2,2},{3,3},{4,8},{5,9},{6,10},{7,11},{8,4},{9,5},{10,... | collective-permute-start | bytes 3145736 | tf_op jit(solution)/shard_map/ppermute | solution.py:1031
  327.9 37.9 %copy-start.9 = (bf16[8,128,1280]{2,1,0:T(8,128)(2,1)S(1)}, bf16[8,128,1280]{2,1,0:T(8,128)(2,1)}, u32[]{:S(2)}) copy-start(bf16[8,128,1280]{2,1,0:T(8,128)(2,1)} %get-tuple-element.89) | copy-start | bytes 7864324
  365.7 4.2 copy-start.16
  365.7 4.3 collective-permute-start.18
  386.7 21.2 %collective-permute-start.20 = (bf16[1024,384]{1,0:T(8,128)(2,1)}, bf16[1024,384]{1,0:T(8,128)(2,1)}, u32[]{:S(2)}, u32[]{:S(2)}) collective-permute-start(bf16[1024,384]{1,0:T(8,128)(2,1)} %grad_heads.3), channel_id=1, source_target_pairs={{0,8},{8,0},{16,24},{24,16},{1,9},{9,1},{17,25},{25,17},{2,10},{10... | collective-permute-start | bytes 2359304 | tf_op jit(solution)/shard_map/ppermute | solution.py:1016
  386.9 29.4 %collective-permute-start.19 = (bf16[2,512,512]{2,1,0:T(8,128)(2,1)}, bf16[2,512,512]{2,1,0:T(8,128)(2,1)S(1)}, u32[]{:S(2)}, u32[]{:S(2)}) collective-permute-start(bf16[2,512,512]{2,1,0:T(8,128)(2,1)} %get-tuple-element.91.y_out), channel_id=1, source_target_pairs={{0,1},{1,0},{2,3},{3,2},{4,5},{5,4},{6,7},{7,6},{8,9},{9,8},{10,11... | collective-permute-start | bytes 3145736 | tf_op jit(solution)/shard_map/ppermute | solution.py:1021
  388.7 38.8 %collective-permute-start.22 = (bf16[2,512,512]{2,1,0:T(8,128)(2,1)}, bf16[2,512,512]{2,1,0:T(8,128)(2,1)S(1)}, u32[]{:S(2)}, u32[]{:S(2)}) collective-permute-start(bf16[2,512,512]{2,1,0:T(8,128)(2,1)} %get-tuple-element.92.z_out), channel_id=1, source_target_pairs={{0,2},{1,3},{2,0},{3,1},{4,6},{5,7},{6,4},{7,5},{8,10},{9,11},{10,... | collective-permute-start | bytes 3145736 | tf_op jit(solution)/shard_map/ppermute | solution.py:1021
  390.5 25.7 %collective-permute-start.21 = (bf16[256,1024]{1,0:T(8,128)(2,1)}, bf16[256,1024]{1,0:T(8,128)(2,1)}, u32[]{:S(2)}, u32[]{:S(2)}) collective-permute-start(bf16[256,1024]{1,0:T(8,128)(2,1)} %reduce-scatter.5.cloned.1.call-done), channel_id=1, source_target_pairs={{0,16},{8,24},{16,0},{24,8},{1,17},{9,25},{17,1},{25,9},{2,18},{10... | collective-permute-start | bytes 1572872 | tf_op jit(solution)/shard_map/ppermute | solution.py:1016
  407.9 8.3 %copy-start.19 = (bf16[256,1024]{1,0:T(8,128)(2,1)S(1)}, bf16[256,1024]{1,0:T(8,128)(2,1)}, u32[]{:S(2)}) copy-start(bf16[256,1024]{1,0:T(8,128)(2,1)} %reduce-scatter.5.cloned.1.call-done) | copy-start | bytes 1572868
  409.5 44.9 %collective-permute-start.26 = (bf16[1024,384]{1,0:T(8,128)(2,1)S(1)}, bf16[1024,384]{1,0:T(8,128)(2,1)}, u32[]{:S(2)}, u32[]{:S(2)}) collective-permute-start(bf16[1024,384]{1,0:T(8,128)(2,1)S(1)} %add_convert_fusion.3), channel_id=1, source_target_pairs={{0,16},{8,24},{16,0},{24,8},{1,17},{9,25},{17,1},{25,9},{2,18},{10... | collective-permute-start | bytes 2359304 | tf_op jit(solution)/shard_map/ppermute | solution.py:1016
  416.2 11.3 %copy-start.6 = (bf16[2,512,512]{2,1,0:T(8,128)(2,1)}, bf16[2,512,512]{2,1,0:T(8,128)(2,1)S(1)}, u32[]{:S(2)}) copy-start(bf16[2,512,512]{2,1,0:T(8,128)(2,1)S(1)} %collective-permute-done.19.y_came) | copy-start | bytes 3145732
  418.7 15.9 %copy-start.26 = (f32[8,1024]{1,0:T(8,128)S(1)}, f32[8,1024]{1,0:T(8,128)}, u32[]{:S(2)}) copy-start(f32[8,1024]{1,0:T(8,128)} %get-tuple-element.96) | copy-start | bytes 98308
  418.7 16.0 %slice-start = ((f32[8,1024]{1,0:T(8,128)}), f32[2,1024]{1,0:T(2,128)S(1)}, s32[]{:S(2)}) async-start(f32[8,1024]{1,0:T(8,128)} %first_sums.1), calls=%async_computation.10 | async-start | bytes 16384 | tf_op jit(solution)/shard_map/slice | solution.py:1346
  432.4 16.7 %collective-permute-start.24 = (bf16[512,512]{1,0:T(8,128)(2,1)}, bf16[512,512]{1,0:T(8,128)(2,1)S(1)}, u32[]{:S(2)}, u32[]{:S(2)}) collective-permute-start(bf16[512,512]{1,0:T(8,128)(2,1)} %get-tuple-element.105), channel_id=1, source_target_pairs={{0,1},{1,0},{2,3},{3,2},{4,5},{5,4},{6,7},{7,6},{8,9},{9,8},{10,11... | collective-permute-start | bytes 1572872 | tf_op jit(solution)/shard_map/ppermute | solution.py:1021
  433.4 21.1 %collective-permute-start.23 = (bf16[512,512]{1,0:T(8,128)(2,1)}, bf16[512,512]{1,0:T(8,128)(2,1)S(1)}, u32[]{:S(2)}, u32[]{:S(2)}) collective-permute-start(bf16[512,512]{1,0:T(8,128)(2,1)} %get-tuple-element.102), channel_id=1, source_target_pairs={{0,2},{1,3},{2,0},{3,1},{4,6},{5,7},{6,4},{7,5},{8,10},{9,11},{10,... | collective-permute-start | bytes 1572872 | tf_op jit(solution)/shard_map/ppermute | solution.py:1021
  435.5 27.7 %all-to-all-start.3 = ((f32[32,16,128]{2,1,0:T(8,128)}), f32[32,16,128]{2,1,0:T(8,128)S(1)}, u32[]{:S(2)}, u32[]{:S(2)}) async-start(f32[32,16,128]{2,1,0:T(8,128)} %bitcast.37), calls=%async_computation.5 | async-start | bytes 524288 | tf_op jit(solution)/shard_map/all_to_all | solution.py:1383
  449.1 18.0 %copy-start.20 = (bf16[512,512]{1,0:T(8,128)(2,1)}, bf16[512,512]{1,0:T(8,128)(2,1)S(1)}, u32[]{:S(2)}) copy-start(bf16[512,512]{1,0:T(8,128)(2,1)S(1)} %collective-permute-done.24.y_second) | copy-start | bytes 1572868
  454.5 12.6 %copy-start.21 = (bf16[512,512]{1,0:T(8,128)(2,1)}, bf16[512,512]{1,0:T(8,128)(2,1)S(1)}, u32[]{:S(2)}) copy-start(bf16[512,512]{1,0:T(8,128)(2,1)S(1)} %collective-permute-done.23.z_second) | copy-start | bytes 1572868
  463.2 33.8 %all-to-all-start.4 = ((bf16[8,128,384]{2,1,0:T(8,128)(2,1)}), bf16[8,128,384]{2,1,0:T(8,128)(2,1)S(1)}, u32[]{:S(2)}, u32[]{:S(2)}) async-start(bf16[8,128,384]{2,1,0:T(8,128)(2,1)} %bitcast.40), calls=%async_computation.6 | async-start | bytes 1572864 | tf_op jit(solution)/shard_map/all_to_all | solution.py:1400
  467.1 12.8 %copy-start.10 = (bf16[256,1024]{1,0:T(8,128)(2,1)S(1)}, bf16[256,1024]{1,0:T(8,128)(2,1)}, u32[]{:S(2)}) copy-start(bf16[256,1024]{1,0:T(8,128)(2,1)} %add_convert_fusion.4.down) | copy-start | bytes 1572868
  473.0 36.9 %collective-permute-start.25 = (bf16[1,512,1024]{2,1,0:T(8,128)(2,1)}, bf16[1,512,1024]{2,1,0:T(8,128)(2,1)S(1)}, u32[]{:S(2)}, u32[]{:S(2)}) collective-permute-start(bf16[1,512,1024]{2,1,0:T(8,128)(2,1)} %bitcast.109), channel_id=1, source_target_pairs={{0,0},{1,1},{2,2},{3,3},{4,8},{5,9},{6,10},{7,11},{8,4},{9,5},{10,... | collective-permute-start | bytes 3145736 | tf_op jit(solution)/shard_map/ppermute | solution.py:1031
  478.6 7.7 %collective-permute-start.29 = (bf16[128,1280]{1,0:T(8,128)(2,1)}, bf16[128,1280]{1,0:T(8,128)(2,1)}, u32[]{:S(2)}, u32[]{:S(2)}) collective-permute-start(bf16[128,1280]{1,0:T(8,128)(2,1)} %reduce-scatter.3.cloned.1.call-done.mixed), channel_id=1, source_target_pairs={{0,16},{8,24},{16,0},{24,8},{1,17},{9,25},{17,1},{25,9},{2,18},{10... | collective-permute-start | bytes 983048 | tf_op jit(solution)/shard_map/ppermute | solution.py:1016
  479.9 20.8 %collective-permute-start.28 = (bf16[256,1024]{1,0:T(8,128)(2,1)S(1)}, bf16[256,1024]{1,0:T(8,128)(2,1)S(1)}, u32[]{:S(2)}, u32[]{:S(2)}) collective-permute-start(bf16[256,1024]{1,0:T(8,128)(2,1)S(1)} %copy-done.10), channel_id=1, source_target_pairs={{0,8},{8,0},{16,24},{24,16},{1,9},{9,1},{17,25},{25,17},{2,10},{10... | collective-permute-start | bytes 1572872 | tf_op jit(solution)/shard_map/ppermute | solution.py:1016
  479.9 20.8 %collective-permute-start.30 = (bf16[128,1280]{1,0:T(8,128)(2,1)}, bf16[128,1280]{1,0:T(8,128)(2,1)}, u32[]{:S(2)}, u32[]{:S(2)}) collective-permute-start(bf16[128,1280]{1,0:T(8,128)(2,1)} %reduce-scatter.3.cloned.1.call-done.mixed), channel_id=1, source_target_pairs={{0,8},{8,0},{16,24},{24,16},{1,9},{9,1},{17,25},{25,17},{2,10},{10... | collective-permute-start | bytes 983048 | tf_op jit(solution)/shard_map/ppermute | solution.py:1016
  486.3 14.5 %collective-permute-start.31 = (bf16[128,1280]{1,0:T(8,128)(2,1)}, bf16[128,1280]{1,0:T(8,128)(2,1)}, u32[]{:S(2)}, u32[]{:S(2)}) collective-permute-start(bf16[128,1280]{1,0:T(8,128)(2,1)} %collective-permute-done.29.mixed_x), channel_id=1, source_target_pairs={{0,8},{8,0},{16,24},{24,16},{1,9},{9,1},{17,25},{25,17},{2,10},{10... | collective-permute-start | bytes 983048 | tf_op jit(solution)/shard_map/ppermute | solution.py:1016
  497.2 12.8 %copy-start.17 = (bf16[1,512,1024]{2,1,0:T(8,128)(2,1)S(1)}, bf16[1,512,1024]{2,1,0:T(8,128)(2,1)}, u32[]{:S(2)}) copy-start(bf16[1,512,1024]{2,1,0:T(8,128)(2,1)} %copy-done.16) | copy-start | bytes 3145732
  497.3 3.7 copy-start.12
  497.3 3.7 collective-permute-start.27
  509.9 1.9 copy-start.1
  (9 other events, 8.8 us)
Sparse Core Ops, SparseCore 0:
  64.0 154.9 all-gather.1
  269.0 101.4 reduce-scatter.4
  374.4 87.9 reduce-scatter.2
